TPU v7x, 32 devices: a whole 2x2x4 slice. The times are simulated.
32 devices in a mesh: seq: 8 (over y, x, core), fsdp: 4 (over z).
Axes of the slice: x: 2, y: 2, z: 4, core: 2. Of those that a mesh axis runs over, the one named last changes fastest.
Arguments:
- hidden_in: bfloat16 [4, 1024, 1024], P('fsdp', 'seq'), may hold values from -6 to 6
- cotangent: bfloat16 [4, 1024, 1024], P('fsdp', 'seq'), may hold values from -6 to 6
- segment_ids: int32 [4, 1024], P('fsdp'), may hold values from 0 to 7, never falling along the last dimension, each value on 1 to 512 neighbouring positions
- projection: float32 [1024, 3072], P('fsdp'), may hold values from -0.1875 to 0.1875
- projection_bias: float32 [3072], P('fsdp'), may hold values from -4 to 4
- output_weight: float32 [1024, 1024], P('fsdp'), may hold values from -1 to 1
- output_bias: float32 [1024], P('fsdp'), may hold values from -4 to 4
- first_gain: float32 [1024], P('fsdp'), may hold values from 0.5 to 1.5
- first_shift: float32 [1024], P('fsdp'), may hold values from -4 to 4
- up_weight: float32 [1024, 4096], P('fsdp'), may hold values from -0.1875 to 0.1875
- up_bias: float32 [4096], P('fsdp'), may hold values from -4 to 4
- down_weight: float32 [4096, 1024], P('fsdp'), may hold values from -0.09375 to 0.09375
- down_bias: float32 [1024], P('fsdp'), may hold values from -4 to 4
- second_gain: float32 [1024], P('fsdp'), may hold values from 0.5 to 1.5
- second_shift: float32 [1024], P('fsdp'), may hold values from -4 to 4
Outputs:
- layer_output: bfloat16 [4, 1024, 1024], P('fsdp', 'seq')
- input_grad: bfloat16 [4, 1024, 1024], P('fsdp', 'seq')
- projection_grad: float32 [1024, 3072], P('fsdp')
- projection_bias_grad: float32 [3072], P('fsdp')
- output_weight_grad: float32 [1024, 1024], P('fsdp')
- output_bias_grad: float32 [1024], P('fsdp')
- first_gain_grad: float32 [1024], P('fsdp')
- first_shift_grad: float32 [1024], P('fsdp')
- up_weight_grad: float32 [1024, 4096], P('fsdp')
- up_bias_grad: float32 [4096], P('fsdp')
- down_weight_grad: float32 [4096, 1024], P('fsdp')
- down_bias_grad: float32 [1024], P('fsdp')
- second_gain_grad: float32 [1024], P('fsdp')
- second_shift_grad: float32 [1024], P('fsdp')
Inputs may be any that keep to these rules, and one draw needn't show every extreme that they name: `segment_ids`: in each sequence the numbers never fall and run through 0 to 7; equal numbers mark one document of 1 to 512 tokens, and some document has exactly 512.
All inputs are finite; a program needn't handle non-finite values.
Results may differ from a plain program's by a relative error of at most 0.02.
Values may be sent and summed in bfloat16 or wider, within the bound.
A program may use at most 192 MiB of HBM per device.

v0:
```python
from functools import partial

import jax
import jax.numpy as jnp
from jax import lax
from jax.sharding import PartitionSpec as P

HEADS = 16
HEAD_DIM = 64


norm_epsilon = 1e-05


def rotary(values, positions):
    half = values.shape[-1] // 2
    channel = jnp.arange(half).astype(jnp.float32)
    inverse = 10000.0 ** (-2.0 * channel / values.shape[-1])
    angles = positions[:, None] * inverse[None, :]
    cosine = jnp.cos(angles)[:, None, :]
    sine = jnp.sin(angles)[:, None, :]
    first = values[..., :half]
    second = values[..., half:]
    return jnp.concatenate(
        [first * cosine - second * sine, second * cosine + first * sine], axis=-1
    )


def rotary_back(grads, positions):
    unused, pullback = jax.vjp(lambda inner: rotary(inner, positions), grads)
    return pullback(grads)[0]


def norm_forward(values, gain, shift):
    centre = values - jnp.mean(values, axis=-1, keepdims=True)
    inverse_root = lax.rsqrt(jnp.mean(centre * centre, axis=-1, keepdims=True) + norm_epsilon)
    normal = centre * inverse_root
    return (normal * gain + shift, normal, inverse_root)


def norm_backward(incoming, normal, inverse_root, gain):
    gain_grad = jnp.sum(incoming * normal, axis=0)
    shift_grad = jnp.sum(incoming, axis=0)
    scaled = incoming * gain
    inner = (
        scaled
        - jnp.mean(scaled, axis=-1, keepdims=True)
        - normal * jnp.mean(scaled * normal, axis=-1, keepdims=True)
    )
    return (inner * inverse_root, gain_grad, shift_grad)


def shards(
    hidden_in,
    cotangent,
    segment_ids,
    projection,
    projection_bias,
    output_weight,
    output_bias,
    first_gain,
    first_shift,
    up_weight,
    up_bias,
    down_weight,
    down_bias,
    second_gain,
    second_shift,
):
    bf16 = jnp.bfloat16
    f32 = jnp.float32
    tokens = hidden_in[0]
    local_rows = tokens.shape[0]
    width = tokens.shape[1]
    seq_rank = lax.axis_index("seq")
    positions = (seq_rank * local_rows + jnp.arange(local_rows)).astype(f32)
    segments = segment_ids[0]
    scale = HEAD_DIM ** (-0.5)
    attention_full = (
        lax.all_gather(projection.astype(bf16), "fsdp", axis=0, tiled=True),
        lax.all_gather(projection_bias.astype(bf16), "fsdp", axis=0, tiled=True),
        lax.all_gather(output_weight.astype(bf16), "fsdp", axis=0, tiled=True),
        lax.all_gather(output_bias.astype(bf16), "fsdp", axis=0, tiled=True),
        lax.all_gather(first_gain.astype(bf16), "fsdp", axis=0, tiled=True),
        lax.all_gather(first_shift.astype(bf16), "fsdp", axis=0, tiled=True),
    )
    proj_weight = attention_full[0]
    projected = jnp.dot(tokens, proj_weight, preferred_element_type=f32) + attention_full[1].astype(
        f32
    )
    heads = projected.reshape(local_rows, 3, HEADS, HEAD_DIM)
    queries = rotary(heads[:, 0], positions)
    keys = rotary(heads[:, 1], positions)
    stacked = jnp.stack([queries, keys, heads[:, 2]]).astype(bf16)
    spread = lax.all_to_all(stacked, "seq", split_axis=2, concat_axis=1, tiled=True)
    query_all = spread[0]
    key_all = spread[1]
    value_all = spread[2]
    length = query_all.shape[0]
    local_heads = query_all.shape[1]
    block = min(512, length)
    count = length // block
    query_blocks = query_all.reshape(count, block, local_heads, HEAD_DIM)
    segment_blocks = segments.reshape(count, block)

    def scores_of(query_block, segment_block):
        raw = jnp.einsum("qhd,khd->hqk", query_block, key_all, preferred_element_type=f32) * scale
        allowed = segment_block[:, None] == segments[None, :]
        return jnp.where(allowed[None], raw, -1e30)

    def forward_block(pieces):
        query_block, segment_block = pieces
        scores = scores_of(query_block, segment_block)
        row_max = jnp.max(scores, axis=-1, keepdims=True)
        exponent = jnp.exp(scores - row_max)
        total = jnp.sum(exponent, axis=-1, keepdims=True)
        weights = exponent / total
        context = jnp.einsum(
            "hqk,khd->qhd", weights.astype(bf16), value_all, preferred_element_type=f32
        )
        return (context.astype(bf16), (row_max + jnp.log(total))[..., 0])

    context_blocks, log_totals = lax.map(forward_block, (query_blocks, segment_blocks))
    context_heads = context_blocks.reshape(length, local_heads, HEAD_DIM)
    context_tokens = lax.all_to_all(
        context_heads, "seq", split_axis=0, concat_axis=1, tiled=True
    ).reshape(local_rows, width)
    attended = jnp.dot(
        context_tokens, attention_full[2], preferred_element_type=f32
    ) + attention_full[3].astype(f32)
    gain_one = attention_full[4].astype(f32)
    normed_one, normal_one, inverse_one = norm_forward(
        tokens.astype(f32) + attended, gain_one, attention_full[5].astype(f32)
    )
    feed_full = (
        lax.all_gather(up_weight.astype(bf16), "fsdp", axis=0, tiled=True),
        lax.all_gather(up_bias.astype(bf16), "fsdp", axis=0, tiled=True),
        lax.all_gather(down_weight.astype(bf16), "fsdp", axis=0, tiled=True),
        lax.all_gather(down_bias.astype(bf16), "fsdp", axis=0, tiled=True),
        lax.all_gather(second_gain.astype(bf16), "fsdp", axis=0, tiled=True),
        lax.all_gather(second_shift.astype(bf16), "fsdp", axis=0, tiled=True),
    )
    normed_low = normed_one.astype(bf16)
    lifted = jnp.dot(normed_low, feed_full[0], preferred_element_type=f32) + feed_full[1].astype(
        f32
    )
    activated = jax.nn.gelu(lifted, approximate=False).astype(bf16)
    lowered = jnp.dot(activated, feed_full[2], preferred_element_type=f32) + feed_full[3].astype(
        f32
    )
    gain_two = feed_full[4].astype(f32)
    layer_out, normal_two, inverse_two = norm_forward(
        normed_one + lowered, gain_two, feed_full[5].astype(f32)
    )
    feed_back = (
        lax.all_gather(up_weight.astype(bf16), "fsdp", axis=0, tiled=True),
        lax.all_gather(up_bias.astype(bf16), "fsdp", axis=0, tiled=True),
        lax.all_gather(down_weight.astype(bf16), "fsdp", axis=0, tiled=True),
        lax.all_gather(down_bias.astype(bf16), "fsdp", axis=0, tiled=True),
        lax.all_gather(second_gain.astype(bf16), "fsdp", axis=0, tiled=True),
        lax.all_gather(second_shift.astype(bf16), "fsdp", axis=0, tiled=True),
    )
    attention_back = (
        lax.all_gather(projection.astype(bf16), "fsdp", axis=0, tiled=True),
        lax.all_gather(projection_bias.astype(bf16), "fsdp", axis=0, tiled=True),
        lax.all_gather(output_weight.astype(bf16), "fsdp", axis=0, tiled=True),
        lax.all_gather(output_bias.astype(bf16), "fsdp", axis=0, tiled=True),
        lax.all_gather(first_gain.astype(bf16), "fsdp", axis=0, tiled=True),
        lax.all_gather(first_shift.astype(bf16), "fsdp", axis=0, tiled=True),
    )
    grad_two, second_gain_grad, second_shift_grad = norm_backward(
        cotangent[0].astype(f32), normal_two, inverse_two, gain_two
    )
    lowered_grad = grad_two.astype(bf16)
    down_weight_grad = jnp.einsum("tf,td->fd", activated, lowered_grad, preferred_element_type=f32)
    down_bias_grad = jnp.sum(lowered_grad.astype(f32), axis=0)
    active_grad = jnp.einsum("td,fd->tf", lowered_grad, feed_back[2], preferred_element_type=f32)
    unused, gelu_pull = jax.vjp(partial(jax.nn.gelu, approximate=False), lifted)
    lifted_grad = gelu_pull(active_grad)[0].astype(bf16)
    up_weight_grad = jnp.einsum("td,tf->df", normed_low, lifted_grad, preferred_element_type=f32)
    up_bias_grad = jnp.sum(lifted_grad.astype(f32), axis=0)
    normed_grad = grad_two + jnp.einsum(
        "tf,df->td", lifted_grad, feed_back[0], preferred_element_type=f32
    )
    grad_one, first_gain_grad, first_shift_grad = norm_backward(
        normed_grad, normal_one, inverse_one, attention_back[4].astype(f32)
    )
    attended_grad = grad_one.astype(bf16)
    output_weight_grad = jnp.einsum(
        "tc,td->cd", context_tokens, attended_grad, preferred_element_type=f32
    )
    output_bias_grad = jnp.sum(attended_grad.astype(f32), axis=0)
    context_grad = jnp.einsum(
        "td,cd->tc", attended_grad, attention_back[2], preferred_element_type=f32
    ).astype(bf16)
    context_grad = context_grad.reshape(local_rows, HEADS, HEAD_DIM)
    context_grad_heads = lax.all_to_all(
        context_grad, "seq", split_axis=1, concat_axis=0, tiled=True
    )
    grad_blocks = context_grad_heads.reshape(count, block, local_heads, HEAD_DIM)

    def backward_block(carry, pieces):
        key_grad, value_grad = carry
        query_block, segment_block, grad_block, log_block = pieces
        scores = scores_of(query_block, segment_block)
        weights = jnp.exp(scores - log_block[..., None])
        value_grad = value_grad + jnp.einsum(
            "hqk,qhd->khd", weights.astype(bf16), grad_block, preferred_element_type=f32
        )
        weight_grad = jnp.einsum("qhd,khd->hqk", grad_block, value_all, preferred_element_type=f32)
        centre = jnp.sum(weights * weight_grad, axis=-1, keepdims=True)
        score_grad = (weights * (weight_grad - centre)).astype(bf16)
        query_grad = (
            jnp.einsum("hqk,khd->qhd", score_grad, key_all, preferred_element_type=f32) * scale
        )
        key_grad = (
            key_grad
            + jnp.einsum("hqk,qhd->khd", score_grad, query_block, preferred_element_type=f32)
            * scale
        )
        return ((key_grad, value_grad), query_grad)

    zeros_heads = jnp.zeros((length, local_heads, HEAD_DIM), f32)
    (key_grad, value_grad), query_grad = lax.scan(
        backward_block,
        (zeros_heads, zeros_heads),
        (query_blocks, segment_blocks, grad_blocks, log_totals),
    )
    query_grad = query_grad.reshape(length, local_heads, HEAD_DIM)
    stacked_grad = jnp.stack([query_grad, key_grad, value_grad]).astype(bf16)
    token_heads = lax.all_to_all(stacked_grad, "seq", split_axis=1, concat_axis=2, tiled=True)
    query_back = rotary_back(token_heads[0].astype(f32), positions)
    key_back = rotary_back(token_heads[1].astype(f32), positions)
    projected_grad = jnp.stack([query_back, key_back, token_heads[2].astype(f32)], axis=1)
    projected_grad = projected_grad.reshape(local_rows, 3 * width).astype(bf16)
    projection_grad = jnp.einsum("td,te->de", tokens, projected_grad, preferred_element_type=f32)
    projection_bias_grad = jnp.sum(projected_grad.astype(f32), axis=0)
    input_grad = grad_one + jnp.einsum(
        "te,de->td", projected_grad, attention_back[0], preferred_element_type=f32
    )
    every_shard = (
        lax.psum_scatter(
            projection_grad.astype(jnp.bfloat16), "fsdp", scatter_dimension=0, tiled=True
        ).astype(jnp.float32),
        lax.psum_scatter(
            projection_bias_grad.astype(jnp.bfloat16), "fsdp", scatter_dimension=0, tiled=True
        ).astype(jnp.float32),
        lax.psum_scatter(
            output_weight_grad.astype(jnp.bfloat16), "fsdp", scatter_dimension=0, tiled=True
        ).astype(jnp.float32),
        lax.psum_scatter(
            output_bias_grad.astype(jnp.bfloat16), "fsdp", scatter_dimension=0, tiled=True
        ).astype(jnp.float32),
        lax.psum_scatter(
            first_gain_grad.astype(jnp.bfloat16), "fsdp", scatter_dimension=0, tiled=True
        ).astype(jnp.float32),
        lax.psum_scatter(
            first_shift_grad.astype(jnp.bfloat16), "fsdp", scatter_dimension=0, tiled=True
        ).astype(jnp.float32),
        lax.psum_scatter(
            up_weight_grad.astype(jnp.bfloat16), "fsdp", scatter_dimension=0, tiled=True
        ).astype(jnp.float32),
        lax.psum_scatter(
            up_bias_grad.astype(jnp.bfloat16), "fsdp", scatter_dimension=0, tiled=True
        ).astype(jnp.float32),
        lax.psum_scatter(
            down_weight_grad.astype(jnp.bfloat16), "fsdp", scatter_dimension=0, tiled=True
        ).astype(jnp.float32),
        lax.psum_scatter(
            down_bias_grad.astype(jnp.bfloat16), "fsdp", scatter_dimension=0, tiled=True
        ).astype(jnp.float32),
        lax.psum_scatter(
            second_gain_grad.astype(jnp.bfloat16), "fsdp", scatter_dimension=0, tiled=True
        ).astype(jnp.float32),
        lax.psum_scatter(
            second_shift_grad.astype(jnp.bfloat16), "fsdp", scatter_dimension=0, tiled=True
        ).astype(jnp.float32),
    )
    finals = (
        lax.psum(every_shard[0].astype(jnp.bfloat16), "seq").astype(jnp.float32),
        lax.psum(every_shard[1].astype(jnp.bfloat16), "seq").astype(jnp.float32),
        lax.psum(every_shard[2].astype(jnp.bfloat16), "seq").astype(jnp.float32),
        lax.psum(every_shard[3].astype(jnp.bfloat16), "seq").astype(jnp.float32),
        lax.psum(every_shard[4].astype(jnp.bfloat16), "seq").astype(jnp.float32),
        lax.psum(every_shard[5].astype(jnp.bfloat16), "seq").astype(jnp.float32),
        lax.psum(every_shard[6].astype(jnp.bfloat16), "seq").astype(jnp.float32),
        lax.psum(every_shard[7].astype(jnp.bfloat16), "seq").astype(jnp.float32),
        lax.psum(every_shard[8].astype(jnp.bfloat16), "seq").astype(jnp.float32),
        lax.psum(every_shard[9].astype(jnp.bfloat16), "seq").astype(jnp.float32),
        lax.psum(every_shard[10].astype(jnp.bfloat16), "seq").astype(jnp.float32),
        lax.psum(every_shard[11].astype(jnp.bfloat16), "seq").astype(jnp.float32),
    )
    return (
        layer_out.astype(bf16)[None],
        input_grad.astype(bf16)[None],
        finals[0],
        finals[1],
        finals[2],
        finals[3],
        finals[4],
        finals[5],
        finals[6],
        finals[7],
        finals[8],
        finals[9],
        finals[10],
        finals[11],
    )


def solution(mesh):
    return jax.shard_map(
        shards,
        mesh=mesh,
        in_specs=(
            P("fsdp", "seq", None),
            P("fsdp", "seq", None),
            P("fsdp", None),
            P("fsdp", None),
            P("fsdp"),
            P("fsdp", None),
            P("fsdp"),
            P("fsdp"),
            P("fsdp"),
            P("fsdp", None),
            P("fsdp"),
            P("fsdp", None),
            P("fsdp"),
            P("fsdp"),
            P("fsdp"),
        ),
        out_specs=(
            P("fsdp", "seq", None),
            P("fsdp", "seq", None),
            P("fsdp", None),
            P("fsdp"),
            P("fsdp", None),
            P("fsdp"),
            P("fsdp"),
            P("fsdp"),
            P("fsdp", None),
            P("fsdp"),
            P("fsdp", None),
            P("fsdp"),
            P("fsdp"),
            P("fsdp"),
        ),
        check_vma=False,
    )
```

profile of v0, /device:TPU:0, one launch (start us, length us, event | category | flops | bytes accessed | tf_op | source)
XLA Modules:
  0.0 1095.8 jit_solution(2755099073005826115)
XLA Ops:
  7.2 3.3 convert_element_type.266
  11.7 3.8 convert_element_type.279
  15.5 3.8 convert_element_type.283
  20.1 17.3 %all-gather = bf16[4,1,768]{2,1,0:T(2,128)(2,1)S(1)} all-gather(bf16[1,1,768]{2,1,0:T(2,128)(2,1)S(1)} %reshape.288), channel_id=1, replica_groups=mesh['seq'=8,'fsdp'=4] {'fsdp'}, dimensions={0}, use_global_device_ids=true | all-gather | bytes 7680 | tf_op jit(solution)/shard_map/all_gather | solution.py:81
  37.5 91.4 %all-gather.12.cloned.1.call-done = bf16[1024,3072]{1,0:T(8,128)(2,1)} async-done(((bf16[256,3072]{1,0:T(8,128)(2,1)}), bf16[1024,3072]{1,0:T(8,128)(2,1)}) %all-gather.12.cloned.1.call-update) | async-done | bytes 6291472 | tf_op jit(solution)/shard_map/all_gather | solution.py:80
  128.9 3.8 convolution_add_fusion.1
  134.6 3.7 all-to-all-start
  139.4 11.4 %all-to-all-done = bf16[3,128,16,64]{1,3,0,2:T(8,128)(2,1)S(1)} async-done(((bf16[3,128,16,64]{1,3,0,2:T(8,128)(2,1)}), bf16[3,128,16,64]{1,3,0,2:T(8,128)(2,1)S(1)}, u32[]{:S(2)}, u32[]{:S(2)}) %all-to-all-start) | async-done | bytes 786464 | tf_op jit(solution)/shard_map/all_to_all | solution.py:95
  153.2 12.0 %while.27 = (s32[]{:T(128)}, bf16[2,512,2,64]{1,3,2,0:T(8,128)(2,1)S(1)}, f32[2,2,512]{2,1,0:T(2,128)S(1)}, s32[2,512]{1,0:T(2,128)S(1)}, s32[1,1024]{1,0:T(1,12...) while((s32[]{:T(128)}, ...), condition=%wide.region_3.4_spmd, body=%wide.region_0.3_spmd.sunk | while | flops 281607168 | bytes 15509621 | solution.py:123
  156.7 2.4 fusion.125
  162.8 2.4 fusion.125
  166.8 3.4 all-to-all-start.1
  170.3 8.2 all-gather.4
  178.5 12.0 %all_gather.48 = bf16[4096]{0:T(1024)(128)(2,1)S(1)} all-gather(bf16[1024]{0:T(1024)(128)(2,1)S(1)} %convert_element_type.280), channel_id=1, replica_groups=mesh['seq'=8,'fsdp'=4] {'fsdp'}, dimensions={0}, use_global_device_ids=true | all-gather | bytes 10240 | tf_op jit(solution)/shard_map/all_gather | solution.py:137
  190.6 8.1 all-gather.1
  198.7 10.4 all-gather.3
  209.1 9.6 all-gather.2
  218.8 10.4 all-gather.5
  229.2 12.5 %all-gather.6 = bf16[4,1,256]{2,1,0:T(2,128)(2,1)S(1)} all-gather(bf16[1,1,256]{2,1,0:T(2,128)(2,1)S(1)} %reshape.300), channel_id=1, replica_groups=mesh['seq'=8,'fsdp'=4] {'fsdp'}, dimensions={0}, use_global_device_ids=true | all-gather | bytes 2560 | tf_op jit(solution)/shard_map/all_gather | solution.py:141
  244.8 80.7 %all-gather.16.cloned.1.call-done = bf16[1024,4096]{1,0:T(8,128)(2,1)} async-done(((bf16[256,4096]{1,0:T(8,128)(2,1)}), bf16[1024,4096]{1,0:T(8,128)(2,1)}) %all-gather.16.cloned.1.call-update) | async-done | bytes 8388624 | tf_op jit(solution)/shard_map/all_gather | solution.py:136
  325.5 9.1 multiply_convert_fusion.1
  334.6 140.9 %all-gather.18.cloned.1.call-done = bf16[4096,1024]{1,0:T(8,128)(2,1)} async-done(((bf16[1024,1024]{1,0:T(8,128)(2,1)}), bf16[4096,1024]{1,0:T(8,128)(2,1)}) %all-gather.18.cloned.1.call-update) | async-done | bytes 8388624 | tf_op jit(solution)/shard_map/all_gather | solution.py:138
  475.5 4.9 fusion.78
  482.4 7.5 fusion.79
  490.0 3.1 multiply_reduce_fusion.1
  495.0 3.7 all-to-all-start.2
  501.0 4.6 all-to-all-done.2
  506.6 28.3 %while.28 = (s32[]{:T(128)}, f32[1024,2,64]{0,2,1:T(8,128)}, f32[1024,2,64]{0,2,1:T(8,128)}, bf16[2,512,2,64]{1,3,2,0:T(8,128)(2,1)}, bf16[2,512,2,64]{1,3,2,0:T...) while((s32[]{:T(128)}, f32[1024,2,64]{0,2,1:T(8,128)}, ...), condition=%wide.region_14.15_spmd.clone, body=%wide.region_12.14_spmd.clone.sunk | while | flops 688061440 | bytes 60332340 | solution.py:224
  508.7 3.1 multiply_reduce_fusion.7
  513.2 2.3 fusion.136
  515.4 3.7 fusion.137
  522.7 3.1 multiply_reduce_fusion.7
  527.2 2.5 fusion.136
  529.7 3.7 fusion.137
  541.0 15.7 %all_to_all.60 = bf16[8,2,24576]{2,1,0:T(2,128)(2,1)} all-to-all(bf16[8,2,24576]{2,1,0:T(2,128)(2,1)S(1)} %reshape.328), channel_id=1, replica_groups=mesh['seq'=8,'fsdp'=4] {'seq'}, dimensions={0} | all-to-all | bytes 1572864 | tf_op jit(solution)/shard_map/all_to_all | solution.py:231
  562.6 4.4 convert_bitcast_fusion
  568.3 5.7 convolution_convert_fusion.1
  575.3 5.6 convolution_convert_fusion
  581.0 93.3 %reduce-scatter.5.cloned.1.call-done = bf16[256,3072]{0,1:T(8,128)(2,1)} async-done(((bf16[1024,3072]{0,1:T(8,128)(2,1)}), bf16[256,3072]{0,1:T(8,128)(2,1)}) %reduce-scatter.5.cloned.1.call-update) | async-done | bytes 1572880 | tf_op jit(solution)/shard_map/reduce_scatter | solution.py:242
  674.3 147.5 %reduce-scatter.9.cloned.1.call-done = bf16[256,4096]{1,0:T(8,128)(2,1)} async-done(((bf16[1024,4096]{1,0:T(8,128)(2,1)}), bf16[256,4096]{1,0:T(8,128)(2,1)}) %reduce-scatter.9.cloned.1.call-update) | async-done | bytes 2097168 | tf_op jit(solution)/shard_map/reduce_scatter | solution.py:260
  821.8 147.7 %reduce-scatter.11.cloned.1.call-done = bf16[1024,1024]{1,0:T(8,128)(2,1)} async-done(((bf16[4096,1024]{1,0:T(8,128)(2,1)}), bf16[1024,1024]{1,0:T(8,128)(2,1)}) %reduce-scatter.11.cloned.1.call-update) | async-done | bytes 2097168 | tf_op jit(solution)/shard_map/reduce_scatter | solution.py:266
  973.1 18.4 %all-reduce.14 = (bf16[3072]{0:T(1024)(128)(2,1)S(1)}, bf16[1024]{0:T(1024)(128)(2,1)S(1)}, bf16[1024]{0:T(1024)(128)(2,1)S(1)}, bf16[1024]{0:T(1024)(128)(2,1)S...) all-reduce(bf16[3072]{0:T(1024)(128)(2,1)S(1)} %reduce_sum.188, ...), channel_id=3, replica_groups=mesh['seq'=8,'fsdp'=4] {'fsdp'}, use_global_device_ids=true, to_apply=%region_18.19.clone | all-reduce | flops 13312 | bytes 53248
  992.1 13.4 %all-reduce.12 = (bf16[768]{0:T(1024)(128)(2,1)S(1)}, bf16[256]{0:T(256)(128)(2,1)S(1)}, bf16[256]{0:T(256)(128)(2,1)S(1)}, bf16[256]{0:T(256)(128)(2,1)S(1)}, b...) all-reduce(bf16[768]{0:T(1024)(128)(2,1)S(1)} %dynamic-slice.1, ...), channel_id=1, replica_groups=mesh['seq'=8,'fsdp'=4] {'seq'}, use_global_device_ids=true, to_apply=%region_19.20 | all-reduce | flops 3328 | bytes 13312 | tf_op jit(solution)/shard_map/psum | solution.py:281
  1010.0 5.7 fusion.51
  1015.7 63.8 %all-reduce.17.cloned.1.call-done = (bf16[256,3072]{0,1:T(8,128)(2,1)}, bf16[256,1024]{1,0:T(8,128)(2,1)}, bf16[256,4096]{1,0:T(8,128)(2,1)}, bf16[1024,1024]{1,0:T(8,128)(2,1)}) async-done(((bf16[256,3072]{0,1:T(8,128)(2,1)}, bf16[256,1024]{1,0:T(8,128)(2,1)}, bf16[256,4096]{1,0:T(8,128)(2,1)}, bf16[1024,1024]{1,0:T(8,128)(2,1)}), (bf16[256,3072]{0,1:T(8,128)(2,1)}, bf16[256,1024]{1,0:T(8,128)(2,1)}, ...) | async-done | bytes 6291472 | tf_op jit(solution)/shard_map/psum | solution.py:280
  1079.5 3.2 copy.77
  1083.8 2.5 convert_element_type.318
  1086.3 2.5 convert_element_type.321
  (247 shorter events, 58.4 us)
Async XLA Ops:
  7.2 3.5 copy-start.17
  7.2 121.7 %all-gather.12.cloned.1.call-start = ((), (), s32[]{:S(2)}) async-start(), calls=%async_computation.8 | async-start | bytes 7864320 | tf_op jit(solution)/shard_map/all_gather | solution.py:80
  10.6 231.8 %all-gather.14.cloned.1.call-start = ((), (), s32[]{:S(2)}) async-start(), calls=%async_computation.9 | async-start | bytes 2621440 | tf_op jit(solution)/shard_map/all_gather | solution.py:82
  11.6 313.9 %all-gather.16.cloned.1.call-start = ((), (), s32[]{:S(2)}) async-start(), calls=%async_computation.10 | async-start | bytes 10485760 | tf_op jit(solution)/shard_map/all_gather | solution.py:136
  15.5 460.0 %all-gather.18.cloned.1.call-start = ((), (), s32[]{:S(2)}) async-start(), calls=%async_computation.11 | async-start | bytes 10485760 | tf_op jit(solution)/shard_map/all_gather | solution.py:138
  19.4 109.6 %copy-start.11 = (bf16[1,128,1024]{2,1,0:T(8,128)(2,1)S(1)}, bf16[1,128,1024]{2,1,0:T(8,128)(2,1)}, u32[]{:S(2)}) copy-start(bf16[1,128,1024]{2,1,0:T(8,128)(2,1)} %param.19) | copy-start | bytes 786436
  37.5 95.7 %copy-start.24 = (f32[128,32]{0,1:T(8,128)}, f32[128,32]{0,1:T(8,128)S(1)}, u32[]{:S(2)}) copy-start(f32[128,32]{0,1:T(8,128)S(1)} %get-tuple-element.366) | copy-start | bytes 49156
  37.5 95.7 %copy-start.26 = (f32[128,32]{0,1:T(8,128)}, f32[128,32]{0,1:T(8,128)S(1)}, u32[]{:S(2)}) copy-start(f32[128,32]{0,1:T(8,128)S(1)} %get-tuple-element.367) | copy-start | bytes 49156
  133.5 5.2 copy-start.21
  134.6 16.3 %all-to-all-start = ((bf16[3,128,16,64]{1,3,0,2:T(8,128)(2,1)}), bf16[3,128,16,64]{1,3,0,2:T(8,128)(2,1)S(1)}, u32[]{:S(2)}, u32[]{:S(2)}) async-start(bf16[3,128,16,64]{1,3,0,2:T(8,128)(2,1)} %copy.63), calls=%async_computation | async-start | bytes 1572864 | tf_op jit(solution)/shard_map/all_to_all | solution.py:95
  165.2 5.0 copy-start.30
  165.3 13.3 %copy-start.29 = (f32[1024]{0:T(1024)S(1)}, f32[1024]{0:T(1024)}, u32[]{:S(2)}) copy-start(f32[1024]{0:T(1024)} %param.29) | copy-start | bytes 12292
  165.3 25.3 %copy-start.31 = (f32[256]{0:T(256)S(1)}, f32[256]{0:T(256)}, u32[]{:S(2)}) copy-start(f32[256]{0:T(256)} %param.25) | copy-start | bytes 3076
  165.3 33.4 %copy-start.32 = (f32[256]{0:T(256)S(1)}, f32[256]{0:T(256)}, u32[]{:S(2)}) copy-start(f32[256]{0:T(256)} %param.27) | copy-start | bytes 3076
  165.3 43.8 %copy-start.33 = (f32[256]{0:T(256)S(1)}, f32[256]{0:T(256)}, u32[]{:S(2)}) copy-start(f32[256]{0:T(256)} %param.26) | copy-start | bytes 3076
  165.3 53.4 %copy-start.34 = (f32[256]{0:T(256)S(1)}, f32[256]{0:T(256)}, u32[]{:S(2)}) copy-start(f32[256]{0:T(256)} %param.32) | copy-start | bytes 3076
  165.3 63.9 %copy-start.35 = (f32[256]{0:T(256)S(1)}, f32[256]{0:T(256)}, u32[]{:S(2)}) copy-start(f32[256]{0:T(256)} %param.33) | copy-start | bytes 3076
  166.8 74.9 %all-to-all-start.1 = ((bf16[8,2,8192]{2,1,0:T(2,128)(2,1)}), bf16[8,2,8192]{2,1,0:T(2,128)(2,1)S(1)}, u32[]{:S(2)}, u32[]{:S(2)}) async-start(bf16[8,2,8192]{2,1,0:T(2,128)(2,1)} %reshape.326), calls=%async_computation.1 | async-start | bytes 524288 | tf_op jit(solution)/shard_map/all_to_all | solution.py:125
  334.6 145.8 %copy-start.2 = (bf16[128,4096]{1,0:T(8,128)(2,1)}, bf16[128,4096]{1,0:T(8,128)(2,1)S(1)}, u32[]{:S(2)}) copy-start(bf16[128,4096]{1,0:T(8,128)(2,1)S(1)} %get-tuple-element.370) | copy-start | bytes 3145732
  475.5 6.4 slice-start
  475.5 5.2 copy-start.13
  475.5 6.4 slice-start.1
  480.4 1.9 copy-start.37
  480.7 9.2 slice-start.2
  481.9 8.0 copy-start.7
  482.4 7.6 slice-start.3
  489.9 3.1 copy-start.9
  490.0 3.3 copy-start.4
  493.3 7.4 copy-start.5
  495.0 10.6 all-to-all-start.2
  498.6 82.4 %reduce-scatter.7.cloned.1.call-start = ((), (), s32[]{:S(2)}) async-start(), calls=%async_computation.13 | async-start | bytes 2621440 | tf_op jit(solution)/shard_map/reduce_scatter | solution.py:248
  500.7 173.5 %reduce-scatter.5.cloned.1.call-start = ((), (), s32[]{:S(2)}) async-start(), calls=%async_computation.12 | async-start | bytes 7864320 | tf_op jit(solution)/shard_map/reduce_scatter | solution.py:242
  508.3 3.5 copy-start
  513.2 2.3 copy-start.19
  515.4 3.7 copy-start.22
  522.3 3.5 copy-start
  527.2 2.5 copy-start.19
  529.7 3.7 copy-start.22
  534.9 2.5 copy-start.1
  567.1 254.7 %reduce-scatter.9.cloned.1.call-start = ((), (), s32[]{:S(2)}) async-start(), calls=%async_computation.14 | async-start | bytes 10485760 | tf_op jit(solution)/shard_map/reduce_scatter | solution.py:260
  574.0 1.2 copy-start.3
  574.0 1.4 copy-start.8
  574.0 395.5 %reduce-scatter.11.cloned.1.call-start = ((), (), s32[]{:S(2)}) async-start(), calls=%async_computation.15 | async-start | bytes 10485760 | tf_op jit(solution)/shard_map/reduce_scatter | solution.py:266
  580.9 498.6 %all-reduce.17.cloned.1.call-start = ((), (), s32[]{:S(2)}) async-start(), calls=%async_computation.16 | async-start | bytes 12582912 | tf_op jit(solution)/shard_map/psum | solution.py:280
  969.5 40.6 %copy-start.6 = (f32[128,1024]{1,0:T(8,128)S(1)}, f32[128,1024]{1,0:T(8,128)}, u32[]{:S(2)}) copy-start(f32[128,1024]{1,0:T(8,128)} %copy-done.5) | copy-start | bytes 1572868
  1079.5 3.2 copy-start.18
  1079.5 4.3 copy-start.16
  1083.8 2.5 copy-start.15
  (11 other events, 9.3 us)
Sparse Core Ops, SparseCore 0:
  10.7 118.1 all-gather.11
  130.5 44.2 all-gather.13
  176.9 148.5 all-gather.15
  327.5 147.9 all-gather.17
  502.0 42.6 reduce-scatter.6
  567.2 107.0 reduce-scatter.4
  676.7 144.9 reduce-scatter.8
  824.2 145.1 reduce-scatter.10
  973.5 105.9 all-reduce.16
where the time goes:
time: 1100 us
  waiting for transfers between devices  781 us (71%)
  blocking collectives  136 us (12%)
  matrix products  86.9 us (8%)
  other arithmetic  34.1 us (3%)
  local copies, waits for them, and re-layouts  28.6 us (3%)
  between operations  17.1 us (2%)
  starting transfers between devices  11.5 us (1%)
    reduce_scatter x1, waiting for transfers between devices, shards(): lax.psum_scatter(down_weight_grad.astype(jnp.bfloat16), 'fsdp', scatter_d...  148 us
    reduce_scatter x1, waiting for transfers between devices, shards(): lax.psum_scatter(up_weight_grad.astype(jnp.bfloat16), 'fsdp', scatter_dim...  147 us
    all_gather x1, waiting for transfers between devices, shards(): lax.all_gather(down_weight.astype(bf16), 'fsdp', axis=0, tiled=True)  141 us
    reduce_scatter x1, waiting for transfers between devices, shards(): lax.psum_scatter(projection_grad.astype(jnp.bfloat16), 'fsdp', scatter_di...  93.3 us
    all_gather x1, waiting for transfers between devices, shards(): lax.all_gather(projection.astype(bf16), 'fsdp', axis=0, tiled=True)  91.4 us
    all_gather x1, waiting for transfers between devices, shards(): lax.all_gather(up_weight.astype(bf16), 'fsdp', axis=0, tiled=True)  80.7 us
    psum x1, waiting for transfers between devices, shards(): lax.psum(every_shard[0].astype(jnp.bfloat16), 'seq').astype(jnp.float32)  63.8 us
  transfers between devices with their start and end apart: 12, of which 9 were waited for; matrix products, arithmetic and copies ran while one was open for 10% of the time, Pallas kernels for 0%

commit v1 on v0

--- a/solution.py
+++ b/solution.py
@@ -2,7 +2,11 @@
 
 import jax
 import jax.numpy as jnp
+import numpy as np
+from types import SimpleNamespace
 from jax import lax
+from jax.experimental import pallas as pl
+from jax.experimental.pallas import tpu as pltpu
 from jax.sharding import PartitionSpec as P
 
 HEADS = 16
@@ -308,9 +312,807 @@
     )
 
 
+MESH = pl.DeviceIdType.MESH
+NN = (((1,), (0,)), ((), ()))
+NT = (((1,), (1,)), ((), ()))
+TN = (((0,), (0,)), ((), ()))
+f32 = jnp.float32
+bf16 = jnp.bfloat16
+MASKED = -1e30
+
+
+def mm(left, right, dims=NN):
+    return lax.dot_general(left, right, dims, preferred_element_type=f32)
+
+
+def block_of(index, size):
+    return pl.ds(pl.multiple_of(index * size, size), size)
+
+
+def flip(bit, other):
+    return bit + other - 2 * bit * other
+
+
+def fused_layer(sizes, *refs):
+    r = SimpleNamespace(**dict(zip(sizes.names, refs)))
+    T, D, L, F = sizes.T, sizes.D, sizes.L, sizes.F
+    S, Z = 8, 4
+    KW = D // Z
+    UZ = F // Z
+    C = 128
+    T2 = 2 * T
+    first_row = sizes.first_row
+    ssem, rsem, lsem = r.ssem, r.rsem, r.lsem
+
+    s = lax.axis_index("seq")
+    z = lax.axis_index("fsdp")
+    core, xbit, ybit = s % 2, (s // 2) % 2, s // 4
+    zlow, zhigh = z % 2, z // 2
+
+    def ps(k):
+        return flip(core, k % 2) + 2 * flip(xbit, (k // 2) % 2) + 4 * flip(ybit, k // 4)
+
+    def pz(k):
+        return flip(zlow, k % 2) + 2 * flip(zhigh, k // 2)
+
+    def chip_of(j):
+        return flip(xbit, j % 2) + 2 * flip(ybit, j // 2)
+
+    counter = [0, 0]
+    pending = []
+
+    def slots(n):
+        counter[0] += n
+        return counter[0] - n
+
+    def remote(src, dst, slot, dev):
+        return pltpu.make_async_remote_copy(
+            src_ref=src, dst_ref=dst, send_sem=ssem.at[slot], recv_sem=rsem.at[slot],
+            device_id=dev, device_id_type=MESH)
+
+    def send(src, dst, slot, dev):
+        copy = remote(src, dst, slot, dev)
+        copy.start()
+        pending.append(copy)
+        return copy
+
+    def drop(copies):
+        for copy in copies:
+            copy.wait_send()
+        pending[:] = [other for other in pending if all(other is not copy for copy in copies)]
+
+    def arrived(ref, slot):
+        remote(ref, ref, slot, (ps(1), z)).wait_recv()
+
+    def local(src, dst):
+        copy = pltpu.make_async_copy(src, dst, lsem.at[counter[1]])
+        counter[1] += 1
+        copy.start()
+        return copy
+
+    class Gather:
+        def __init__(self, place):
+            self.place, self.base = place, slots(8)
+
+        def start(self, src=None):
+            mine = self.place(s)
+            for k in (1, 2, 4, 6):
+                send(mine if src is None else src, mine, self.base + k, (ps(k), z))
+
+        def pass_on(self, k):
+            there = self.place(ps(k))
+            arrived(there, self.base + k)
+            send(there, there, self.base + k + 1, (ps(1), z))
+
+        def wait(self, k):
+            arrived(self.place(ps(k)), self.base + k)
+
+    class Spread:
+        def __init__(self, place):
+            self.place, self.base = place, slots(4)
+
+        def start(self):
+            mine = self.place(z)
+            for k in (2, 1):
+                send(mine, mine, self.base + k, (s, pz(k)))
+
+        def pass_on(self):
+            there = self.place(pz(2))
+            arrived(there, self.base + 2)
+            send(there, there, self.base + 3, (s, pz(1)))
+
+        def wait(self):
+            for k in (1, 3):
+                arrived(self.place(pz(k)), self.base + k)
+
+    class Fold:
+        def __init__(self, parts, landing, passing):
+            self.parts, self.landing, self.passing, self.base = parts, landing, passing, slots(3)
+
+        def start(self):
+            send(self.parts.at[pz(1)], self.landing.at[0], self.base, (s, pz(1)))
+            send(self.parts.at[pz(3)], self.landing.at[1], self.base + 1, (s, pz(1)))
+
+        def middle(self):
+            arrived(self.landing.at[1], self.base + 1)
+            self.passing[...] = (self.parts[pz(2)].astype(f32) + self.landing[1].astype(f32)).astype(bf16)
+            send(self.passing, self.landing.at[2], self.base + 2, (s, pz(2)))
+
+        def finish(self):
+            arrived(self.landing.at[0], self.base)
+            arrived(self.landing.at[2], self.base + 2)
+            return (self.parts[z].astype(f32) + self.landing[0].astype(f32)
+                    + self.landing[2].astype(f32)).astype(bf16)
+
+    class Scatter:
+        def __init__(self, parts, low, mid, high):
+            self.parts, self.low, self.mid, self.high, self.base = parts, low, mid, high, slots(8)
+            self.sent = []
+
+        def pair(self, j):
+            self.sent.append(send(self.parts.at[j, block_of(1 - core, T)], self.low.at[j],
+                                  self.base + j, (ps(1), z)))
+
+        def onward(self, j):
+            arrived(self.low.at[j], self.base + j)
+            own = self.parts[j, block_of(core, T), :].astype(f32)
+            self.mid[j] = (own + self.low[j].astype(f32)).astype(bf16)
+            self.sent.append(send(self.mid.at[j], self.high.at[j], self.base + 4 + j, (ps(2 * j), z)))
+
+        def ready(self):
+            arrived(self.low.at[0], self.base)
+            for j in (1, 2, 3):
+                arrived(self.high.at[j], self.base + 4 + j)
+
+        def rows(self, at, n):
+            own = self.parts[0, pl.ds(pl.multiple_of(core * T + at, n), n), :].astype(f32)
+            total = own + self.low[0, pl.ds(at, n), :].astype(f32)
+            for j in (1, 2, 3):
+                total = total + self.high[j, pl.ds(at, n), :].astype(f32)
+            return total
+
+    def loop(count, body, unroll=1):
+        def step(i, carry):
+            body(i)
+            return carry
+        lax.fori_loop(0, count, step, 0, unroll=unroll)
+
+    def at(i, n):
+        return pl.multiple_of(i * n, n)
+
+    vec, vecg = r.vec, r.vecg
+
+    OUTPUT_BIAS, FIRST_GAIN, FIRST_SHIFT, DOWN_BIAS, SECOND_GAIN, SECOND_SHIFT, PROJECTION_BIAS, UP_BIAS = range(8)
+    wide = ((first_row.output_bias, OUTPUT_BIAS), (first_row.first_gain, FIRST_GAIN),
+            (first_row.first_shift, FIRST_SHIFT), (first_row.down_bias, DOWN_BIAS),
+            (first_row.second_gain, SECOND_GAIN), (first_row.second_shift, SECOND_SHIFT))
+
+    def row(i, width=D):
+        return vec[i:i + 1, :width]
+
+    lanes = lax.broadcasted_iota(jnp.int32, (T, C), 1)
+    low_head = lanes < HEAD_DIM
+    low_half = lanes % HEAD_DIM < HEAD_DIM // 2
+
+    def swapped(w):
+        return jnp.where(low_half, pltpu.roll(w, C - HEAD_DIM // 2, 1), pltpu.roll(w, HEAD_DIM // 2, 1))
+
+    def stacked(w):
+        nothing = jnp.zeros_like(w)
+        return jnp.concatenate([jnp.where(low_head, w, nothing), jnp.where(low_head, nothing, w)], axis=0)
+
+    def unstacked(w):
+        return jnp.where(low_head, w[:T], w[T:])
+
+    proj_loads = [local(r.proj.at[:, block_of(i * (D // C) + s, C)], r.st_proj.at[:, pl.ds(i * C, C)])
+                  for i in range(3)]
+    wo_load = local(r.wo.at[:, block_of(s, C)], r.st_wo)
+    up_loads = [local(r.up.at[:, block_of(i * (D // C) + s, C)], r.st_up.at[:, pl.ds(i * C, C)])
+                for i in range(Z)]
+    dn_load = local(r.dn.at[block_of(s, UZ), :], r.st_dn)
+
+    barrier = pltpu.get_barrier_semaphore()
+    for k in range(1, S):
+        pl.semaphore_signal(barrier, inc=1, device_id=(ps(k), z), device_id_type=MESH)
+    for k in range(1, Z):
+        pl.semaphore_signal(barrier, inc=1, device_id=(s, pz(k)), device_id_type=MESH)
+    pl.semaphore_wait(barrier, S + Z - 2)
+
+    x_ref, x_all = r.x, r.x_all
+    w_qkv, w_o, w_up, w_dn = r.w_qkv, r.w_o, r.w_up, r.w_dn
+    gather_x = Gather(lambda o: x_all.at[block_of(o, T)])
+    gather_x.start(x_ref)
+    spread_qkv = Spread(lambda p: w_qkv.at[block_of(p, KW)])
+    spread_o = Spread(lambda p: w_o.at[block_of(p, KW), block_of(s, C)])
+    spread_up = Spread(lambda p: w_up.at[block_of(p, KW)])
+    spread_dn = Spread(lambda p: w_dn.at[block_of(p, UZ)])
+    gather_o = Gather(lambda o: w_o.at[:, block_of(o, C)])
+
+    for copy in proj_loads:
+        copy.wait()
+    w_qkv[block_of(z, KW), :] = r.st_proj[...].astype(bf16)
+    spread_qkv.start()
+
+    small_all = r.small_all
+    small_base = slots(4)
+    small_all[z] = r.small[...]
+    for k in (1, 2, 3):
+        send(r.small, small_all.at[z], small_base + k, (s, pz(k)))
+
+    x_all[block_of(s, T), :] = x_ref[...]
+    wo_load.wait()
+    w_o[block_of(z, KW), block_of(s, C)] = r.st_wo[...].astype(bf16)
+    spread_o.start()
+    for copy in up_loads:
+        copy.wait()
+    w_up[block_of(z, KW), :] = r.st_up[...].astype(bf16)
+    dn_load.wait()
+    w_dn[block_of(z, UZ), :] = r.st_dn[...].astype(bf16)
+    for i in range(8):
+        vecg[i:i + 1, :] = jnp.zeros((1, D), f32)
+
+    spread_qkv.pass_on()
+    gather_x.pass_on(2)
+    gather_x.pass_on(4)
+    spread_o.pass_on()
+    spread_up.start()
+    gather_x.pass_on(6)
+    for k in (1, 2, 3):
+        arrived(small_all.at[pz(k)], small_base + k)
+    for p in range(Z):
+        for start, i in wide:
+            for half in range(KW // C):
+                at_row = start + half
+                lane = (p * (KW // C) + half) * C
+                vec[i:i + 1, lane:lane + C] = small_all[p, at_row:at_row + 1, :]
+        vec[7:8, p * C:(p + 1) * C] = small_all[p, pl.ds(first_row.up_bias + s, 1), :]
+    per = 3 * D // (C * Z)
+    for t in range(3):
+        number = t * (D // C) + s
+        vec[6:7, t * C:(t + 1) * C] = small_all[number // per, pl.ds(first_row.projection_bias + number % per, 1), :]
+    for k in (1, 3, 5, 7):
+        gather_x.wait(k)
+
+    x_t = r.x_t
+    spread_qkv.wait()
+    spread_o.wait()
+    gather_o.start()
+    q_ref, k_ref, v_ref = r.q, r.k, r.v
+    scale = HEAD_DIM ** -0.5
+
+    def project(i):
+        here = pl.ds(at(i, T), T)
+        out = mm(x_all[here, :], w_qkv[...]) + row(PROJECTION_BIAS, 3 * C)
+        cosine, sine = r.cos[here, :], r.sin[here, :]
+        q0, k0 = out[:, :C], out[:, C:2 * C]
+        q_ref[here, :] = ((q0 * cosine + swapped(q0) * sine).astype(bf16).astype(f32) * scale).astype(bf16)
+        k_ref[here, :] = (k0 * cosine + swapped(k0) * sine).astype(bf16)
+        v_ref[here, :] = out[:, 2 * C:].astype(bf16)
+    loop(L // T, project)
+
+    s_buf, p_buf, col_a, col_b = r.s_buf, r.p_buf, r.col_a, r.col_b
+    segr, segc = r.segr, r.segc
+    lse, c_f, c_heads, c_tok = r.lse, r.c_f, r.c_heads, r.c_tok
+    R = 16
+
+    def attend(o):
+        here = block_of(o, T)
+        s_buf[...] = mm(stacked(q_ref[here, :]), k_ref[...], NT)
+
+        def chunk(i):
+            rows = pl.ds(at(i, R), R)
+            same = segc[pl.ds(pl.multiple_of(o * T + (i % (T // R)) * R, R), R), :] == segr[...]
+            score = jnp.where(same, s_buf[rows, :], MASKED)
+            top = jnp.max(score, axis=-1, keepdims=True)
+            power = jnp.exp(score - top)
+            total = jnp.sum(power, axis=-1, keepdims=True)
+            p_buf[rows, :] = power.astype(bf16)
+            col_a[rows, :] = jnp.broadcast_to(1.0 / total, (R, C))
+            col_b[rows, :] = jnp.broadcast_to(top + jnp.log(total), (R, C))
+        loop(T2 // R, chunk)
+        context = unstacked(mm(p_buf[...], v_ref[...]) * col_a[...])
+        c_f[here, :] = context
+        c_heads[here, :] = context.astype(bf16)
+        for h in range(2):
+            lse[h:h + 1, here] = jnp.transpose(col_b[h * T:(h + 1) * T, :])[0:1, :]
+
+    c_base = slots(8)
+
+    def c_copy(k):
+        return remote(c_heads.at[block_of(ps(k), T)], c_tok.at[:, block_of(s, C)], c_base + k, (ps(k), z))
+
+    def attend_and_send(i):
+        k = 7 - i
+        attend(ps(k))
+        c_copy(k).start()
+
+    loop(3, attend_and_send)
+    spread_up.pass_on()
+    spread_dn.start()
+    loop(2, lambda i: attend_and_send(i + 3))
+    gather_o.pass_on(2)
+    gather_o.pass_on(4)
+    loop(2, lambda i: attend_and_send(i + 5))
+    attend(s)
+    gather_o.pass_on(6)
+    c_tok[:, block_of(s, C)] = c_heads[block_of(s, T), :]
+    for k in (1, 3, 5, 7):
+        gather_o.wait(k)
+    for k in range(1, 8):
+        arrived(c_tok.at[:, block_of(ps(k), C)], c_base + k)
+
+    a_buf = r.a_buf
+    a_buf[...] = mm(c_tok[...], w_o[...])
+    n1, y1, r1, y_all = r.n1, r.y1, r.r1, r.y_all
+
+    def norm(h):
+        centre = h - jnp.mean(h, axis=-1, keepdims=True)
+        root = lax.rsqrt(jnp.mean(centre * centre, axis=-1, keepdims=True) + norm_epsilon)
+        return centre * root, root
+
+    def first_norm(i):
+        rows = pl.ds(at(i, R), R)
+        normal, root = norm(x_ref[rows, :].astype(f32) + a_buf[rows, :] + row(OUTPUT_BIAS))
+        out = normal * row(FIRST_GAIN) + row(FIRST_SHIFT)
+        n1[rows, :] = normal
+        r1[rows, :] = jnp.broadcast_to(root, (R, C))
+        y1[rows, :] = out
+        y_all[pl.ds(pl.multiple_of(s * T + i * R, R), R), :] = out.astype(bf16)
+    loop(T // R, first_norm)
+    gather_y = Gather(lambda o: y_all.at[block_of(o, T)])
+    gather_y.start()
+
+    u_buf, g_ref, d_ref, du_ref, dz_all = r.u_buf, r.g, r.d, r.du, r.dz_all
+    parts, mid = r.parts, r.mid
+    spread_dn.pass_on()
+    spread_up.wait()
+    E = 32
+
+    def lift(j):
+        q = chip_of(j)
+        u_buf[...] = mm(y_all[block_of(q, T2), :], w_up[...])
+
+        def chunk(i):
+            rows = pl.ds(at(i, E), E)
+            there = pl.ds(pl.multiple_of(q * T2 + i * E, E), E)
+            u = u_buf[rows, :] + row(UP_BIAS, F)
+            share = 0.5 + 0.5 * lax.erf(u * (0.5 ** 0.5))
+            g_ref[there, :] = (u * share).astype(bf16)
+            d_ref[there, :] = share + u * (jnp.exp(-0.5 * u * u) * 0.3989422804014327)
+        loop(T2 // E, chunk)
+
+    def lower(j):
+        parts[j] = mm(g_ref[block_of(chip_of(j), T2), :], w_dn[...]).astype(bf16)
+
+    fold_z = Scatter(parts, r.low0, mid, r.high0)
+    gather_y.wait(1)
+    lift(0)
+    spread_dn.wait()
+    lower(0)
+    fold_z.pair(0)
+    gather_y.pass_on(2)
+    gather_y.pass_on(4)
+    gather_y.wait(3)
+    lift(1)
+    lower(1)
+    fold_z.pair(1)
+    gather_y.wait(5)
+    lift(2)
+    fold_z.onward(1)
+    lower(2)
+    fold_z.pair(2)
+    gather_y.pass_on(6)
+    gather_y.wait(7)
+    lift(3)
+    fold_z.onward(2)
+    lower(3)
+    fold_z.pair(3)
+    fold_z.onward(3)
+    y_t, g_t = r.y_t, r.g_t
+
+    def turn(src, dst, wide):
+        def one(i):
+            dst[:, pl.ds(at(i, T), T)] = jnp.transpose(src[pl.ds(at(i, T), T), :])
+        loop(L // T, one)
+    turn(g_ref, g_t, F)
+    fold_z.ready()
+
+    dh2, out_ref, ct_ref = r.dh2, r.out, r.ct
+
+    def add_row(i, value):
+        vecg[i:i + 1, :] = vecg[i:i + 1, :] + jnp.sum(value, axis=0, keepdims=True)
+
+    def norm_back(incoming, normal, root, gain):
+        scaled = incoming * gain
+        return root * (scaled - jnp.mean(scaled, axis=-1, keepdims=True)
+                       - normal * jnp.mean(scaled * normal, axis=-1, keepdims=True))
+
+    def second_norm(i):
+        start = at(i, R)
+        rows = pl.ds(start, R)
+        normal, root = norm(y1[rows, :] + fold_z.rows(start, R) + row(DOWN_BIAS))
+        out_ref[rows, :] = (normal * row(SECOND_GAIN) + row(SECOND_SHIFT)).astype(bf16)
+        e = ct_ref[rows, :].astype(f32)
+        grad = norm_back(e, normal, root, row(SECOND_GAIN))
+        dh2[rows, :] = grad
+        dz = grad.astype(bf16)
+        dz_all[pl.ds(pl.multiple_of(s * T + i * R, R), R), :] = dz
+        add_row(3, dz.astype(f32))
+        add_row(4, e * normal)
+        add_row(5, e)
+    loop(T // R, second_norm)
+    gather_dz = Gather(lambda o: dz_all.at[block_of(o, T)])
+    gather_dz.start()
+    drop(fold_z.sent)
+
+    colg = r.colg
+    colg[...] = jnp.zeros((8, F), f32)
+
+    def unlower(j):
+        q = chip_of(j)
+        u_buf[...] = mm(dz_all[block_of(q, T2), :], w_dn[...], NT)
+
+        def chunk(i):
+            rows = pl.ds(at(i, E), E)
+            there = pl.ds(pl.multiple_of(q * T2 + i * E, E), E)
+            du = (u_buf[rows, :] * d_ref[there, :]).astype(bf16)
+            du_ref[there, :] = du
+            colg[0:1, :] = colg[0:1, :] + jnp.sum(du.astype(f32), axis=0, keepdims=True)
+        loop(T2 // E, chunk)
+
+    def unlift(j):
+        parts[j] = mm(du_ref[block_of(chip_of(j), T2), :], w_up[...], NT).astype(bf16)
+
+    fold_y = Scatter(parts, r.low1, mid, r.high1)
+    turn(y_all, y_t, D)
+    gather_dz.wait(1)
+    unlower(0)
+    unlift(0)
+    fold_y.pair(0)
+    gather_dz.pass_on(2)
+    gather_dz.pass_on(4)
+    gather_dz.wait(3)
+    unlower(1)
+    unlift(1)
+    fold_y.pair(1)
+    gather_dz.wait(5)
+    unlower(2)
+    fold_y.onward(1)
+    unlift(2)
+    fold_y.pair(2)
+    gather_dz.pass_on(6)
+    gather_dz.wait(7)
+    unlower(3)
+    fold_y.onward(2)
+    unlift(3)
+    fold_y.pair(3)
+    fold_y.onward(3)
+
+    gd_part, gu_part = r.gd_part, r.gu_part
+
+    def down_grad(i):
+        gd_part[i] = mm(g_t[pl.ds(at(i, UZ), UZ), :], dz_all[...]).astype(bf16)
+    loop(Z, down_grad)
+    fold_dn = Fold(gd_part, r.gd_land, r.gd_pass)
+    fold_dn.start()
+
+    def up_grad(i):
+        gu_part[i] = mm(y_t[pl.ds(at(i, KW), KW), :], du_ref[...]).astype(bf16)
+    loop(Z, up_grad)
+    fold_up = Fold(gu_part, r.gu_land, r.gu_pass)
+    fold_up.start()
+    fold_y.ready()
+
+    dh1, da = r.dh1, r.da
+
+    def first_back(i):
+        start = at(i, R)
+        rows = pl.ds(start, R)
+        incoming = dh2[rows, :] + fold_y.rows(start, R)
+        normal = n1[rows, :]
+        grad = norm_back(incoming, normal, r1[rows, 0:1], row(FIRST_GAIN))
+        dh1[rows, :] = grad
+        low = grad.astype(bf16)
+        da[rows, :] = low
+        add_row(0, low.astype(f32))
+        add_row(1, incoming * normal)
+        add_row(2, incoming)
+    loop(T // R, first_back)
+    drop(fold_y.sent)
+
+    dc_tok, dc = r.dc_tok, r.dc
+    dc_tok[...] = mm(da[...], w_o[...], NT).astype(bf16)
+    dc_base = slots(8)
+    for k in (7, 6, 5, 4, 3, 2, 1):
+        send(dc_tok.at[:, block_of(ps(k), C)], dc.at[block_of(s, T)], dc_base + k, (ps(k), z))
+    dc[block_of(s, T), :] = dc_tok[:, block_of(s, C)]
+    da_cols = r.da_cols
+    da_base = slots(8)
+    for k in (7, 6, 5, 4, 3, 2, 1):
+        send(da.at[:, block_of(ps(k), C)], da_cols.at[block_of(s, T)], da_base + k, (ps(k), z))
+    da_cols[block_of(s, T), :] = da[:, block_of(s, C)]
+    vec_all = r.vec_all
+    vec_base = slots(8)
+    for k in (7, 6, 5, 4, 3, 2, 1):
+        send(vecg, vec_all.at[s], vec_base + k, (ps(k), z))
+    c_all = r.c_all
+    c_all[block_of(s, T), :] = c_tok[...]
+    gather_c = Gather(lambda o: c_all.at[block_of(o, T)])
+    gather_c.start(c_tok)
+    turn(x_all, x_t, D)
+    for k in range(1, 8):
+        arrived(dc.at[block_of(ps(k), T)], dc_base + k)
+
+    delta, dp_buf, ds_buf, dq, dproj = r.delta, r.dp_buf, r.ds_buf, r.dq, r.dproj
+
+    def deltas(i):
+        here = pl.ds(at(i, T), T)
+        turned = jnp.transpose(dc[here, :].astype(f32) * c_f[here, :])
+        delta[0:1, here] = jnp.sum(turned[:HEAD_DIM], axis=0, keepdims=True)
+        delta[1:2, here] = jnp.sum(turned[HEAD_DIM:], axis=0, keepdims=True)
+        dq[here, :] = jnp.zeros((T, C), f32)
+    loop(L // T, deltas)
+
+    def attend_back(i):
+        here = pl.ds(at(i, T), T)
+        keys = stacked(k_ref[here, :])
+        s_buf[...] = mm(keys, q_ref[...], NT)
+        dp_buf[...] = mm(stacked(v_ref[here, :]), dc[...], NT)
+
+        def chunk(n):
+            rows = pl.ds(at(n, R), R)
+            head = n // (T // R)
+            same = segc[pl.ds(pl.multiple_of(i * T + (n % (T // R)) * R, R), R), :] == segr[...]
+            weight = jnp.exp(jnp.where(same, s_buf[rows, :], MASKED) - lse[pl.ds(head, 1), :])
+            p_buf[rows, :] = weight.astype(bf16)
+            ds_buf[rows, :] = (weight * (dp_buf[rows, :] - delta[pl.ds(head, 1), :])).astype(bf16)
+        loop(T2 // R, chunk)
+        dv = unstacked(mm(p_buf[...], dc[...])).astype(bf16)
+        dk = unstacked(mm(ds_buf[...], q_ref[...])).astype(bf16).astype(f32)
+        dproj[here, 2 * C:] = dv
+        dproj[here, C:2 * C] = (dk * r.cos[here, :] - swapped(dk) * r.sin[here, :]).astype(bf16)
+        dq[...] = dq[...] + mm(ds_buf[...], keys, TN)
+
+    go_part = r.go_part
+    loop(3, attend_back)
+    fold_dn.middle()
+    gather_c.pass_on(2)
+    gather_c.pass_on(4)
+    loop(2, lambda i: attend_back(i + 3))
+    fold_up.middle()
+    gather_c.pass_on(6)
+    gd_all, gu_all, go_all, gq_all = r.gd_all, r.gu_all, r.go_all, r.gq_all
+    gather_gd = Gather(lambda o: gd_all.at[block_of(o, UZ)])
+    gather_gu = Gather(lambda o: gu_all.at[o])
+    gather_go = Gather(lambda o: go_all.at[:, block_of(o, C)])
+    gather_gq = Gather(lambda o: gq_all.at[o])
+    gd_all[block_of(s, UZ), :] = fold_dn.finish()
+    gather_gd.start()
+    for k in (1, 3, 5, 7):
+        gather_c.wait(k)
+    for k in range(1, 8):
+        arrived(da_cols.at[block_of(ps(k), T)], da_base + k)
+
+    def out_grad(i):
+        go_part[i] = mm(c_all[:, pl.ds(at(i, KW), KW)], da_cols[...], TN).astype(bf16)
+    loop(Z, out_grad)
+    fold_o = Fold(go_part, r.go_land, r.go_pass)
+    fold_o.start()
+    vec_all[s] = vecg[...]
+    for k in range(1, 8):
+        arrived(vec_all.at[ps(k)], vec_base + k)
+    vec_plane, vec_z = r.vec_plane, r.vec_z
+    total = vec_all[0]
+    for o in range(1, S):
+        total = total + vec_all[o]
+    vec_plane[...] = total
+    vz_base = slots(4)
+    for k in (1, 2, 3):
+        send(vec_plane, vec_z.at[z], vz_base + k, (s, pz(k)))
+    vec_z[z] = total
+    loop(3, lambda i: attend_back(i + 5))
+
+    def dq_rows(i):
+        here = pl.ds(at(i, T), T)
+        whole = (dq[here, :] * scale).astype(bf16).astype(f32)
+        dproj[here, :C] = (whole * r.cos[here, :] - swapped(whole) * r.sin[here, :]).astype(bf16)
+        colg[1:2, :3 * C] = colg[1:2, :3 * C] + jnp.sum(dproj[here, :].astype(f32), axis=0, keepdims=True)
+    loop(L // T, dq_rows)
+
+    gq_part = r.gq_part
+    for k in (1, 3, 2, 0):
+        gq_part[pz(k)] = mm(x_t[block_of(pz(k), KW), :], dproj[...]).astype(bf16)
+        if k == 3:
+            fold_qkv = Fold(gq_part, r.gq_land, r.gq_pass)
+            fold_qkv.start()
+    col_z = r.col_z
+    cz_base = slots(4)
+    for k in (1, 2, 3):
+        send(colg, col_z.at[z], cz_base + k, (s, pz(k)))
+    col_z[z] = colg[...]
+    fold_x = Scatter(parts, r.low2, mid, r.high2)
+
+    def unproject(j):
+        parts[j] = mm(dproj[block_of(chip_of(j), T2), :], w_qkv[...], NT).astype(bf16)
+        fold_x.pair(j)
+    unproject(1)
+    unproject(2)
+    fold_x.onward(1)
+    unproject(3)
+    fold_x.onward(2)
+    unproject(0)
+    fold_x.onward(3)
+    fold_o.middle()
+    fold_qkv.middle()
+    gu_all[s] = fold_up.finish()
+    gather_gu.start()
+    for k in (2, 4, 6):
+        gather_gd.pass_on(k)
+    go_all[:, block_of(s, C)] = fold_o.finish()
+    gather_go.start()
+    for k in (1, 2, 3):
+        arrived(col_z.at[pz(k)], cz_base + k)
+    col_all = r.col_all
+    col_sum = r.col_sum
+    col_sum[...] = col_z[0] + col_z[1] + col_z[2] + col_z[3]
+    ca_base = slots(8)
+    for k in range(1, 8):
+        send(col_sum, col_all.at[s], ca_base + k, (ps(k), z))
+    col_all[s] = col_sum[...]
+    fold_x.ready()
+    dx_ref = r.dx
+
+    def input_back(i):
+        start = at(i, R)
+        rows = pl.ds(start, R)
+        dx_ref[rows, :] = (dh1[rows, :] + fold_x.rows(start, R)).astype(bf16)
+    loop(T // R, input_back)
+    gq_all[s] = fold_qkv.finish()
+    gather_gq.start()
+    for k in (1, 3, 5, 7):
+        gather_gd.wait(k)
+    outs = [local(gd_all, r.gd)]
+    for k in (2, 4, 6):
+        gather_gu.pass_on(k)
+    for k in (2, 4, 6):
+        gather_go.pass_on(k)
+    for k in (1, 3, 5, 7):
+        gather_gu.wait(k)
+    for o in range(S):
+        for p in range(Z):
+            lane = (p * S + o) * C
+            outs.append(local(gu_all.at[o, :, pl.ds(p * C, C)], r.gu.at[:, pl.ds(lane, C)]))
+    for k in (1, 3, 5, 7):
+        gather_go.wait(k)
+    outs.append(local(go_all, r.go))
+
+    for k in (1, 2, 3):
+        arrived(vec_z.at[pz(k)], vz_base + k)
+    for k in range(1, 8):
+        arrived(col_all.at[ps(k)], ca_base + k)
+    vec_plane2 = r.vec_sum
+    vec_plane2[...] = vec_z[0] + vec_z[1] + vec_z[2] + vec_z[3]
+    gsm = r.gsm
+    gsm[...] = jnp.zeros(gsm.shape, f32)
+    for start, i in wide:
+        for half in range(KW // C):
+            at_row = start + half
+            gsm[at_row:at_row + 1, :] = vec_plane2[i:i + 1, block_of(z * (KW // C) + half, C)]
+    for o in range(S):
+        at_row = first_row.up_bias + o
+        gsm[at_row:at_row + 1, :] = col_all[o, 0:1, block_of(z, C)]
+    for i in range(per):
+        number = z * per + i
+        at_row = first_row.projection_bias + i
+        gsm[at_row:at_row + 1, :] = col_all[number % S, 1:2, block_of(number // S, C)]
+
+    for k in (2, 4, 6):
+        gather_gq.pass_on(k)
+    for k in (1, 3, 5, 7):
+        gather_gq.wait(k)
+    for o in range(S):
+        for t in range(3):
+            lane = (t * S + o) * C
+            outs.append(local(gq_all.at[o, :, pl.ds(t * C, C)], r.gq.at[:, pl.ds(lane, C)]))
+    for copy in outs:
+        copy.wait()
+    for copy in pending:
+        copy.wait_send()
+    loop(7, lambda i: c_copy(7 - i).wait_send())
+
+
+def fused_shards(*args):
+    (hidden_in, cotangent, segment_ids, projection, projection_bias, output_weight, output_bias, first_gain,
+     first_shift, up_weight, up_bias, down_weight, down_bias, second_gain, second_shift) = args
+    T, D = hidden_in.shape[1:]
+    L = segment_ids.shape[1]
+    KW = projection.shape[0]
+    F = up_weight.shape[1] // 8
+    C, Z = 128, 4
+    UZ = F // Z
+    small = dict(projection_bias=projection_bias, output_bias=output_bias, first_gain=first_gain,
+                 first_shift=first_shift, up_bias=up_bias, down_bias=down_bias, second_gain=second_gain,
+                 second_shift=second_shift)
+    starts, at_row = {}, 0
+    for name, value in small.items():
+        starts[name] = at_row
+        at_row += value.shape[0] // C
+    rows = -(-at_row // 8) * 8
+    packed = jnp.concatenate(list(small.values())).astype(bf16).astype(f32).reshape(at_row, C)
+    packed = jnp.pad(packed, ((0, rows - at_row), (0, 0)))
+
+    half = HEAD_DIM // 2
+    inverse = np.float32(10000.0) ** (np.float32(-2.0) * np.arange(half, dtype=np.float32) / np.float32(HEAD_DIM))
+    angles = np.arange(L, dtype=np.float32)[:, None] * inverse.astype(np.float32)[None, :]
+    cosine = np.tile(np.cos(angles), (1, C // half))
+    sine = np.tile(np.concatenate([-np.sin(angles), np.sin(angles)], axis=1), (1, C // HEAD_DIM))
+
+    inputs = dict(x=(hidden_in[0], 0), ct=(cotangent[0], 0), segr=(segment_ids, 0),
+              segc=(segment_ids.reshape(L, 1), 0), cos=(jnp.asarray(cosine), 0), sin=(jnp.asarray(sine), 0),
+              small=(packed, 0), proj=(projection, 1), wo=(output_weight, 1), up=(up_weight, 1),
+              dn=(down_weight, 1))
+    outputs = dict(out=((T, D), bf16, 0), dx=((T, D), bf16, 0), gsm=((rows, C), f32, 0),
+               gq=(projection.shape, bf16, 1), go=(output_weight.shape, bf16, 1),
+               gu=(up_weight.shape, bf16, 1), gd=(down_weight.shape, bf16, 1))
+    PART = (4, T, D)
+    scratch = dict(
+        x_all=((L, D), bf16), x_t=((D, L), bf16), w_qkv=((D, 3 * C), bf16), st_proj=((KW, 3 * C), f32),
+        w_o=((D, D), bf16), st_wo=((KW, C), f32), w_up=((D, F), bf16), st_up=((KW, F), f32),
+        w_dn=((F, D), bf16), st_dn=((UZ, D), f32), small_all=((Z, rows, C), f32), vec=((8, D), f32),
+        vecg=((8, D), f32), q=((L, C), bf16), k=((L, C), bf16), v=((L, C), bf16),
+        s_buf=((2 * T, L), f32), dp_buf=((2 * T, L), f32), p_buf=((2 * T, L), bf16),
+        ds_buf=((2 * T, L), bf16), col_a=((2 * T, C), f32), col_b=((2 * T, C), f32), lse=((8, L), f32),
+        delta=((8, L), f32), c_f=((L, C), f32), c_heads=((L, C), bf16), c_tok=((T, D), bf16),
+        a_buf=((T, D), f32), n1=((T, D), f32), y1=((T, D), f32), r1=((T, C), f32),
+        y_all=((L, D), bf16), y_t=((D, L), bf16), u_buf=((2 * T, F), f32), g=((L, F), bf16),
+        g_t=((F, L), bf16), d=((L, F), f32), du=((L, F), bf16), dz_all=((L, D), bf16),
+        parts=((4, 2 * T, D), bf16), mid=((4, T, D), bf16), dh2=((T, D), f32), dh1=((T, D), f32),
+        colg=((8, F), f32), gd_part=((Z, UZ, D), bf16), gd_land=((3, UZ, D), bf16), gd_pass=((UZ, D), bf16),
+        gu_part=((Z, KW, F), bf16), gu_land=((3, KW, F), bf16), gu_pass=((KW, F), bf16),
+        go_part=((Z, KW, C), bf16), go_land=((3, KW, C), bf16), go_pass=((KW, C), bf16),
+        gq_part=((Z, KW, 3 * C), bf16), gq_land=((3, KW, 3 * C), bf16), gq_pass=((KW, 3 * C), bf16),
+        gd_all=((8 * UZ, D), bf16), gu_all=((8, KW, F), bf16), go_all=((KW, D), bf16),
+        gq_all=((8, KW, 3 * C), bf16), da=((T, D), bf16), dc_tok=((T, D), bf16), dc=((L, C), bf16),
+        da_cols=((L, C), bf16), c_all=((L, D), bf16), dq=((L, C), f32), dproj=((L, 3 * C), bf16),
+        vec_all=((8, 8, D), f32), vec_plane=((8, D), f32), vec_z=((Z, 8, D), f32), vec_sum=((8, D), f32),
+        col_z=((Z, 8, F), f32), col_sum=((8, F), f32), col_all=((8, 8, F), f32),
+        low0=(PART, bf16), high0=(PART, bf16), low1=(PART, bf16), high1=(PART, bf16), low2=(PART, bf16),
+        high2=(PART, bf16), ssem=(SLOTS,), rsem=(SLOTS,), lsem=(LOCAL,))
+    names = [*inputs, *outputs, *scratch]
+    sizes = SimpleNamespace(names=names, T=T, D=D, L=L, F=F, first_row=SimpleNamespace(**starts))
+
+    def spec(anywhere):
+        return pl.BlockSpec(memory_space=pl.ANY if anywhere else pltpu.VMEM)
+    results = pl.pallas_call(
+        partial(fused_layer, sizes),
+        out_shape=[jax.ShapeDtypeStruct(shape, dtype) for shape, dtype, _ in outputs.values()],
+        in_specs=[spec(w) for _, w in inputs.values()],
+        out_specs=[spec(w) for *_, w in outputs.values()],
+        scratch_shapes=[pltpu.VMEM(*what) if len(what) == 2 else pltpu.SemaphoreType.DMA(what)
+                        for what in scratch.values()],
+        compiler_params=pltpu.CompilerParams(collective_id=0, has_side_effects=True, vmem_limit_bytes=67043328),
+        name="fused_layer",
+    )(*[value for value, _ in inputs.values()])
+    out, dx, gsm, gq, go, gu, gd = results
+    flat = gsm.reshape(-1)
+    small_grads = [lax.slice(flat, (starts[name] * C,), (starts[name] * C + value.shape[0],))
+                   for name, value in small.items()]
+    pb, ob, g1, s1, ub, db, g2, s2 = small_grads
+    return (out[None], dx[None], gq.astype(f32), pb, go.astype(f32), ob, g1, s1, gu.astype(f32), ub, gd.astype(f32),
+            db, g2, s2)
+
+
+SLOTS = 192
+LOCAL = 80
+
+
+def fits(mesh):
+    return mesh.shape["seq"] == 8 and mesh.shape["fsdp"] == 4
+
+
 def solution(mesh):
     return jax.shard_map(
-        shards,
+        fused_shards if fits(mesh) else shards,
         mesh=mesh,
         in_specs=(
             P("fsdp", "seq", None),

time: 1100 us -> 257 us (0.23)
  waiting for transfers between devices: 781 us -> 0 us
  Pallas kernels: 0 us -> 231 us
  blocking collectives: 136 us -> 0 us
  matrix products: 86.9 us -> 0 us
  local copies, waits for them, and re-layouts: 28.6 us -> 8.3 us
  other arithmetic: 34.1 us -> 15.9 us
  between operations: 17.1 us -> 0.67 us
  starting transfers between devices: 11.5 us -> 0 us
    reduce_scatter x4 -> x0, waiting for transfers between devices: 388 us -> none  [the longest x1 148 us: shards(): lax.psum_scatter(down_weight_grad.astype(jnp.bfloat16), 'fsdp', scatter_d...]
    all_gather x4 -> x0, waiting for transfers between devices: 313 us -> none  [the longest x1 141 us: shards(): lax.all_gather(down_weight.astype(bf16), 'fsdp', axis=0, tiled=True)]
    pallas_call x0 -> x1, Pallas kernels: none -> 231 us  [fused_shards(): pl.pallas_call(partial(fused_layer, sizes), out_shape=[jax.ShapeDtypeStru...]
    all_gather x8 -> x0, blocking collectives: 88.5 us -> none  [the longest x1 17.3 us: shards(): lax.all_gather(projection_bias.astype(bf16), 'fsdp', axis=0, tiled=True)]
    dot_general x26 -> x0, matrix products: 86.9 us -> none  [the longest x1 9.08 us: shards(): jnp.dot(normed_low, feed_full[0], preferred_element_type=f32)]
    psum x1 -> x0, waiting for transfers between devices: 63.8 us -> none  [shards(): lax.psum(every_shard[0].astype(jnp.bfloat16), 'seq').astype(jnp.float32)]
    unnamed x1 -> x0, blocking collectives: 18.4 us -> none
    all_to_all x3 -> x0, waiting for transfers between devices: 16 us -> none  [the longest x1 11.4 us: shards(): lax.all_to_all(stacked, 'seq', split_axis=2, concat_axis=1, tiled=True)]
  transfers between devices with their start and end apart: 12 -> 0, of which waited for: 9 -> 0; matrix products, arithmetic and copies ran while one was open for 10% -> 0% of each run, Pallas kernels for 0% -> 0%
where the time goes in v1:
time: 257 us; the launch traced here: 256 us
  Pallas kernels  231 us (90%)
  other arithmetic  15.9 us (6%)
  local copies, waits for them, and re-layouts  8.3 us (3%)
    pallas_call x1, Pallas kernels, fused_shards(): pl.pallas_call(partial(fused_layer, sizes), out_shape=[jax.ShapeDtypeStru...  231 us

profile of v1, /device:TPU:0, one launch (start us, length us, event | category | flops | bytes accessed | tf_op | source)
XLA Modules:
  0.0 256.2 jit_solution(17132449969709327739)
XLA Ops:
  0.6 1.7 copy.31.refs_3_
  2.4 0.7 convert.27
  3.0 0.2 dynamic-update-slice
  3.2 0.7 convert.28
  3.9 0.2 dynamic-update-slice.1
  4.1 0.7 convert.29
  4.8 0.2 dynamic-update-slice.2
  4.9 0.7 convert.30
  5.6 0.2 dynamic-update-slice.3
  5.8 0.7 convert.31
  6.5 0.2 dynamic-update-slice.4
  6.7 0.7 convert.32
  7.4 0.2 dynamic-update-slice.5
  7.5 0.7 convert.33
  8.2 0.2 dynamic-update-slice.6
  8.4 0.7 constant_dynamic-update-slice_fusion
  9.1 0.6 pad_convert_fusion.refs_6_
  9.7 231.3 %fused_layer.1 = (bf16[128,1024]{1,0:T(8,128)(2,1)}, bf16[128,1024]{1,0:T(8,128)(2,1)}, f32[32,128]{1,0:T(8,128)}, bf16[256,3072]{1,0:T(8,128)(2,1)}, bf16[256,1...) custom-call(bf16[128,1024]{1,0:T(8,128)(2,1)} %bitcast.22, bf16[128,1024]{1,0:T(8,128)(2,1)} %bitcast.23, ...), custom_call_target="tpu_custom_call" | custom-call | tf_op jit(solution)/shard_map/fused_layer/pallas_call | solution.py:1086
  241.0 1.4 slice_bitcast_fusion.2
  242.4 1.3 slice_bitcast_fusion
  243.7 1.3 slice_bitcast_fusion.1
  244.9 0.0 copy-start
  244.9 4.2 %convert_element_type.25 = f32[256,4096]{1,0:T(8,128)} convert(bf16[256,4096]{1,0:T(8,128)(2,1)} %get-tuple-element.26) | non-fusion elementwise | flops 1048576 | bytes 6291456 | tf_op jit(solution)/shard_map/convert_element_type | solution.py:1101
  249.2 0.0 copy-done
  249.2 0.0 copy-start.1
  249.2 2.5 convert_element_type.26
  251.7 0.0 copy-start.2
  251.7 0.0 copy-done.1
  251.7 0.0 copy-start.4
  251.7 0.0 copy-start.3
  251.7 2.0 convert_element_type.23
  253.7 0.0 copy-done.2
  253.7 1.1 convert_element_type.24
  254.8 0.0 copy-done.4
  254.8 0.7 copy.42
  255.5 0.0 copy-done.3
  255.5 0.7 copy.43
  (1 shorter events, 0.0 us)
Async XLA Ops:
  244.9 4.3 %copy-start = (bf16[1024,1024]{1,0:T(8,128)(2,1)S(1)}, bf16[1024,1024]{1,0:T(8,128)(2,1)}, u32[]{:S(2)}) copy-start(bf16[1024,1024]{1,0:T(8,128)(2,1)} %get-tuple-element.27) | copy-start | bytes 6291460
  249.2 2.5 copy-start.1
  251.7 2.0 copy-start.2
  251.7 3.1 %copy-start.4 = (bf16[128,1024]{1,0:T(8,128)(2,1)S(1)}, bf16[128,1024]{1,0:T(8,128)(2,1)}, u32[]{:S(2)}) copy-start(bf16[128,1024]{1,0:T(8,128)(2,1)} %get-tuple-element.21) | copy-start | bytes 786436
  251.7 3.8 %copy-start.3 = (bf16[128,1024]{1,0:T(8,128)(2,1)S(1)}, bf16[128,1024]{1,0:T(8,128)(2,1)}, u32[]{:S(2)}) copy-start(bf16[128,1024]{1,0:T(8,128)(2,1)} %get-tuple-element.22) | copy-start | bytes 786436

commit v2 on v1

--- a/solution.py
+++ b/solution.py
@@ -392,28 +392,46 @@
 
     class Gather:
         def __init__(self, place):
-            self.place, self.base = place, slots(8)
+            self.place, self.base = place, slots(9)
+
+        def half(self, k, part):
+            there = self.place(ps(k))
+            n = there.shape[0] // 2
+            return there.at[pl.ds(part * n, n)]
 
         def start(self, src=None):
             mine = self.place(s)
-            for k in (1, 2, 4, 6):
+            for k in (2, 4, 1):
                 send(mine if src is None else src, mine, self.base + k, (ps(k), z))
 
         def pass_on(self, k):
             there = self.place(ps(k))
-            arrived(there, self.base + k)
+            if k == 2:
+                arrived(there, self.base + 2)
+                send(self.half(2, 0), self.half(2, 0), self.base + 6, (ps(4), z))
+            elif k == 4:
+                arrived(there, self.base + 4)
+                send(self.half(4, 1), self.half(4, 1), self.base + 8, (ps(2), z))
+            else:
+                arrived(self.half(6, 0), self.base + 6)
+                arrived(self.half(6, 1), self.base + 8)
             send(there, there, self.base + k + 1, (ps(1), z))
 
-        def wait(self, k):
-            arrived(self.place(ps(k)), self.base + k)
+        def pass_all(self):
+            for k in (2, 4, 6):
+                self.pass_on(k)
+
+        def wait(self, *which):
+            for k in which or (1, 3, 5, 7):
+                arrived(self.place(ps(k)), self.base + k)
 
     class Spread:
         def __init__(self, place):
             self.place, self.base = place, slots(4)
 
-        def start(self):
+        def start(self, *which):
             mine = self.place(z)
-            for k in (2, 1):
+            for k in which or (2, 1):
                 send(mine, mine, self.base + k, (s, pz(k)))
 
         def pass_on(self):
@@ -480,6 +498,11 @@
     def at(i, n):
         return pl.multiple_of(i * n, n)
 
+    def turn(src, dst):
+        def one(i):
+            dst[:, pl.ds(at(i, T), T)] = jnp.transpose(src[pl.ds(at(i, T), T), :])
+        loop(L // T, one)
+
     vec, vecg = r.vec, r.vecg
 
     OUTPUT_BIAS, FIRST_GAIN, FIRST_SHIFT, DOWN_BIAS, SECOND_GAIN, SECOND_SHIFT, PROJECTION_BIAS, UP_BIAS = range(8)
@@ -492,9 +515,9 @@
 
     lanes = lax.broadcasted_iota(jnp.int32, (T, C), 1)
     low_head = lanes < HEAD_DIM
-    low_half = lanes % HEAD_DIM < HEAD_DIM // 2
 
     def swapped(w):
+        low_half = lax.broadcasted_iota(jnp.int32, w.shape, 1) % HEAD_DIM < HEAD_DIM // 2
         return jnp.where(low_half, pltpu.roll(w, C - HEAD_DIM // 2, 1), pltpu.roll(w, HEAD_DIM // 2, 1))
 
     def stacked(w):
@@ -504,18 +527,17 @@
     def unstacked(w):
         return jnp.where(low_head, w[:T], w[T:])
 
+    barrier = pltpu.get_barrier_semaphore()
+    for k in range(1, S):
+        pl.semaphore_signal(barrier, inc=1, device_id=(ps(k), z), device_id_type=MESH)
+    for k in range(1, Z):
+        pl.semaphore_signal(barrier, inc=1, device_id=(s, pz(k)), device_id_type=MESH)
     proj_loads = [local(r.proj.at[:, block_of(i * (D // C) + s, C)], r.st_proj.at[:, pl.ds(i * C, C)])
                   for i in range(3)]
     wo_load = local(r.wo.at[:, block_of(s, C)], r.st_wo)
     up_loads = [local(r.up.at[:, block_of(i * (D // C) + s, C)], r.st_up.at[:, pl.ds(i * C, C)])
                 for i in range(Z)]
     dn_load = local(r.dn.at[block_of(s, UZ), :], r.st_dn)
-
-    barrier = pltpu.get_barrier_semaphore()
-    for k in range(1, S):
-        pl.semaphore_signal(barrier, inc=1, device_id=(ps(k), z), device_id_type=MESH)
-    for k in range(1, Z):
-        pl.semaphore_signal(barrier, inc=1, device_id=(s, pz(k)), device_id_type=MESH)
     pl.semaphore_wait(barrier, S + Z - 2)
 
     x_ref, x_all = r.x, r.x_all
@@ -533,30 +555,44 @@
     w_qkv[block_of(z, KW), :] = r.st_proj[...].astype(bf16)
     spread_qkv.start()
 
-    small_all = r.small_all
+    small, small_all, seg_c, seg_r = r.small, r.small_all, r.seg_c, r.seg_r
+    raw = ((r.b_projection, first_row.projection_bias), (r.b_output, first_row.output_bias),
+           (r.gain1, first_row.first_gain), (r.shift1, first_row.first_shift), (r.b_up, first_row.up_bias),
+           (r.b_down, first_row.down_bias), (r.gain2, first_row.second_gain), (r.shift2, first_row.second_shift))
+    for ref, start in raw:
+        for i in range(ref.shape[1] // C):
+            small[start + i:start + i + 1, :] = ref[0:1, i * C:(i + 1) * C].astype(bf16).astype(f32)
     small_base = slots(4)
-    small_all[z] = r.small[...]
-    for k in (1, 2, 3):
-        send(r.small, small_all.at[z], small_base + k, (s, pz(k)))
-
     x_all[block_of(s, T), :] = x_ref[...]
     wo_load.wait()
     w_o[block_of(z, KW), block_of(s, C)] = r.st_wo[...].astype(bf16)
-    spread_o.start()
     for copy in up_loads:
         copy.wait()
     w_up[block_of(z, KW), :] = r.st_up[...].astype(bf16)
     dn_load.wait()
     w_dn[block_of(z, UZ), :] = r.st_dn[...].astype(bf16)
-    for i in range(8):
-        vecg[i:i + 1, :] = jnp.zeros((1, D), f32)
+    vecg[...] = jnp.zeros((8, D), f32)
+    seg_r[...] = jnp.broadcast_to(r.seg[...].astype(f32), (8, L))
+
+    def seg_turn(i):
+        here = pl.ds(at(i, T), T)
+        seg_c[here, :] = jnp.transpose(jnp.broadcast_to(seg_r[0:1, here], (T, T)))
+    loop(L // T, seg_turn)
 
     spread_qkv.pass_on()
+    small_all[z] = small[...]
+    for k in (1, 2, 3):
+        send(small, small_all.at[z], small_base + k, (s, pz(k)))
+    spread_o.start()
     gather_x.pass_on(2)
     gather_x.pass_on(4)
+    spread_up.start(2)
+    gather_x.pass_on(6)
+    gather_x.wait()
+    x_t = r.x_t
+    turn(x_all, x_t)
     spread_o.pass_on()
-    spread_up.start()
-    gather_x.pass_on(6)
+    spread_up.start(1)
     for k in (1, 2, 3):
         arrived(small_all.at[pz(k)], small_base + k)
     for p in range(Z):
@@ -570,51 +606,44 @@
     for t in range(3):
         number = t * (D // C) + s
         vec[6:7, t * C:(t + 1) * C] = small_all[number // per, pl.ds(first_row.projection_bias + number % per, 1), :]
-    for k in (1, 3, 5, 7):
-        gather_x.wait(k)
-
-    x_t = r.x_t
+
     spread_qkv.wait()
-    spread_o.wait()
-    gather_o.start()
     q_ref, k_ref, v_ref = r.q, r.k, r.v
     scale = HEAD_DIM ** -0.5
 
     def project(i):
-        here = pl.ds(at(i, T), T)
+        here = pl.ds(at(i, T2), T2)
         out = mm(x_all[here, :], w_qkv[...]) + row(PROJECTION_BIAS, 3 * C)
         cosine, sine = r.cos[here, :], r.sin[here, :]
         q0, k0 = out[:, :C], out[:, C:2 * C]
         q_ref[here, :] = ((q0 * cosine + swapped(q0) * sine).astype(bf16).astype(f32) * scale).astype(bf16)
         k_ref[here, :] = (k0 * cosine + swapped(k0) * sine).astype(bf16)
         v_ref[here, :] = out[:, 2 * C:].astype(bf16)
-    loop(L // T, project)
-
-    s_buf, p_buf, col_a, col_b = r.s_buf, r.p_buf, r.col_a, r.col_b
-    segr, segc = r.segr, r.segc
+    loop(L // T2, project)
+    spread_o.wait()
+    gather_o.start()
+
     lse, c_f, c_heads, c_tok = r.lse, r.c_f, r.c_heads, r.c_tok
     R = 16
 
+    def same_document(here):
+        return jnp.tile(seg_c[here, :], (1, L // C)) == seg_r[0:1, :]
+
+    def both(w):
+        return jnp.concatenate([w, w], axis=0)
+
     def attend(o):
         here = block_of(o, T)
-        s_buf[...] = mm(stacked(q_ref[here, :]), k_ref[...], NT)
-
-        def chunk(i):
-            rows = pl.ds(at(i, R), R)
-            same = segc[pl.ds(pl.multiple_of(o * T + (i % (T // R)) * R, R), R), :] == segr[...]
-            score = jnp.where(same, s_buf[rows, :], MASKED)
-            top = jnp.max(score, axis=-1, keepdims=True)
-            power = jnp.exp(score - top)
-            total = jnp.sum(power, axis=-1, keepdims=True)
-            p_buf[rows, :] = power.astype(bf16)
-            col_a[rows, :] = jnp.broadcast_to(1.0 / total, (R, C))
-            col_b[rows, :] = jnp.broadcast_to(top + jnp.log(total), (R, C))
-        loop(T2 // R, chunk)
-        context = unstacked(mm(p_buf[...], v_ref[...]) * col_a[...])
+        score = jnp.where(both(same_document(here)), mm(stacked(q_ref[here, :]), k_ref[...], NT), MASKED)
+        top = jnp.max(score, axis=-1, keepdims=True)
+        power = jnp.exp(score - top)
+        total = jnp.sum(power, axis=-1, keepdims=True)
+        context = unstacked(mm(power.astype(bf16), v_ref[...]) * (1.0 / total))
         c_f[here, :] = context
         c_heads[here, :] = context.astype(bf16)
+        logs = jnp.broadcast_to(top + jnp.log(total), (T2, C))
         for h in range(2):
-            lse[h:h + 1, here] = jnp.transpose(col_b[h * T:(h + 1) * T, :])[0:1, :]
+            lse[h:h + 1, here] = jnp.transpose(logs[h * T:(h + 1) * T, :])[0:1, :]
 
     c_base = slots(8)
 
@@ -624,20 +653,18 @@
     def attend_and_send(i):
         k = 7 - i
         attend(ps(k))
-        c_copy(k).start()
-
-    loop(3, attend_and_send)
+
+        @pl.when(k > 0)
+        def _():
+            c_copy(k).start()
+    loop(8, attend_and_send)
     spread_up.pass_on()
     spread_dn.start()
-    loop(2, lambda i: attend_and_send(i + 3))
+    c_tok[:, block_of(s, C)] = c_heads[block_of(s, T), :]
     gather_o.pass_on(2)
     gather_o.pass_on(4)
-    loop(2, lambda i: attend_and_send(i + 5))
-    attend(s)
     gather_o.pass_on(6)
-    c_tok[:, block_of(s, C)] = c_heads[block_of(s, T), :]
-    for k in (1, 3, 5, 7):
-        gather_o.wait(k)
+    gather_o.wait()
     for k in range(1, 8):
         arrived(c_tok.at[:, block_of(ps(k), C)], c_base + k)
 
@@ -658,13 +685,16 @@
         r1[rows, :] = jnp.broadcast_to(root, (R, C))
         y1[rows, :] = out
         y_all[pl.ds(pl.multiple_of(s * T + i * R, R), R), :] = out.astype(bf16)
-    loop(T // R, first_norm)
+    loop(T // R, first_norm, 4)
     gather_y = Gather(lambda o: y_all.at[block_of(o, T)])
     gather_y.start()
+    c_all = r.c_all
+    gather_c = Gather(lambda o: c_all.at[block_of(o, T)])
+    gather_c.start(c_tok)
+    c_all[block_of(s, T), :] = c_tok[...]
 
     u_buf, g_ref, d_ref, du_ref, dz_all = r.u_buf, r.g, r.d, r.du, r.dz_all
     parts, mid = r.parts, r.mid
-    spread_dn.pass_on()
     spread_up.wait()
     E = 32
 
@@ -685,36 +715,34 @@
         parts[j] = mm(g_ref[block_of(chip_of(j), T2), :], w_dn[...]).astype(bf16)
 
     fold_z = Scatter(parts, r.low0, mid, r.high0)
+    y_t, g_t = r.y_t, r.g_t
     gather_y.wait(1)
     lift(0)
-    spread_dn.wait()
-    lower(0)
-    fold_z.pair(0)
     gather_y.pass_on(2)
     gather_y.pass_on(4)
     gather_y.wait(3)
     lift(1)
-    lower(1)
-    fold_z.pair(1)
     gather_y.wait(5)
     lift(2)
-    fold_z.onward(1)
-    lower(2)
-    fold_z.pair(2)
+    spread_dn.pass_on()
     gather_y.pass_on(6)
     gather_y.wait(7)
     lift(3)
+    gather_c.pass_on(2)
+    gather_c.pass_on(4)
+    turn(y_all, y_t)
+    turn(g_ref, g_t)
+    spread_dn.wait()
+    for j in (3, 1, 2, 0):
+        lower(j)
+        fold_z.pair(j)
+        if j == 1:
+            fold_z.onward(3)
+        if j == 2:
+            fold_z.onward(1)
     fold_z.onward(2)
-    lower(3)
-    fold_z.pair(3)
-    fold_z.onward(3)
-    y_t, g_t = r.y_t, r.g_t
-
-    def turn(src, dst, wide):
-        def one(i):
-            dst[:, pl.ds(at(i, T), T)] = jnp.transpose(src[pl.ds(at(i, T), T), :])
-        loop(L // T, one)
-    turn(g_ref, g_t, F)
+    gather_c.pass_on(6)
+    gather_c.wait()
     fold_z.ready()
 
     dh2, out_ref, ct_ref = r.dh2, r.out, r.ct
@@ -740,7 +768,7 @@
         add_row(3, dz.astype(f32))
         add_row(4, e * normal)
         add_row(5, e)
-    loop(T // R, second_norm)
+    loop(T // R, second_norm, 2)
     gather_dz = Gather(lambda o: dz_all.at[block_of(o, T)])
     gather_dz.start()
     drop(fold_z.sent)
@@ -764,7 +792,16 @@
         parts[j] = mm(du_ref[block_of(chip_of(j), T2), :], w_up[...], NT).astype(bf16)
 
     fold_y = Scatter(parts, r.low1, mid, r.high1)
-    turn(y_all, y_t, D)
+    gd_part, gu_part = r.gd_part, r.gu_part
+    fold_dn = Fold(gd_part, r.gd_land, r.gd_pass)
+    fold_up = Fold(gu_part, r.gu_land, r.gu_pass)
+
+    def down_grad(k):
+        gd_part[pz(k)] = mm(g_t[block_of(pz(k), UZ), :], dz_all[...]).astype(bf16)
+
+    def up_grad(k):
+        gu_part[pz(k)] = mm(y_t[block_of(pz(k), KW), :], du_ref[...]).astype(bf16)
+
     gather_dz.wait(1)
     unlower(0)
     unlift(0)
@@ -781,26 +818,23 @@
     unlift(2)
     fold_y.pair(2)
     gather_dz.pass_on(6)
+    fold_y.onward(2)
     gather_dz.wait(7)
     unlower(3)
-    fold_y.onward(2)
     unlift(3)
     fold_y.pair(3)
+    down_grad(1)
+    down_grad(3)
+    fold_dn.start()
     fold_y.onward(3)
 
-    gd_part, gu_part = r.gd_part, r.gu_part
-
-    def down_grad(i):
-        gd_part[i] = mm(g_t[pl.ds(at(i, UZ), UZ), :], dz_all[...]).astype(bf16)
-    loop(Z, down_grad)
-    fold_dn = Fold(gd_part, r.gd_land, r.gd_pass)
-    fold_dn.start()
-
-    def up_grad(i):
-        gu_part[i] = mm(y_t[pl.ds(at(i, KW), KW), :], du_ref[...]).astype(bf16)
-    loop(Z, up_grad)
-    fold_up = Fold(gu_part, r.gu_land, r.gu_pass)
+    up_grad(1)
+    up_grad(3)
     fold_up.start()
+    down_grad(2)
+    down_grad(0)
+    up_grad(2)
+    up_grad(0)
     fold_y.ready()
 
     dh1, da = r.dh1, r.da
@@ -817,7 +851,7 @@
         add_row(0, low.astype(f32))
         add_row(1, incoming * normal)
         add_row(2, incoming)
-    loop(T // R, first_back)
+    loop(T // R, first_back, 2)
     drop(fold_y.sent)
 
     dc_tok, dc = r.dc_tok, r.dc
@@ -835,15 +869,11 @@
     vec_base = slots(8)
     for k in (7, 6, 5, 4, 3, 2, 1):
         send(vecg, vec_all.at[s], vec_base + k, (ps(k), z))
-    c_all = r.c_all
-    c_all[block_of(s, T), :] = c_tok[...]
-    gather_c = Gather(lambda o: c_all.at[block_of(o, T)])
-    gather_c.start(c_tok)
-    turn(x_all, x_t, D)
+    fold_dn.middle()
     for k in range(1, 8):
         arrived(dc.at[block_of(ps(k), T)], dc_base + k)
 
-    delta, dp_buf, ds_buf, dq, dproj = r.delta, r.dp_buf, r.ds_buf, r.dq, r.dproj
+    delta, dq, dproj = r.delta, r.dq, r.dproj
 
     def deltas(i):
         here = pl.ds(at(i, T), T)
@@ -855,49 +885,78 @@
 
     def attend_back(i):
         here = pl.ds(at(i, T), T)
-        keys = stacked(k_ref[here, :])
-        s_buf[...] = mm(keys, q_ref[...], NT)
-        dp_buf[...] = mm(stacked(v_ref[here, :]), dc[...], NT)
-
-        def chunk(n):
-            rows = pl.ds(at(n, R), R)
-            head = n // (T // R)
-            same = segc[pl.ds(pl.multiple_of(i * T + (n % (T // R)) * R, R), R), :] == segr[...]
-            weight = jnp.exp(jnp.where(same, s_buf[rows, :], MASKED) - lse[pl.ds(head, 1), :])
-            p_buf[rows, :] = weight.astype(bf16)
-            ds_buf[rows, :] = (weight * (dp_buf[rows, :] - delta[pl.ds(head, 1), :])).astype(bf16)
-        loop(T2 // R, chunk)
-        dv = unstacked(mm(p_buf[...], dc[...])).astype(bf16)
-        dk = unstacked(mm(ds_buf[...], q_ref[...])).astype(bf16).astype(f32)
+        same = same_document(here)
+        k_here, v_here = k_ref[here, :], v_ref[here, :]
+        keys, values, slopes = [], [], []
+        for h in range(2):
+            own = low_head if h == 0 else jnp.logical_not(low_head)
+            nothing = jnp.zeros_like(k_here)
+            key = jnp.where(own, k_here, nothing)
+            weight = jnp.exp(jnp.where(same, mm(key, q_ref[...], NT), MASKED) - lse[h:h + 1, :])
+            slope = mm(jnp.where(own, v_here, nothing), dc[...], NT) - delta[h:h + 1, :]
+            slopes.append((weight * slope).astype(bf16))
+            values.append(mm(weight.astype(bf16), dc[...]))
+            keys.append(key)
+        dv = jnp.where(low_head, values[0], values[1]).astype(bf16)
+        dk = jnp.where(low_head, mm(slopes[0], q_ref[...]), mm(slopes[1], q_ref[...])).astype(bf16).astype(f32)
         dproj[here, 2 * C:] = dv
         dproj[here, C:2 * C] = (dk * r.cos[here, :] - swapped(dk) * r.sin[here, :]).astype(bf16)
-        dq[...] = dq[...] + mm(ds_buf[...], keys, TN)
-
-    go_part = r.go_part
-    loop(3, attend_back)
-    fold_dn.middle()
-    gather_c.pass_on(2)
-    gather_c.pass_on(4)
-    loop(2, lambda i: attend_back(i + 3))
-    fold_up.middle()
-    gather_c.pass_on(6)
+        dq[...] = dq[...] + mm(jnp.concatenate(slopes, axis=0), jnp.concatenate(keys, axis=0), TN)
+
     gd_all, gu_all, go_all, gq_all = r.gd_all, r.gu_all, r.go_all, r.gq_all
     gather_gd = Gather(lambda o: gd_all.at[block_of(o, UZ)])
     gather_gu = Gather(lambda o: gu_all.at[o])
     gather_go = Gather(lambda o: go_all.at[:, block_of(o, C)])
     gather_gq = Gather(lambda o: gq_all.at[o])
-    gd_all[block_of(s, UZ), :] = fold_dn.finish()
-    gather_gd.start()
-    for k in (1, 3, 5, 7):
-        gather_c.wait(k)
+    loop(L // T, attend_back)
+    fold_up.middle()
+
+    def dq_rows(i):
+        here = pl.ds(at(i, T), T)
+        whole = (dq[here, :] * scale).astype(bf16).astype(f32)
+        dproj[here, :C] = (whole * r.cos[here, :] - swapped(whole) * r.sin[here, :]).astype(bf16)
+        colg[1:2, :3 * C] = colg[1:2, :3 * C] + jnp.sum(dproj[here, :].astype(f32), axis=0, keepdims=True)
+    loop(L // T, dq_rows)
+
+    gq_part = r.gq_part
+    fold_qkv = Fold(gq_part, r.gq_land, r.gq_pass)
+
+    def projection_grad(k):
+        gq_part[pz(k)] = mm(x_t[block_of(pz(k), KW), :], dproj[...]).astype(bf16)
+    projection_grad(1)
+    projection_grad(3)
+    fold_qkv.start()
+    fold_x = Scatter(parts, r.low2, mid, r.high2)
+
+    def unproject(j):
+        parts[j] = mm(dproj[block_of(chip_of(j), T2), :], w_qkv[...], NT).astype(bf16)
+        fold_x.pair(j)
+    unproject(3)
+    unproject(1)
+    fold_x.onward(3)
+    unproject(2)
+    fold_x.onward(1)
+    unproject(0)
+    fold_x.onward(2)
     for k in range(1, 8):
         arrived(da_cols.at[block_of(ps(k), T)], da_base + k)
-
-    def out_grad(i):
-        go_part[i] = mm(c_all[:, pl.ds(at(i, KW), KW)], da_cols[...], TN).astype(bf16)
-    loop(Z, out_grad)
+    go_part = r.go_part
     fold_o = Fold(go_part, r.go_land, r.go_pass)
+
+    def out_grad(k):
+        go_part[pz(k)] = mm(c_all[:, block_of(pz(k), KW)], da_cols[...], TN).astype(bf16)
+    out_grad(1)
+    out_grad(3)
     fold_o.start()
+    out_grad(2)
+    out_grad(0)
+    projection_grad(2)
+    projection_grad(0)
+    col_z = r.col_z
+    cz_base = slots(4)
+    for k in (1, 2, 3):
+        send(colg, col_z.at[z], cz_base + k, (s, pz(k)))
+    col_z[z] = colg[...]
     vec_all[s] = vecg[...]
     for k in range(1, 8):
         arrived(vec_all.at[ps(k)], vec_base + k)
@@ -910,80 +969,47 @@
     for k in (1, 2, 3):
         send(vec_plane, vec_z.at[z], vz_base + k, (s, pz(k)))
     vec_z[z] = total
-    loop(3, lambda i: attend_back(i + 5))
-
-    def dq_rows(i):
-        here = pl.ds(at(i, T), T)
-        whole = (dq[here, :] * scale).astype(bf16).astype(f32)
-        dproj[here, :C] = (whole * r.cos[here, :] - swapped(whole) * r.sin[here, :]).astype(bf16)
-        colg[1:2, :3 * C] = colg[1:2, :3 * C] + jnp.sum(dproj[here, :].astype(f32), axis=0, keepdims=True)
-    loop(L // T, dq_rows)
-
-    gq_part = r.gq_part
-    for k in (1, 3, 2, 0):
-        gq_part[pz(k)] = mm(x_t[block_of(pz(k), KW), :], dproj[...]).astype(bf16)
-        if k == 3:
-            fold_qkv = Fold(gq_part, r.gq_land, r.gq_pass)
-            fold_qkv.start()
-    col_z = r.col_z
-    cz_base = slots(4)
-    for k in (1, 2, 3):
-        send(colg, col_z.at[z], cz_base + k, (s, pz(k)))
-    col_z[z] = colg[...]
-    fold_x = Scatter(parts, r.low2, mid, r.high2)
-
-    def unproject(j):
-        parts[j] = mm(dproj[block_of(chip_of(j), T2), :], w_qkv[...], NT).astype(bf16)
-        fold_x.pair(j)
-    unproject(1)
-    unproject(2)
-    fold_x.onward(1)
-    unproject(3)
-    fold_x.onward(2)
-    unproject(0)
-    fold_x.onward(3)
+    gd_all[block_of(s, UZ), :] = fold_dn.finish()
+    gather_gd.start()
     fold_o.middle()
-    fold_qkv.middle()
     gu_all[s] = fold_up.finish()
     gather_gu.start()
-    for k in (2, 4, 6):
-        gather_gd.pass_on(k)
+    fold_qkv.middle()
+    gather_gd.pass_on(2)
+    gather_gd.pass_on(4)
+    fold_x.ready()
+    dx_ref = r.dx
+
+    def input_back(i):
+        start = at(i, R)
+        rows = pl.ds(start, R)
+        dx_ref[rows, :] = (dh1[rows, :] + fold_x.rows(start, R)).astype(bf16)
+    loop(T // R, input_back, 2)
     go_all[:, block_of(s, C)] = fold_o.finish()
     gather_go.start()
+    gather_gd.pass_on(6)
+    gather_gu.pass_on(2)
+    gather_gu.pass_on(4)
+    gq_all[s] = fold_qkv.finish()
+    gather_gq.start()
     for k in (1, 2, 3):
         arrived(col_z.at[pz(k)], cz_base + k)
-    col_all = r.col_all
-    col_sum = r.col_sum
+    col_all, col_sum = r.col_all, r.col_sum
     col_sum[...] = col_z[0] + col_z[1] + col_z[2] + col_z[3]
     ca_base = slots(8)
     for k in range(1, 8):
         send(col_sum, col_all.at[s], ca_base + k, (ps(k), z))
     col_all[s] = col_sum[...]
-    fold_x.ready()
-    dx_ref = r.dx
-
-    def input_back(i):
-        start = at(i, R)
-        rows = pl.ds(start, R)
-        dx_ref[rows, :] = (dh1[rows, :] + fold_x.rows(start, R)).astype(bf16)
-    loop(T // R, input_back)
-    gq_all[s] = fold_qkv.finish()
-    gather_gq.start()
-    for k in (1, 3, 5, 7):
-        gather_gd.wait(k)
+    gather_gu.pass_on(6)
+    gather_go.pass_all()
+    gather_gd.wait()
     outs = [local(gd_all, r.gd)]
-    for k in (2, 4, 6):
-        gather_gu.pass_on(k)
-    for k in (2, 4, 6):
-        gather_go.pass_on(k)
-    for k in (1, 3, 5, 7):
-        gather_gu.wait(k)
+    gather_gu.wait()
     for o in range(S):
         for p in range(Z):
             lane = (p * S + o) * C
             outs.append(local(gu_all.at[o, :, pl.ds(p * C, C)], r.gu.at[:, pl.ds(lane, C)]))
-    for k in (1, 3, 5, 7):
-        gather_go.wait(k)
+    gather_go.wait()
     outs.append(local(go_all, r.go))
 
     for k in (1, 2, 3):
@@ -1006,10 +1032,8 @@
         at_row = first_row.projection_bias + i
         gsm[at_row:at_row + 1, :] = col_all[number % S, 1:2, block_of(number // S, C)]
 
-    for k in (2, 4, 6):
-        gather_gq.pass_on(k)
-    for k in (1, 3, 5, 7):
-        gather_gq.wait(k)
+    gather_gq.pass_all()
+    gather_gq.wait()
     for o in range(S):
         for t in range(3):
             lane = (t * S + o) * C
@@ -1038,19 +1062,18 @@
         starts[name] = at_row
         at_row += value.shape[0] // C
     rows = -(-at_row // 8) * 8
-    packed = jnp.concatenate(list(small.values())).astype(bf16).astype(f32).reshape(at_row, C)
-    packed = jnp.pad(packed, ((0, rows - at_row), (0, 0)))
-
     half = HEAD_DIM // 2
     inverse = np.float32(10000.0) ** (np.float32(-2.0) * np.arange(half, dtype=np.float32) / np.float32(HEAD_DIM))
     angles = np.arange(L, dtype=np.float32)[:, None] * inverse.astype(np.float32)[None, :]
     cosine = np.tile(np.cos(angles), (1, C // half))
     sine = np.tile(np.concatenate([-np.sin(angles), np.sin(angles)], axis=1), (1, C // HEAD_DIM))
 
-    inputs = dict(x=(hidden_in[0], 0), ct=(cotangent[0], 0), segr=(segment_ids, 0),
-              segc=(segment_ids.reshape(L, 1), 0), cos=(jnp.asarray(cosine), 0), sin=(jnp.asarray(sine), 0),
-              small=(packed, 0), proj=(projection, 1), wo=(output_weight, 1), up=(up_weight, 1),
-              dn=(down_weight, 1))
+    inputs = dict(x=(hidden_in[0], 0), ct=(cotangent[0], 0), seg=(segment_ids, 0),
+                  cos=(jnp.asarray(cosine), 0), sin=(jnp.asarray(sine), 0),
+                  b_projection=(projection_bias[None], 0), b_output=(output_bias[None], 0),
+                  gain1=(first_gain[None], 0), shift1=(first_shift[None], 0), b_up=(up_bias[None], 0),
+                  b_down=(down_bias[None], 0), gain2=(second_gain[None], 0), shift2=(second_shift[None], 0),
+                  proj=(projection, 1), wo=(output_weight, 1), up=(up_weight, 1), dn=(down_weight, 1))
     outputs = dict(out=((T, D), bf16, 0), dx=((T, D), bf16, 0), gsm=((rows, C), f32, 0),
                gq=(projection.shape, bf16, 1), go=(output_weight.shape, bf16, 1),
                gu=(up_weight.shape, bf16, 1), gd=(down_weight.shape, bf16, 1))
@@ -1060,8 +1083,7 @@
         w_o=((D, D), bf16), st_wo=((KW, C), f32), w_up=((D, F), bf16), st_up=((KW, F), f32),
         w_dn=((F, D), bf16), st_dn=((UZ, D), f32), small_all=((Z, rows, C), f32), vec=((8, D), f32),
         vecg=((8, D), f32), q=((L, C), bf16), k=((L, C), bf16), v=((L, C), bf16),
-        s_buf=((2 * T, L), f32), dp_buf=((2 * T, L), f32), p_buf=((2 * T, L), bf16),
-        ds_buf=((2 * T, L), bf16), col_a=((2 * T, C), f32), col_b=((2 * T, C), f32), lse=((8, L), f32),
+        seg_r=((8, L), f32), seg_c=((L, C), f32), small=((rows, C), f32), lse=((8, L), f32),
         delta=((8, L), f32), c_f=((L, C), f32), c_heads=((L, C), bf16), c_tok=((T, D), bf16),
         a_buf=((T, D), f32), n1=((T, D), f32), y1=((T, D), f32), r1=((T, C), f32),
         y_all=((L, D), bf16), y_t=((D, L), bf16), u_buf=((2 * T, F), f32), g=((L, F), bf16),
@@ -1094,15 +1116,39 @@
         name="fused_layer",
     )(*[value for value, _ in inputs.values()])
     out, dx, gsm, gq, go, gu, gd = results
-    flat = gsm.reshape(-1)
-    small_grads = [lax.slice(flat, (starts[name] * C,), (starts[name] * C + value.shape[0],))
-                   for name, value in small.items()]
-    pb, ob, g1, s1, ub, db, g2, s2 = small_grads
-    return (out[None], dx[None], gq.astype(f32), pb, go.astype(f32), ob, g1, s1, gu.astype(f32), ub, gd.astype(f32),
-            db, g2, s2)
-
-
-SLOTS = 192
+    steps = 8
+
+    def tile(value):
+        return pl.BlockSpec((value.shape[0] // steps, value.shape[1]), lambda i: (i, 0))
+
+    def whole(n):
+        return pl.BlockSpec((1, n), lambda i: (0, 0))
+    wide = (gq, go, gu, gd)
+    counts = [value.shape[0] for value in small.values()]
+    results = pl.pallas_call(
+        partial(widen, tuple(starts.values())),
+        grid=(steps,),
+        out_shape=[jax.ShapeDtypeStruct(value.shape, value.dtype) for value in (out, dx)]
+        + [jax.ShapeDtypeStruct(value.shape, f32) for value in wide]
+        + [jax.ShapeDtypeStruct((1, n), f32) for n in counts],
+        in_specs=[tile(out), tile(dx), *map(tile, wide), pl.BlockSpec((rows, C), lambda i: (0, 0))],
+        out_specs=[tile(out), tile(dx), *map(tile, wide), *map(whole, counts)],
+        name="widen",
+    )(out, dx, *wide, gsm)
+    out, dx, gq, go, gu, gd = results[:6]
+    pb, ob, g1, s1, ub, db, g2, s2 = [value[0] for value in results[6:]]
+    return (out[None], dx[None], gq, pb, go, ob, g1, s1, gu, ub, gd, db, g2, s2)
+
+
+def widen(starts, out, dx, gq, go, gu, gd, small, *results):
+    for source, result in zip((out, dx, gq, go, gu, gd), results):
+        result[...] = source[...].astype(result.dtype)
+    for start, result in zip(starts, results[6:]):
+        for i in range(result.shape[1] // 128):
+            result[0:1, i * 128:(i + 1) * 128] = small[start + i:start + i + 1, :]
+
+
+SLOTS = 200
 LOCAL = 80
 
 

time: 257 us -> 200 us (0.78)
  Pallas kernels: 231 us -> 196 us
  other arithmetic: 15.9 us -> 1.28 us
  local copies, waits for them, and re-layouts: 8.3 us -> 1.27 us
    pallas_call x1, Pallas kernels: 231 us -> 187 us  [fused_shards(): pl.pallas_call(partial(fused_layer, sizes), out_shape=[jax.ShapeDtypeStru...]
    convert_element_type x4 -> x0, other arithmetic: 9.83 us -> none  [the longest x1 4.25 us: fused_shards(): gu.astype(f32)]
    pallas_call x0 -> x1, Pallas kernels: none -> 9.25 us  [fused_shards(): pl.pallas_call(partial(widen, tuple(starts.values())), grid=(steps,), out...]
    another operation x7 -> x0, other arithmetic: 4.78 us -> none
    slice x3 -> x0, local copies, waits for them, and re-layouts: 3.91 us -> none  [fused_shards(): lax.slice(flat, (starts[name] * C,), (starts[name] * C + value.shape[0],))]
    unnamed x19 -> x0, local copies, waits for them, and re-layouts: 2.69 us -> none
where the time goes in v2:
time: 200 us; the launch traced here: 199 us
  Pallas kernels  196 us (98%)
    pallas_call x1, Pallas kernels, fused_shards(): pl.pallas_call(partial(fused_layer, sizes), out_shape=[jax.ShapeDtypeStru...  187 us
    pallas_call x1, Pallas kernels, fused_shards(): pl.pallas_call(partial(widen, tuple(starts.values())), grid=(steps,), out...  9.25 us

profile of v2, /device:TPU:0, one launch (start us, length us, event | category | flops | bytes accessed | tf_op | source)
XLA Modules:
  0.0 199.2 jit_solution(16902963919424118999)
XLA Ops:
  0.6 1.3 broadcast_in_dim.30.refs_5_
  1.9 186.8 %fused_layer.1 = (bf16[128,1024]{1,0:T(8,128)(2,1)}, bf16[128,1024]{1,0:T(8,128)(2,1)}, f32[32,128]{1,0:T(8,128)}, bf16[256,3072]{1,0:T(8,128)(2,1)}, bf16[256,1...) custom-call(bf16[128,1024]{1,0:T(8,128)(2,1)} %bitcast.18, bf16[128,1024]{1,0:T(8,128)(2,1)} %bitcast.19, ...), custom_call_target="tpu_custom_call" | custom-call | tf_op jit(solution)/shard_map/fused_layer/pallas_call | solution.py:1108
  188.7 9.2 %widen.1 = (bf16[128,1024]{1,0:T(8,128)(2,1)}, bf16[128,1024]{1,0:T(8,128)(2,1)}, f32[256,3072]{1,0:T(8,128)}, f32[256,1024]{1,0:T(8,128)}, f32[256,4096]{1,0:T(...) custom-call(bf16[128,1024]{1,0:T(8,128)(2,1)} %get-tuple-element.35., ...), custom_call_target="tpu_custom_call" | custom-call | tf_op jit(solution)/shard_map/widen/pallas_call | solution.py:1128
  197.9 1.3 reduce

commit v3 on v2

--- a/solution.py
+++ b/solution.py
@@ -3,6 +3,7 @@
 import jax
 import jax.numpy as jnp
 import numpy as np
+import math
 from types import SimpleNamespace
 from jax import lax
 from jax.experimental import pallas as pl
@@ -358,41 +359,54 @@
     def chip_of(j):
         return flip(xbit, j % 2) + 2 * flip(ybit, j // 2)
 
-    counter = [0, 0]
-    pending = []
-
-    def slots(n):
-        counter[0] += n
-        return counter[0] - n
-
-    def remote(src, dst, slot, dev):
-        return pltpu.make_async_remote_copy(
-            src_ref=src, dst_ref=dst, send_sem=ssem.at[slot], recv_sem=rsem.at[slot],
-            device_id=dev, device_id_type=MESH)
-
-    def send(src, dst, slot, dev):
-        copy = remote(src, dst, slot, dev)
-        copy.start()
-        pending.append(copy)
-        return copy
-
-    def drop(copies):
-        for copy in copies:
-            copy.wait_send()
-        pending[:] = [other for other in pending if all(other is not copy for copy in copies)]
+    counter = [0, 0, 0]
+    closing = []
+
+    def take(which, n=1):
+        counter[which] += n
+        return counter[which] - n
+
+    def landings(n=1):
+        return take(0, n)
+
+    def size(ref):
+        return math.prod(ref.shape) * jnp.dtype(ref.dtype).itemsize
+
+    def extent(n):
+        if n <= size(r.c_f):
+            return r.c_f.at[pl.ds(0, n * L // size(r.c_f))]
+        return r.y_all.at[pl.ds(0, n * L // size(r.y_all))]
 
     def arrived(ref, slot):
-        remote(ref, ref, slot, (ps(1), z)).wait_recv()
+        pltpu.make_async_copy(ref, ref, rsem.at[slot]).wait()
+
+    class Batch:
+        def __init__(self, count, like):
+            self.slot, self.bytes, self.open = take(1), count * size(like), True
+            closing.append(self)
+
+        def send(self, src, dst, slot, dev):
+            pltpu.make_async_remote_copy(
+                src_ref=src, dst_ref=dst, send_sem=ssem.at[self.slot], recv_sem=rsem.at[slot],
+                device_id=dev, device_id_type=MESH).start()
+
+        def close(self):
+            if self.open:
+                everything = extent(self.bytes)
+                pltpu.make_async_copy(everything, everything, ssem.at[self.slot]).wait()
+            self.open = False
 
     def local(src, dst):
-        copy = pltpu.make_async_copy(src, dst, lsem.at[counter[1]])
-        counter[1] += 1
+        copy = pltpu.make_async_copy(src, dst, lsem.at[take(2)])
         copy.start()
         return copy
 
     class Gather:
-        def __init__(self, place):
-            self.place, self.base = place, slots(9)
+        def __init__(self, place, at_once=True):
+            self.place, self.at_once = place, at_once
+            self.batch = Batch(7, place(0))
+            self.near, self.across = landings(2), landings(2)
+            self.other = landings() if at_once else landings(4)
 
         def half(self, k, part):
             there = self.place(ps(k))
@@ -401,60 +415,69 @@
 
         def start(self, src=None):
             mine = self.place(s)
-            for k in (2, 4, 1):
-                send(mine if src is None else src, mine, self.base + k, (ps(k), z))
+            src = mine if src is None else src
+            self.batch.send(src, mine, self.near, (ps(2), z))
+            self.batch.send(src, mine, self.near + 1, (ps(4), z))
+            self.batch.send(src, mine, self.other, (ps(1), z))
 
         def pass_on(self, k):
             there = self.place(ps(k))
             if k == 2:
-                arrived(there, self.base + 2)
-                send(self.half(2, 0), self.half(2, 0), self.base + 6, (ps(4), z))
+                arrived(there, self.near)
+                self.batch.send(self.half(2, 0), self.half(2, 0), self.across, (ps(4), z))
             elif k == 4:
-                arrived(there, self.base + 4)
-                send(self.half(4, 1), self.half(4, 1), self.base + 8, (ps(2), z))
+                arrived(there, self.near + 1)
+                self.batch.send(self.half(4, 1), self.half(4, 1), self.across + 1, (ps(2), z))
             else:
-                arrived(self.half(6, 0), self.base + 6)
-                arrived(self.half(6, 1), self.base + 8)
-            send(there, there, self.base + k + 1, (ps(1), z))
+                arrived(self.half(6, 0), self.across)
+                arrived(self.half(6, 1), self.across + 1)
+            self.batch.send(there, there, self.other + (0 if self.at_once else k // 2), (ps(1), z))
 
         def pass_all(self):
             for k in (2, 4, 6):
                 self.pass_on(k)
 
-        def wait(self, *which):
-            for k in which or (1, 3, 5, 7):
-                arrived(self.place(ps(k)), self.base + k)
+        def wait(self, k=None):
+            if self.at_once:
+                arrived(extent(4 * size(self.place(0))), self.other)
+            else:
+                arrived(self.place(ps(k)), self.other + k // 2)
 
     class Spread:
         def __init__(self, place):
-            self.place, self.base = place, slots(4)
+            self.place, self.batch, self.base = place, Batch(3, place(0)), landings(3)
 
         def start(self, *which):
             mine = self.place(z)
             for k in which or (2, 1):
-                send(mine, mine, self.base + k, (s, pz(k)))
+                self.batch.send(mine, mine, self.base + k - 1, (s, pz(k)))
 
         def pass_on(self):
             there = self.place(pz(2))
-            arrived(there, self.base + 2)
-            send(there, there, self.base + 3, (s, pz(1)))
+            arrived(there, self.base + 1)
+            self.batch.send(there, there, self.base + 2, (s, pz(1)))
 
         def wait(self):
             for k in (1, 3):
-                arrived(self.place(pz(k)), self.base + k)
+                arrived(self.place(pz(k)), self.base + k - 1)
+
+        def wait_all(self):
+            for k in (1, 2, 3):
+                arrived(self.place(pz(k)), self.base + k - 1)
 
     class Fold:
         def __init__(self, parts, landing, passing):
-            self.parts, self.landing, self.passing, self.base = parts, landing, passing, slots(3)
+            self.parts, self.landing, self.passing = parts, landing, passing
+            self.batch, self.base = Batch(3, passing), landings(3)
 
         def start(self):
-            send(self.parts.at[pz(1)], self.landing.at[0], self.base, (s, pz(1)))
-            send(self.parts.at[pz(3)], self.landing.at[1], self.base + 1, (s, pz(1)))
+            self.batch.send(self.parts.at[pz(3)], self.landing.at[1], self.base + 1, (s, pz(1)))
+            self.batch.send(self.parts.at[pz(1)], self.landing.at[0], self.base, (s, pz(1)))
 
         def middle(self):
             arrived(self.landing.at[1], self.base + 1)
             self.passing[...] = (self.parts[pz(2)].astype(f32) + self.landing[1].astype(f32)).astype(bf16)
-            send(self.passing, self.landing.at[2], self.base + 2, (s, pz(2)))
+            self.batch.send(self.passing, self.landing.at[2], self.base + 2, (s, pz(2)))
 
         def finish(self):
             arrived(self.landing.at[0], self.base)
@@ -464,23 +487,21 @@
 
     class Scatter:
         def __init__(self, parts, low, mid, high):
-            self.parts, self.low, self.mid, self.high, self.base = parts, low, mid, high, slots(8)
-            self.sent = []
+            self.parts, self.low, self.mid, self.high = parts, low, mid, high
+            self.batch, self.base, self.last = Batch(7, mid.at[0]), landings(4), landings()
 
         def pair(self, j):
-            self.sent.append(send(self.parts.at[j, block_of(1 - core, T)], self.low.at[j],
-                                  self.base + j, (ps(1), z)))
+            self.batch.send(self.parts.at[j, block_of(1 - core, T)], self.low.at[j], self.base + j, (ps(1), z))
 
         def onward(self, j):
             arrived(self.low.at[j], self.base + j)
             own = self.parts[j, block_of(core, T), :].astype(f32)
             self.mid[j] = (own + self.low[j].astype(f32)).astype(bf16)
-            self.sent.append(send(self.mid.at[j], self.high.at[j], self.base + 4 + j, (ps(2 * j), z)))
+            self.batch.send(self.mid.at[j], self.high.at[j], self.last, (ps(2 * j), z))
 
         def ready(self):
             arrived(self.low.at[0], self.base)
-            for j in (1, 2, 3):
-                arrived(self.high.at[j], self.base + 4 + j)
+            arrived(self.high.at[pl.ds(1, 3)], self.last)
 
         def rows(self, at, n):
             own = self.parts[0, pl.ds(pl.multiple_of(core * T + at, n), n), :].astype(f32)
@@ -489,6 +510,21 @@
                 total = total + self.high[j, pl.ds(at, n), :].astype(f32)
             return total
 
+    class Share:
+        def __init__(self, count, like):
+            self.count, self.batch, self.slot, self.bytes = count, Batch(count, like), landings(), count * size(like)
+
+        def plane(self, src, dst):
+            for k in (6, 7, 2, 3, 4, 5, 1):
+                self.batch.send(src(ps(k)), dst, self.slot, (ps(k), z))
+
+        def column(self, src, dst):
+            for k in (2, 3, 1):
+                self.batch.send(src, dst, self.slot, (s, pz(k)))
+
+        def wait(self):
+            arrived(extent(self.bytes), self.slot)
+
     def loop(count, body, unroll=1):
         def step(i, carry):
             body(i)
@@ -532,69 +568,80 @@
         pl.semaphore_signal(barrier, inc=1, device_id=(ps(k), z), device_id_type=MESH)
     for k in range(1, Z):
         pl.semaphore_signal(barrier, inc=1, device_id=(s, pz(k)), device_id_type=MESH)
+    x_ref, ct_ref = r.v_x, r.v_ct
+    x_load = local(r.x, x_ref)
+    wo_load = local(r.wo.at[:, block_of(s, C)], r.st_wo)
     proj_loads = [local(r.proj.at[:, block_of(i * (D // C) + s, C)], r.st_proj.at[:, pl.ds(i * C, C)])
                   for i in range(3)]
-    wo_load = local(r.wo.at[:, block_of(s, C)], r.st_wo)
+    raw = ((r.b_projection, r.v_projection, first_row.projection_bias), (r.b_output, r.v_output, first_row.output_bias),
+           (r.gain1, r.v_gain1, first_row.first_gain), (r.shift1, r.v_shift1, first_row.first_shift),
+           (r.b_up, r.v_up, first_row.up_bias), (r.b_down, r.v_down, first_row.down_bias),
+           (r.gain2, r.v_gain2, first_row.second_gain), (r.shift2, r.v_shift2, first_row.second_shift))
+    raw_loads = [local(source, ref) for source, ref, _ in raw]
+    seg_load = local(r.seg, r.v_seg)
     up_loads = [local(r.up.at[:, block_of(i * (D // C) + s, C)], r.st_up.at[:, pl.ds(i * C, C)])
                 for i in range(Z)]
     dn_load = local(r.dn.at[block_of(s, UZ), :], r.st_dn)
-    pl.semaphore_wait(barrier, S + Z - 2)
-
-    x_ref, x_all = r.x, r.x_all
-    w_qkv, w_o, w_up, w_dn = r.w_qkv, r.w_o, r.w_up, r.w_dn
+    late_loads = [local(r.cos, r.v_cos), local(r.sin, r.v_sin), local(r.ct, ct_ref)]
+    cos_ref, sin_ref = r.v_cos, r.v_sin
+
+    x_all, w_qkv, w_o, w_up, w_dn = r.x_all, r.w_qkv, r.w_o, r.w_up, r.w_dn
     gather_x = Gather(lambda o: x_all.at[block_of(o, T)])
-    gather_x.start(x_ref)
     spread_qkv = Spread(lambda p: w_qkv.at[block_of(p, KW)])
     spread_o = Spread(lambda p: w_o.at[block_of(p, KW), block_of(s, C)])
     spread_up = Spread(lambda p: w_up.at[block_of(p, KW)])
     spread_dn = Spread(lambda p: w_dn.at[block_of(p, UZ)])
     gather_o = Gather(lambda o: w_o.at[:, block_of(o, C)])
-
+    x_load.wait()
+    pl.semaphore_wait(barrier, S + Z - 2)
+    gather_x.start(x_ref)
+    wo_load.wait()
+    w_o[block_of(z, KW), block_of(s, C)] = r.st_wo[...].astype(bf16)
+    spread_o.start(2, 3, 1)
     for copy in proj_loads:
         copy.wait()
     w_qkv[block_of(z, KW), :] = r.st_proj[...].astype(bf16)
     spread_qkv.start()
 
     small, small_all, seg_c, seg_r = r.small, r.small_all, r.seg_c, r.seg_r
-    raw = ((r.b_projection, first_row.projection_bias), (r.b_output, first_row.output_bias),
-           (r.gain1, first_row.first_gain), (r.shift1, first_row.first_shift), (r.b_up, first_row.up_bias),
-           (r.b_down, first_row.down_bias), (r.gain2, first_row.second_gain), (r.shift2, first_row.second_shift))
-    for ref, start in raw:
+    for copy, (_, ref, start) in zip(raw_loads, raw):
+        copy.wait()
         for i in range(ref.shape[1] // C):
             small[start + i:start + i + 1, :] = ref[0:1, i * C:(i + 1) * C].astype(bf16).astype(f32)
-    small_base = slots(4)
     x_all[block_of(s, T), :] = x_ref[...]
-    wo_load.wait()
-    w_o[block_of(z, KW), block_of(s, C)] = r.st_wo[...].astype(bf16)
+    vecg[...] = jnp.zeros((8, D), f32)
+    seg_load.wait()
+    seg_r[...] = jnp.broadcast_to(r.v_seg[...].astype(f32), (8, L))
+
+    def seg_turn(i):
+        here = pl.ds(at(i, T), T)
+        seg_c[here, :] = jnp.transpose(jnp.broadcast_to(seg_r[0:1, here], (T, T)))
+    loop(L // T, seg_turn)
     for copy in up_loads:
         copy.wait()
     w_up[block_of(z, KW), :] = r.st_up[...].astype(bf16)
     dn_load.wait()
     w_dn[block_of(z, UZ), :] = r.st_dn[...].astype(bf16)
-    vecg[...] = jnp.zeros((8, D), f32)
-    seg_r[...] = jnp.broadcast_to(r.seg[...].astype(f32), (8, L))
-
-    def seg_turn(i):
-        here = pl.ds(at(i, T), T)
-        seg_c[here, :] = jnp.transpose(jnp.broadcast_to(seg_r[0:1, here], (T, T)))
-    loop(L // T, seg_turn)
-
-    spread_qkv.pass_on()
+    share_small = Share(3, small)
     small_all[z] = small[...]
-    for k in (1, 2, 3):
-        send(small, small_all.at[z], small_base + k, (s, pz(k)))
-    spread_o.start()
+
     gather_x.pass_on(2)
     gather_x.pass_on(4)
-    spread_up.start(2)
+    spread_o.wait_all()
+    gather_o.start()
     gather_x.pass_on(6)
     gather_x.wait()
+    spread_qkv.pass_on()
+    share_small.column(small, small_all.at[z])
+    spread_up.start()
     x_t = r.x_t
     turn(x_all, x_t)
-    spread_o.pass_on()
-    spread_up.start(1)
-    for k in (1, 2, 3):
-        arrived(small_all.at[pz(k)], small_base + k)
+    for copy in late_loads:
+        copy.wait()
+    gather_o.pass_on(2)
+    gather_o.pass_on(4)
+    spread_qkv.wait()
+    share_small.wait()
     for p in range(Z):
         for start, i in wide:
             for half in range(KW // C):
@@ -607,21 +654,19 @@
         number = t * (D // C) + s
         vec[6:7, t * C:(t + 1) * C] = small_all[number // per, pl.ds(first_row.projection_bias + number % per, 1), :]
 
-    spread_qkv.wait()
     q_ref, k_ref, v_ref = r.q, r.k, r.v
     scale = HEAD_DIM ** -0.5
 
     def project(i):
         here = pl.ds(at(i, T2), T2)
         out = mm(x_all[here, :], w_qkv[...]) + row(PROJECTION_BIAS, 3 * C)
-        cosine, sine = r.cos[here, :], r.sin[here, :]
+        cosine, sine = cos_ref[here, :], sin_ref[here, :]
         q0, k0 = out[:, :C], out[:, C:2 * C]
         q_ref[here, :] = ((q0 * cosine + swapped(q0) * sine).astype(bf16).astype(f32) * scale).astype(bf16)
         k_ref[here, :] = (k0 * cosine + swapped(k0) * sine).astype(bf16)
         v_ref[here, :] = out[:, 2 * C:].astype(bf16)
     loop(L // T2, project)
-    spread_o.wait()
-    gather_o.start()
+    gather_o.pass_on(6)
 
     lse, c_f, c_heads, c_tok = r.lse, r.c_f, r.c_heads, r.c_tok
     R = 16
@@ -645,10 +690,7 @@
         for h in range(2):
             lse[h:h + 1, here] = jnp.transpose(logs[h * T:(h + 1) * T, :])[0:1, :]
 
-    c_base = slots(8)
-
-    def c_copy(k):
-        return remote(c_heads.at[block_of(ps(k), T)], c_tok.at[:, block_of(s, C)], c_base + k, (ps(k), z))
+    share_c = Share(7, c_heads.at[pl.ds(0, T)])
 
     def attend_and_send(i):
         k = 7 - i
@@ -656,17 +698,13 @@
 
         @pl.when(k > 0)
         def _():
-            c_copy(k).start()
+            share_c.batch.send(c_heads.at[block_of(ps(k), T)], c_tok.at[:, block_of(s, C)], share_c.slot, (ps(k), z))
     loop(8, attend_and_send)
     spread_up.pass_on()
     spread_dn.start()
     c_tok[:, block_of(s, C)] = c_heads[block_of(s, T), :]
-    gather_o.pass_on(2)
-    gather_o.pass_on(4)
-    gather_o.pass_on(6)
     gather_o.wait()
-    for k in range(1, 8):
-        arrived(c_tok.at[:, block_of(ps(k), C)], c_base + k)
+    share_c.wait()
 
     a_buf = r.a_buf
     a_buf[...] = mm(c_tok[...], w_o[...])
@@ -686,11 +724,10 @@
         y1[rows, :] = out
         y_all[pl.ds(pl.multiple_of(s * T + i * R, R), R), :] = out.astype(bf16)
     loop(T // R, first_norm, 4)
-    gather_y = Gather(lambda o: y_all.at[block_of(o, T)])
+    gather_y = Gather(lambda o: y_all.at[block_of(o, T)], False)
     gather_y.start()
     c_all = r.c_all
     gather_c = Gather(lambda o: c_all.at[block_of(o, T)])
-    gather_c.start(c_tok)
     c_all[block_of(s, T), :] = c_tok[...]
 
     u_buf, g_ref, d_ref, du_ref, dz_all = r.u_buf, r.g, r.d, r.du, r.dz_all
@@ -726,10 +763,9 @@
     lift(2)
     spread_dn.pass_on()
     gather_y.pass_on(6)
+    gather_c.start(c_tok)
     gather_y.wait(7)
     lift(3)
-    gather_c.pass_on(2)
-    gather_c.pass_on(4)
     turn(y_all, y_t)
     turn(g_ref, g_t)
     spread_dn.wait()
@@ -741,11 +777,11 @@
         if j == 2:
             fold_z.onward(1)
     fold_z.onward(2)
-    gather_c.pass_on(6)
-    gather_c.wait()
+    gather_c.pass_on(2)
+    gather_c.pass_on(4)
     fold_z.ready()
 
-    dh2, out_ref, ct_ref = r.dh2, r.out, r.ct
+    dh2, out_ref = r.dh2, r.v_out
 
     def add_row(i, value):
         vecg[i:i + 1, :] = vecg[i:i + 1, :] + jnp.sum(value, axis=0, keepdims=True)
@@ -769,9 +805,10 @@
         add_row(4, e * normal)
         add_row(5, e)
     loop(T // R, second_norm, 2)
-    gather_dz = Gather(lambda o: dz_all.at[block_of(o, T)])
+    outs = [local(out_ref, r.out)]
+    gather_dz = Gather(lambda o: dz_all.at[block_of(o, T)], False)
     gather_dz.start()
-    drop(fold_z.sent)
+    fold_z.batch.close()
 
     colg = r.colg
     colg[...] = jnp.zeros((8, F), f32)
@@ -802,6 +839,7 @@
     def up_grad(k):
         gu_part[pz(k)] = mm(y_t[block_of(pz(k), KW), :], du_ref[...]).astype(bf16)
 
+    gather_c.pass_on(6)
     gather_dz.wait(1)
     unlower(0)
     unlift(0)
@@ -830,11 +868,11 @@
 
     up_grad(1)
     up_grad(3)
-    fold_up.start()
     down_grad(2)
     down_grad(0)
     up_grad(2)
     up_grad(0)
+    gather_c.wait()
     fold_y.ready()
 
     dh1, da = r.dh1, r.da
@@ -852,26 +890,23 @@
         add_row(1, incoming * normal)
         add_row(2, incoming)
     loop(T // R, first_back, 2)
-    drop(fold_y.sent)
+    fold_y.batch.close()
 
     dc_tok, dc = r.dc_tok, r.dc
     dc_tok[...] = mm(da[...], w_o[...], NT).astype(bf16)
-    dc_base = slots(8)
-    for k in (7, 6, 5, 4, 3, 2, 1):
-        send(dc_tok.at[:, block_of(ps(k), C)], dc.at[block_of(s, T)], dc_base + k, (ps(k), z))
+    share_dc = Share(7, dc.at[pl.ds(0, T)])
+    share_dc.plane(lambda o: dc_tok.at[:, block_of(o, C)], dc.at[block_of(s, T)])
     dc[block_of(s, T), :] = dc_tok[:, block_of(s, C)]
     da_cols = r.da_cols
-    da_base = slots(8)
-    for k in (7, 6, 5, 4, 3, 2, 1):
-        send(da.at[:, block_of(ps(k), C)], da_cols.at[block_of(s, T)], da_base + k, (ps(k), z))
+    share_da = Share(7, da_cols.at[pl.ds(0, T)])
+    share_da.plane(lambda o: da.at[:, block_of(o, C)], da_cols.at[block_of(s, T)])
     da_cols[block_of(s, T), :] = da[:, block_of(s, C)]
     vec_all = r.vec_all
-    vec_base = slots(8)
-    for k in (7, 6, 5, 4, 3, 2, 1):
-        send(vecg, vec_all.at[s], vec_base + k, (ps(k), z))
+    share_vec = Share(7, vecg)
+    share_vec.plane(lambda o: vecg, vec_all.at[s])
     fold_dn.middle()
-    for k in range(1, 8):
-        arrived(dc.at[block_of(ps(k), T)], dc_base + k)
+    fold_up.start()
+    share_dc.wait()
 
     delta, dq, dproj = r.delta, r.dq, r.dproj
 
@@ -900,7 +935,7 @@
         dv = jnp.where(low_head, values[0], values[1]).astype(bf16)
         dk = jnp.where(low_head, mm(slopes[0], q_ref[...]), mm(slopes[1], q_ref[...])).astype(bf16).astype(f32)
         dproj[here, 2 * C:] = dv
-        dproj[here, C:2 * C] = (dk * r.cos[here, :] - swapped(dk) * r.sin[here, :]).astype(bf16)
+        dproj[here, C:2 * C] = (dk * cos_ref[here, :] - swapped(dk) * sin_ref[here, :]).astype(bf16)
         dq[...] = dq[...] + mm(jnp.concatenate(slopes, axis=0), jnp.concatenate(keys, axis=0), TN)
 
     gd_all, gu_all, go_all, gq_all = r.gd_all, r.gu_all, r.go_all, r.gq_all
@@ -908,13 +943,20 @@
     gather_gu = Gather(lambda o: gu_all.at[o])
     gather_go = Gather(lambda o: go_all.at[:, block_of(o, C)])
     gather_gq = Gather(lambda o: gq_all.at[o])
-    loop(L // T, attend_back)
-    fold_up.middle()
+
+    def attend_back_and_fold(i):
+        attend_back(i)
+
+        @pl.when(i == 3)
+        def _():
+            gd_all[block_of(s, UZ), :] = fold_dn.finish()
+            gather_gd.start()
+    loop(L // T, attend_back_and_fold)
 
     def dq_rows(i):
         here = pl.ds(at(i, T), T)
         whole = (dq[here, :] * scale).astype(bf16).astype(f32)
-        dproj[here, :C] = (whole * r.cos[here, :] - swapped(whole) * r.sin[here, :]).astype(bf16)
+        dproj[here, :C] = (whole * cos_ref[here, :] - swapped(whole) * sin_ref[here, :]).astype(bf16)
         colg[1:2, :3 * C] = colg[1:2, :3 * C] + jnp.sum(dproj[here, :].astype(f32), axis=0, keepdims=True)
     loop(L // T, dq_rows)
 
@@ -925,7 +967,10 @@
         gq_part[pz(k)] = mm(x_t[block_of(pz(k), KW), :], dproj[...]).astype(bf16)
     projection_grad(1)
     projection_grad(3)
+    fold_up.middle()
     fold_qkv.start()
+    gather_gd.pass_on(2)
+    gather_gd.pass_on(4)
     fold_x = Scatter(parts, r.low2, mid, r.high2)
 
     def unproject(j):
@@ -938,8 +983,7 @@
     fold_x.onward(1)
     unproject(0)
     fold_x.onward(2)
-    for k in range(1, 8):
-        arrived(da_cols.at[block_of(ps(k), T)], da_base + k)
+    share_da.wait()
     go_part = r.go_part
     fold_o = Fold(go_part, r.go_land, r.go_pass)
 
@@ -953,77 +997,61 @@
     projection_grad(2)
     projection_grad(0)
     col_z = r.col_z
-    cz_base = slots(4)
-    for k in (1, 2, 3):
-        send(colg, col_z.at[z], cz_base + k, (s, pz(k)))
+    share_col = Share(3, colg)
+    share_col.column(colg, col_z.at[z])
     col_z[z] = colg[...]
     vec_all[s] = vecg[...]
-    for k in range(1, 8):
-        arrived(vec_all.at[ps(k)], vec_base + k)
+    share_vec.wait()
     vec_plane, vec_z = r.vec_plane, r.vec_z
     total = vec_all[0]
     for o in range(1, S):
         total = total + vec_all[o]
     vec_plane[...] = total
-    vz_base = slots(4)
-    for k in (1, 2, 3):
-        send(vec_plane, vec_z.at[z], vz_base + k, (s, pz(k)))
+    share_sum = Share(3, vec_plane)
+    share_sum.column(vec_plane, vec_z.at[z])
     vec_z[z] = total
-    gd_all[block_of(s, UZ), :] = fold_dn.finish()
-    gather_gd.start()
-    fold_o.middle()
+    gather_gd.pass_on(6)
     gu_all[s] = fold_up.finish()
     gather_gu.start()
-    fold_qkv.middle()
-    gather_gd.pass_on(2)
-    gather_gd.pass_on(4)
+    gather_gd.wait()
+    outs.append(local(gd_all, r.gd))
     fold_x.ready()
-    dx_ref = r.dx
+    dx_ref = r.v_dx
 
     def input_back(i):
         start = at(i, R)
         rows = pl.ds(start, R)
         dx_ref[rows, :] = (dh1[rows, :] + fold_x.rows(start, R)).astype(bf16)
     loop(T // R, input_back, 2)
+    outs.append(local(dx_ref, r.dx))
+    fold_qkv.middle()
+    gather_gu.pass_on(2)
+    gather_gu.pass_on(4)
+    share_col.wait()
+    col_all, col_sum = r.col_all, r.col_sum
+    col_sum[...] = col_z[0] + col_z[1] + col_z[2] + col_z[3]
+    share_cols = Share(7, col_sum)
+    share_cols.plane(lambda o: col_sum, col_all.at[s])
+    col_all[s] = col_sum[...]
+    fold_o.middle()
+    gather_gu.pass_on(6)
+    gq_all[s] = fold_qkv.finish()
+    gather_gq.start()
+    gather_gu.wait()
+    outs.append(local(gu_all, r.gu))
     go_all[:, block_of(s, C)] = fold_o.finish()
     gather_go.start()
-    gather_gd.pass_on(6)
-    gather_gu.pass_on(2)
-    gather_gu.pass_on(4)
-    gq_all[s] = fold_qkv.finish()
-    gather_gq.start()
-    for k in (1, 2, 3):
-        arrived(col_z.at[pz(k)], cz_base + k)
-    col_all, col_sum = r.col_all, r.col_sum
-    col_sum[...] = col_z[0] + col_z[1] + col_z[2] + col_z[3]
-    ca_base = slots(8)
-    for k in range(1, 8):
-        send(col_sum, col_all.at[s], ca_base + k, (ps(k), z))
-    col_all[s] = col_sum[...]
-    gather_gu.pass_on(6)
-    gather_go.pass_all()
-    gather_gd.wait()
-    outs = [local(gd_all, r.gd)]
-    gather_gu.wait()
-    for o in range(S):
-        for p in range(Z):
-            lane = (p * S + o) * C
-            outs.append(local(gu_all.at[o, :, pl.ds(p * C, C)], r.gu.at[:, pl.ds(lane, C)]))
-    gather_go.wait()
-    outs.append(local(go_all, r.go))
-
-    for k in (1, 2, 3):
-        arrived(vec_z.at[pz(k)], vz_base + k)
-    for k in range(1, 8):
-        arrived(col_all.at[ps(k)], ca_base + k)
-    vec_plane2 = r.vec_sum
-    vec_plane2[...] = vec_z[0] + vec_z[1] + vec_z[2] + vec_z[3]
-    gsm = r.gsm
+
+    share_sum.wait()
+    share_cols.wait()
+    vec_sum = r.vec_sum
+    vec_sum[...] = vec_z[0] + vec_z[1] + vec_z[2] + vec_z[3]
+    gsm = r.v_gsm
     gsm[...] = jnp.zeros(gsm.shape, f32)
     for start, i in wide:
         for half in range(KW // C):
             at_row = start + half
-            gsm[at_row:at_row + 1, :] = vec_plane2[i:i + 1, block_of(z * (KW // C) + half, C)]
+            gsm[at_row:at_row + 1, :] = vec_sum[i:i + 1, block_of(z * (KW // C) + half, C)]
     for o in range(S):
         at_row = first_row.up_bias + o
         gsm[at_row:at_row + 1, :] = col_all[o, 0:1, block_of(z, C)]
@@ -1031,18 +1059,20 @@
         number = z * per + i
         at_row = first_row.projection_bias + i
         gsm[at_row:at_row + 1, :] = col_all[number % S, 1:2, block_of(number // S, C)]
-
-    gather_gq.pass_all()
+    outs.append(local(gsm, r.gsm))
+    gather_gq.pass_on(2)
+    gather_gq.pass_on(4)
+    gather_go.pass_all()
+    gather_gq.pass_on(6)
+    gather_go.wait()
+    outs.append(local(go_all, r.go))
     gather_gq.wait()
-    for o in range(S):
-        for t in range(3):
-            lane = (t * S + o) * C
-            outs.append(local(gq_all.at[o, :, pl.ds(t * C, C)], r.gq.at[:, pl.ds(lane, C)]))
+    outs.append(local(gq_all, r.gq))
     for copy in outs:
         copy.wait()
-    for copy in pending:
-        copy.wait_send()
-    loop(7, lambda i: c_copy(7 - i).wait_send())
+    for batch in closing:
+        batch.close()
+    assert counter[0] <= LANDINGS and counter[1] <= BATCHES and counter[2] <= LOCAL, counter
 
 
 def fused_shards(*args):
@@ -1068,17 +1098,20 @@
     cosine = np.tile(np.cos(angles), (1, C // half))
     sine = np.tile(np.concatenate([-np.sin(angles), np.sin(angles)], axis=1), (1, C // HEAD_DIM))
 
-    inputs = dict(x=(hidden_in[0], 0), ct=(cotangent[0], 0), seg=(segment_ids, 0),
-                  cos=(jnp.asarray(cosine), 0), sin=(jnp.asarray(sine), 0),
-                  b_projection=(projection_bias[None], 0), b_output=(output_bias[None], 0),
-                  gain1=(first_gain[None], 0), shift1=(first_shift[None], 0), b_up=(up_bias[None], 0),
-                  b_down=(down_bias[None], 0), gain2=(second_gain[None], 0), shift2=(second_shift[None], 0),
-                  proj=(projection, 1), wo=(output_weight, 1), up=(up_weight, 1), dn=(down_weight, 1))
-    outputs = dict(out=((T, D), bf16, 0), dx=((T, D), bf16, 0), gsm=((rows, C), f32, 0),
-               gq=(projection.shape, bf16, 1), go=(output_weight.shape, bf16, 1),
-               gu=(up_weight.shape, bf16, 1), gd=(down_weight.shape, bf16, 1))
+    inputs = dict(x=hidden_in[0], ct=cotangent[0], seg=segment_ids, cos=jnp.asarray(cosine), sin=jnp.asarray(sine),
+                  b_projection=projection_bias[None], b_output=output_bias[None], gain1=first_gain[None],
+                  shift1=first_shift[None], b_up=up_bias[None], b_down=down_bias[None], gain2=second_gain[None],
+                  shift2=second_shift[None], proj=projection, wo=output_weight, up=up_weight, dn=down_weight)
+    outputs = dict(out=((T, D), bf16), dx=((T, D), bf16), gsm=((rows, C), f32), gq=((8, KW, 3 * C), bf16),
+                   go=((KW, D), bf16), gu=((8, KW, F), bf16), gd=((8 * UZ, D), bf16))
+    landed = dict(v_x=inputs["x"], v_ct=inputs["ct"], v_seg=segment_ids, v_cos=inputs["cos"], v_sin=inputs["sin"],
+                  v_projection=inputs["b_projection"], v_output=inputs["b_output"], v_gain1=inputs["gain1"],
+                  v_shift1=inputs["shift1"], v_up=inputs["b_up"], v_down=inputs["b_down"], v_gain2=inputs["gain2"],
+                  v_shift2=inputs["shift2"])
     PART = (4, T, D)
-    scratch = dict(
+    scratch = {name: (value.shape, value.dtype) for name, value in landed.items()}
+    scratch.update(
+        v_out=((T, D), bf16), v_dx=((T, D), bf16), v_gsm=((rows, C), f32),
         x_all=((L, D), bf16), x_t=((D, L), bf16), w_qkv=((D, 3 * C), bf16), st_proj=((KW, 3 * C), f32),
         w_o=((D, D), bf16), st_wo=((KW, C), f32), w_up=((D, F), bf16), st_up=((KW, F), f32),
         w_dn=((F, D), bf16), st_dn=((UZ, D), f32), small_all=((Z, rows, C), f32), vec=((8, D), f32),
@@ -1099,57 +1132,67 @@
         vec_all=((8, 8, D), f32), vec_plane=((8, D), f32), vec_z=((Z, 8, D), f32), vec_sum=((8, D), f32),
         col_z=((Z, 8, F), f32), col_sum=((8, F), f32), col_all=((8, 8, F), f32),
         low0=(PART, bf16), high0=(PART, bf16), low1=(PART, bf16), high1=(PART, bf16), low2=(PART, bf16),
-        high2=(PART, bf16), ssem=(SLOTS,), rsem=(SLOTS,), lsem=(LOCAL,))
+        high2=(PART, bf16), ssem=(BATCHES,), rsem=(LANDINGS,), lsem=(LOCAL,))
     names = [*inputs, *outputs, *scratch]
     sizes = SimpleNamespace(names=names, T=T, D=D, L=L, F=F, first_row=SimpleNamespace(**starts))
 
-    def spec(anywhere):
-        return pl.BlockSpec(memory_space=pl.ANY if anywhere else pltpu.VMEM)
+    anywhere = pl.BlockSpec(memory_space=pl.ANY)
     results = pl.pallas_call(
         partial(fused_layer, sizes),
-        out_shape=[jax.ShapeDtypeStruct(shape, dtype) for shape, dtype, _ in outputs.values()],
-        in_specs=[spec(w) for _, w in inputs.values()],
-        out_specs=[spec(w) for *_, w in outputs.values()],
+        out_shape=[jax.ShapeDtypeStruct(*what) for what in outputs.values()],
+        in_specs=[anywhere] * len(inputs),
+        out_specs=[anywhere] * len(outputs),
         scratch_shapes=[pltpu.VMEM(*what) if len(what) == 2 else pltpu.SemaphoreType.DMA(what)
                         for what in scratch.values()],
         compiler_params=pltpu.CompilerParams(collective_id=0, has_side_effects=True, vmem_limit_bytes=67043328),
         name="fused_layer",
-    )(*[value for value, _ in inputs.values()])
+    )(*inputs.values())
     out, dx, gsm, gq, go, gu, gd = results
     steps = 8
 
     def tile(value):
         return pl.BlockSpec((value.shape[0] // steps, value.shape[1]), lambda i: (i, 0))
 
+    def grouped(value):
+        return pl.BlockSpec((8, value.shape[1] // steps, value.shape[2]), lambda i: (0, i, 0))
+
     def whole(n):
         return pl.BlockSpec((1, n), lambda i: (0, 0))
-    wide = (gq, go, gu, gd)
+    wide = [jax.ShapeDtypeStruct(value.shape, f32) for value in (projection, output_weight, up_weight, down_weight)]
     counts = [value.shape[0] for value in small.values()]
     results = pl.pallas_call(
         partial(widen, tuple(starts.values())),
         grid=(steps,),
-        out_shape=[jax.ShapeDtypeStruct(value.shape, value.dtype) for value in (out, dx)]
-        + [jax.ShapeDtypeStruct(value.shape, f32) for value in wide]
-        + [jax.ShapeDtypeStruct((1, n), f32) for n in counts],
-        in_specs=[tile(out), tile(dx), *map(tile, wide), pl.BlockSpec((rows, C), lambda i: (0, 0))],
+        out_shape=[jax.ShapeDtypeStruct((T, D), bf16)] * 2 + wide + [jax.ShapeDtypeStruct((1, n), f32) for n in counts],
+        in_specs=[tile(out), tile(dx), grouped(gq), tile(go), grouped(gu), tile(gd),
+                  pl.BlockSpec((rows, C), lambda i: (0, 0))],
         out_specs=[tile(out), tile(dx), *map(tile, wide), *map(whole, counts)],
         name="widen",
-    )(out, dx, *wide, gsm)
+    )(out, dx, gq, go, gu, gd, gsm)
     out, dx, gq, go, gu, gd = results[:6]
     pb, ob, g1, s1, ub, db, g2, s2 = [value[0] for value in results[6:]]
     return (out[None], dx[None], gq, pb, go, ob, g1, s1, gu, ub, gd, db, g2, s2)
 
 
 def widen(starts, out, dx, gq, go, gu, gd, small, *results):
-    for source, result in zip((out, dx, gq, go, gu, gd), results):
-        result[...] = source[...].astype(result.dtype)
+    C = small.shape[1]
+    for source, result in zip((out, dx), results):
+        result[...] = source[...]
+    results[3][...] = go[...].astype(f32)
+    results[5][...] = gd[...].astype(f32)
+    for source, result in ((gq, results[2]), (gu, results[4])):
+        for o in range(source.shape[0]):
+            for p in range(source.shape[2] // C):
+                lane = (p * source.shape[0] + o) * C
+                result[:, lane:lane + C] = source[o, :, p * C:(p + 1) * C].astype(f32)
     for start, result in zip(starts, results[6:]):
-        for i in range(result.shape[1] // 128):
-            result[0:1, i * 128:(i + 1) * 128] = small[start + i:start + i + 1, :]
-
-
-SLOTS = 200
-LOCAL = 80
+        for i in range(result.shape[1] // C):
+            result[0:1, i * C:(i + 1) * C] = small[start + i:start + i + 1, :]
+
+
+BATCHES = 36
+LANDINGS = 112
+LOCAL = 32
 
 
 def fits(mesh):

time: 200 us -> 186 us (0.930)
  Pallas kernels: 196 us -> 181 us
    pallas_call x1, Pallas kernels: 187 us -> 172 us  [fused_shards(): pl.pallas_call(partial(fused_layer, sizes), out_shape=[jax.ShapeDtypeStru...]
where the time goes in v3:
time: 186 us; the launch traced here: 184 us
  Pallas kernels  181 us (97%)
    pallas_call x1, Pallas kernels, fused_shards(): pl.pallas_call(partial(fused_layer, sizes), out_shape=[jax.ShapeDtypeStru...  172 us
    pallas_call x1, Pallas kernels, fused_shards(): pl.pallas_call(partial(widen, tuple(starts.values())), grid=(steps,), out...  9.3 us

profile of v3, /device:TPU:0, one launch (start us, length us, event | category | flops | bytes accessed | tf_op | source)
XLA Modules:
  0.0 184.2 jit_solution(193790204885325492)
XLA Ops:
  0.6 1.3 broadcast_in_dim.30.refs_5_
  1.9 171.7 %fused_layer.1 = (bf16[128,1024]{1,0:T(8,128)(2,1)}, bf16[128,1024]{1,0:T(8,128)(2,1)}, f32[32,128]{1,0:T(8,128)}, bf16[8,256,384]{2,1,0:T(8,128)(2,1)}, bf16[25...) custom-call(bf16[128,1024]{1,0:T(8,128)(2,1)} %bitcast.18, ...), custom_call_target="tpu_custom_call" | custom-call | tf_op jit(solution)/shard_map/fused_layer/pallas_call | solution.py:1140
  173.6 9.3 %widen.1 = (bf16[128,1024]{1,0:T(8,128)(2,1)}, bf16[128,1024]{1,0:T(8,128)(2,1)}, f32[256,3072]{1,0:T(8,128)}, f32[256,1024]{1,0:T(8,128)}, f32[256,4096]{1,0:T(...) custom-call(bf16[128,1024]{1,0:T(8,128)(2,1)} %get-tuple-element.35., ...), custom_call_target="tpu_custom_call" | custom-call | tf_op jit(solution)/shard_map/widen/pallas_call | solution.py:1163
  182.9 1.3 reduce

commit v4 on v3

--- a/solution.py
+++ b/solution.py
@@ -405,37 +405,45 @@
         def __init__(self, place, at_once=True):
             self.place, self.at_once = place, at_once
             self.batch = Batch(7, place(0))
-            self.near, self.across = landings(2), landings(2)
+            self.near, self.across = landings(4), landings(2)
             self.other = landings() if at_once else landings(4)
 
-        def half(self, k, part):
-            there = self.place(ps(k))
-            n = there.shape[0] // 2
-            return there.at[pl.ds(part * n, n)]
+        def part(self, ref, i):
+            n = ref.shape[0] // 2
+            return ref.at[pl.ds(i * n, n)]
 
         def start(self, src=None):
             mine = self.place(s)
             src = mine if src is None else src
-            self.batch.send(src, mine, self.near, (ps(2), z))
-            self.batch.send(src, mine, self.near + 1, (ps(4), z))
+            for slot, half, k in ((0, 0, 2), (3, 1, 4), (1, 1, 2), (2, 0, 4)):
+                self.batch.send(self.part(src, half), self.part(mine, half), self.near + slot, (ps(k), z))
             self.batch.send(src, mine, self.other, (ps(1), z))
 
-        def pass_on(self, k):
+        def to_partner(self, k):
             there = self.place(ps(k))
-            if k == 2:
-                arrived(there, self.near)
-                self.batch.send(self.half(2, 0), self.half(2, 0), self.across, (ps(4), z))
-            elif k == 4:
-                arrived(there, self.near + 1)
-                self.batch.send(self.half(4, 1), self.half(4, 1), self.across + 1, (ps(2), z))
-            else:
-                arrived(self.half(6, 0), self.across)
-                arrived(self.half(6, 1), self.across + 1)
             self.batch.send(there, there, self.other + (0 if self.at_once else k // 2), (ps(1), z))
 
+        def pass_near(self):
+            along_x, along_y = self.place(ps(2)), self.place(ps(4))
+            first, second = self.part(along_x, 0), self.part(along_y, 1)
+            arrived(first, self.near)
+            self.batch.send(first, first, self.across, (ps(4), z))
+            arrived(second, self.near + 3)
+            self.batch.send(second, second, self.across + 1, (ps(2), z))
+            arrived(self.part(along_x, 1), self.near + 1)
+            self.to_partner(2)
+            arrived(self.part(along_y, 0), self.near + 2)
+            self.to_partner(4)
+
+        def pass_far(self):
+            far = self.place(ps(6))
+            arrived(self.part(far, 0), self.across)
+            arrived(self.part(far, 1), self.across + 1)
+            self.to_partner(6)
+
         def pass_all(self):
-            for k in (2, 4, 6):
-                self.pass_on(k)
+            self.pass_near()
+            self.pass_far()
 
         def wait(self, k=None):
             if self.at_once:
@@ -488,7 +496,13 @@
     class Scatter:
         def __init__(self, parts, low, mid, high):
             self.parts, self.low, self.mid, self.high = parts, low, mid, high
-            self.batch, self.base, self.last = Batch(7, mid.at[0]), landings(4), landings()
+            self.batch, self.base, self.far, self.last = Batch(7, mid.at[0]), landings(4), landings(2), landings()
+
+        def half(self, ref, j, i):
+            return ref.at[j, :, pl.ds(i * (D // 2), D // 2)]
+
+        def send(self, j, i, slot, k):
+            self.batch.send(self.half(self.mid, j, i), self.half(self.high, j, i), slot, (ps(k), z))
 
         def pair(self, j):
             self.batch.send(self.parts.at[j, block_of(1 - core, T)], self.low.at[j], self.base + j, (ps(1), z))
@@ -497,16 +511,29 @@
             arrived(self.low.at[j], self.base + j)
             own = self.parts[j, block_of(core, T), :].astype(f32)
             self.mid[j] = (own + self.low[j].astype(f32)).astype(bf16)
-            self.batch.send(self.mid.at[j], self.high.at[j], self.last, (ps(2 * j), z))
+            if j == 1:
+                self.send(1, 0, self.last, 2)
+            elif j == 2:
+                self.send(2, 1, self.last, 4)
+            else:
+                self.send(3, 0, self.far, 2)
+                self.send(3, 1, self.far + 1, 4)
+
+        def cross(self):
+            for j, i, k in ((2, 0, 4), (1, 1, 2)):
+                arrived(self.half(self.high, 3, i), self.far + i)
+                ref = self.half(self.mid, j, i)
+                ref[...] = (ref[...].astype(f32) + self.half(self.high, 3, i)[...].astype(f32)).astype(bf16)
+                self.send(j, i, self.last, k)
 
         def ready(self):
             arrived(self.low.at[0], self.base)
-            arrived(self.high.at[pl.ds(1, 3)], self.last)
+            arrived(self.high.at[pl.ds(1, 2)], self.last)
 
         def rows(self, at, n):
             own = self.parts[0, pl.ds(pl.multiple_of(core * T + at, n), n), :].astype(f32)
             total = own + self.low[0, pl.ds(at, n), :].astype(f32)
-            for j in (1, 2, 3):
+            for j in (1, 2):
                 total = total + self.high[j, pl.ds(at, n), :].astype(f32)
             return total
 
@@ -592,22 +619,25 @@
     spread_up = Spread(lambda p: w_up.at[block_of(p, KW)])
     spread_dn = Spread(lambda p: w_dn.at[block_of(p, UZ)])
     gather_o = Gather(lambda o: w_o.at[:, block_of(o, C)])
-    x_load.wait()
-    pl.semaphore_wait(barrier, S + Z - 2)
-    gather_x.start(x_ref)
     wo_load.wait()
     w_o[block_of(z, KW), block_of(s, C)] = r.st_wo[...].astype(bf16)
-    spread_o.start(2, 3, 1)
     for copy in proj_loads:
         copy.wait()
     w_qkv[block_of(z, KW), :] = r.st_proj[...].astype(bf16)
+    x_load.wait()
+    pl.semaphore_wait(barrier, S + Z - 2)
+    spread_o.start(2, 3, 1)
     spread_qkv.start()
+    gather_x.start(x_ref)
 
     small, small_all, seg_c, seg_r = r.small, r.small_all, r.seg_c, r.seg_r
     for copy, (_, ref, start) in zip(raw_loads, raw):
         copy.wait()
-        for i in range(ref.shape[1] // C):
-            small[start + i:start + i + 1, :] = ref[0:1, i * C:(i + 1) * C].astype(bf16).astype(f32)
+        if ref.shape[1] == C:
+            small[start:start + ref.shape[0], :] = ref[...].astype(bf16).astype(f32)
+        else:
+            for i in range(ref.shape[1] // C):
+                small[start + i:start + i + 1, :] = ref[0:1, i * C:(i + 1) * C].astype(bf16).astype(f32)
     x_all[block_of(s, T), :] = x_ref[...]
     vecg[...] = jnp.zeros((8, D), f32)
     seg_load.wait()
@@ -625,11 +655,10 @@
     share_small = Share(3, small)
     small_all[z] = small[...]
 
-    gather_x.pass_on(2)
-    gather_x.pass_on(4)
+    gather_x.pass_near()
     spread_o.wait_all()
     gather_o.start()
-    gather_x.pass_on(6)
+    gather_x.pass_far()
     gather_x.wait()
     spread_qkv.pass_on()
     share_small.column(small, small_all.at[z])
@@ -638,8 +667,7 @@
     turn(x_all, x_t)
     for copy in late_loads:
         copy.wait()
-    gather_o.pass_on(2)
-    gather_o.pass_on(4)
+    gather_o.pass_near()
     spread_qkv.wait()
     share_small.wait()
     for p in range(Z):
@@ -666,7 +694,7 @@
         k_ref[here, :] = (k0 * cosine + swapped(k0) * sine).astype(bf16)
         v_ref[here, :] = out[:, 2 * C:].astype(bf16)
     loop(L // T2, project)
-    gather_o.pass_on(6)
+    gather_o.pass_far()
 
     lse, c_f, c_heads, c_tok = r.lse, r.c_f, r.c_heads, r.c_tok
     R = 16
@@ -755,14 +783,13 @@
     y_t, g_t = r.y_t, r.g_t
     gather_y.wait(1)
     lift(0)
-    gather_y.pass_on(2)
-    gather_y.pass_on(4)
+    gather_y.pass_near()
     gather_y.wait(3)
     lift(1)
     gather_y.wait(5)
     lift(2)
     spread_dn.pass_on()
-    gather_y.pass_on(6)
+    gather_y.pass_far()
     gather_c.start(c_tok)
     gather_y.wait(7)
     lift(3)
@@ -777,8 +804,8 @@
         if j == 2:
             fold_z.onward(1)
     fold_z.onward(2)
-    gather_c.pass_on(2)
-    gather_c.pass_on(4)
+    fold_z.cross()
+    gather_c.pass_near()
     fold_z.ready()
 
     dh2, out_ref = r.dh2, r.v_out
@@ -839,13 +866,12 @@
     def up_grad(k):
         gu_part[pz(k)] = mm(y_t[block_of(pz(k), KW), :], du_ref[...]).astype(bf16)
 
-    gather_c.pass_on(6)
+    gather_c.pass_far()
     gather_dz.wait(1)
     unlower(0)
     unlift(0)
     fold_y.pair(0)
-    gather_dz.pass_on(2)
-    gather_dz.pass_on(4)
+    gather_dz.pass_near()
     gather_dz.wait(3)
     unlower(1)
     unlift(1)
@@ -855,7 +881,7 @@
     fold_y.onward(1)
     unlift(2)
     fold_y.pair(2)
-    gather_dz.pass_on(6)
+    gather_dz.pass_far()
     fold_y.onward(2)
     gather_dz.wait(7)
     unlower(3)
@@ -869,6 +895,7 @@
     up_grad(1)
     up_grad(3)
     down_grad(2)
+    fold_y.cross()
     down_grad(0)
     up_grad(2)
     up_grad(0)
@@ -938,19 +965,32 @@
         dproj[here, C:2 * C] = (dk * cos_ref[here, :] - swapped(dk) * sin_ref[here, :]).astype(bf16)
         dq[...] = dq[...] + mm(jnp.concatenate(slopes, axis=0), jnp.concatenate(keys, axis=0), TN)
 
-    gd_all, gu_all, go_all, gq_all = r.gd_all, r.gu_all, r.go_all, r.gq_all
+    gd_all, gu_all, go_all, gqk_all, gv_all = r.gd_all, r.gu_all, r.go_all, r.gqk_all, r.gv_all
     gather_gd = Gather(lambda o: gd_all.at[block_of(o, UZ)])
     gather_gu = Gather(lambda o: gu_all.at[o])
     gather_go = Gather(lambda o: go_all.at[:, block_of(o, C)])
-    gather_gq = Gather(lambda o: gq_all.at[o])
+    gather_gqk = Gather(lambda o: gqk_all.at[o])
+    gather_gv = Gather(lambda o: gv_all.at[o])
+    go_part = r.go_part
+    fold_o = Fold(go_part, r.go_land, r.go_pass)
+
+    def out_grad(k):
+        go_part[pz(k)] = mm(c_all[:, block_of(pz(k), KW)], da_cols[...], TN).astype(bf16)
 
     def attend_back_and_fold(i):
         attend_back(i)
 
+        @pl.when(i == 1)
+        def _():
+            share_da.wait()
+            out_grad(1)
+            out_grad(3)
+            fold_o.start()
+
         @pl.when(i == 3)
         def _():
-            gd_all[block_of(s, UZ), :] = fold_dn.finish()
-            gather_gd.start()
+            out_grad(2)
+            out_grad(0)
     loop(L // T, attend_back_and_fold)
 
     def dq_rows(i):
@@ -960,17 +1000,19 @@
         colg[1:2, :3 * C] = colg[1:2, :3 * C] + jnp.sum(dproj[here, :].astype(f32), axis=0, keepdims=True)
     loop(L // T, dq_rows)
 
-    gq_part = r.gq_part
-    fold_qkv = Fold(gq_part, r.gq_land, r.gq_pass)
+    gqk_part, gv_part = r.gqk_part, r.gv_part
+    fold_qk = Fold(gqk_part, r.gqk_land, r.gqk_pass)
+    fold_v = Fold(gv_part, r.gv_land, r.gv_pass)
 
     def projection_grad(k):
-        gq_part[pz(k)] = mm(x_t[block_of(pz(k), KW), :], dproj[...]).astype(bf16)
+        grad = mm(x_t[block_of(pz(k), KW), :], dproj[...]).astype(bf16)
+        gqk_part[pz(k)] = grad[:, :2 * C]
+        gv_part[pz(k)] = grad[:, 2 * C:]
+    projection_grad(3)
     projection_grad(1)
-    projection_grad(3)
-    fold_up.middle()
-    fold_qkv.start()
-    gather_gd.pass_on(2)
-    gather_gd.pass_on(4)
+    fold_qk.start()
+    gd_all[block_of(s, UZ), :] = fold_dn.finish()
+    gather_gd.start()
     fold_x = Scatter(parts, r.low2, mid, r.high2)
 
     def unproject(j):
@@ -979,23 +1021,16 @@
     unproject(3)
     unproject(1)
     fold_x.onward(3)
+    fold_up.middle()
+    fold_v.start()
     unproject(2)
     fold_x.onward(1)
     unproject(0)
     fold_x.onward(2)
-    share_da.wait()
-    go_part = r.go_part
-    fold_o = Fold(go_part, r.go_land, r.go_pass)
-
-    def out_grad(k):
-        go_part[pz(k)] = mm(c_all[:, block_of(pz(k), KW)], da_cols[...], TN).astype(bf16)
-    out_grad(1)
-    out_grad(3)
-    fold_o.start()
-    out_grad(2)
-    out_grad(0)
     projection_grad(2)
     projection_grad(0)
+    fold_x.cross()
+    gather_gd.pass_near()
     col_z = r.col_z
     share_col = Share(3, colg)
     share_col.column(colg, col_z.at[z])
@@ -1010,11 +1045,9 @@
     share_sum = Share(3, vec_plane)
     share_sum.column(vec_plane, vec_z.at[z])
     vec_z[z] = total
-    gather_gd.pass_on(6)
-    gu_all[s] = fold_up.finish()
-    gather_gu.start()
-    gather_gd.wait()
-    outs.append(local(gd_all, r.gd))
+    fold_o.middle()
+    fold_qk.middle()
+    gather_gd.pass_far()
     fold_x.ready()
     dx_ref = r.v_dx
 
@@ -1024,23 +1057,31 @@
         dx_ref[rows, :] = (dh1[rows, :] + fold_x.rows(start, R)).astype(bf16)
     loop(T // R, input_back, 2)
     outs.append(local(dx_ref, r.dx))
-    fold_qkv.middle()
-    gather_gu.pass_on(2)
-    gather_gu.pass_on(4)
+    gu_all[s] = fold_up.finish()
+    gather_gu.start()
+    fold_v.middle()
+    go_all[:, block_of(s, C)] = fold_o.finish()
+    gather_go.start()
+    gather_gd.wait()
+    outs.append(local(gd_all, r.gd))
     share_col.wait()
     col_all, col_sum = r.col_all, r.col_sum
     col_sum[...] = col_z[0] + col_z[1] + col_z[2] + col_z[3]
     share_cols = Share(7, col_sum)
     share_cols.plane(lambda o: col_sum, col_all.at[s])
     col_all[s] = col_sum[...]
-    fold_o.middle()
-    gather_gu.pass_on(6)
-    gq_all[s] = fold_qkv.finish()
-    gather_gq.start()
+    gather_gu.pass_near()
+    gqk_all[s] = fold_qk.finish()
+    gather_gqk.start()
+    gather_go.pass_near()
+    gather_gu.pass_far()
+    gv_all[s] = fold_v.finish()
+    gather_gv.start()
+    gather_go.pass_far()
     gather_gu.wait()
     outs.append(local(gu_all, r.gu))
-    go_all[:, block_of(s, C)] = fold_o.finish()
-    gather_go.start()
+    gather_go.wait()
+    outs.append(local(go_all, r.go))
 
     share_sum.wait()
     share_cols.wait()
@@ -1060,14 +1101,14 @@
         at_row = first_row.projection_bias + i
         gsm[at_row:at_row + 1, :] = col_all[number % S, 1:2, block_of(number // S, C)]
     outs.append(local(gsm, r.gsm))
-    gather_gq.pass_on(2)
-    gather_gq.pass_on(4)
-    gather_go.pass_all()
-    gather_gq.pass_on(6)
-    gather_go.wait()
-    outs.append(local(go_all, r.go))
-    gather_gq.wait()
-    outs.append(local(gq_all, r.gq))
+    gather_gqk.pass_near()
+    gather_gv.pass_near()
+    gather_gqk.pass_far()
+    gather_gv.pass_far()
+    gather_gqk.wait()
+    outs.append(local(gqk_all, r.gqk))
+    gather_gv.wait()
+    outs.append(local(gv_all, r.gv))
     for copy in outs:
         copy.wait()
     for batch in closing:
@@ -1099,10 +1140,10 @@
     sine = np.tile(np.concatenate([-np.sin(angles), np.sin(angles)], axis=1), (1, C // HEAD_DIM))
 
     inputs = dict(x=hidden_in[0], ct=cotangent[0], seg=segment_ids, cos=jnp.asarray(cosine), sin=jnp.asarray(sine),
-                  b_projection=projection_bias[None], b_output=output_bias[None], gain1=first_gain[None],
+                  b_projection=projection_bias.reshape(-1, C), b_output=output_bias[None], gain1=first_gain[None],
                   shift1=first_shift[None], b_up=up_bias[None], b_down=down_bias[None], gain2=second_gain[None],
                   shift2=second_shift[None], proj=projection, wo=output_weight, up=up_weight, dn=down_weight)
-    outputs = dict(out=((T, D), bf16), dx=((T, D), bf16), gsm=((rows, C), f32), gq=((8, KW, 3 * C), bf16),
+    outputs = dict(out=((T, D), bf16), dx=((T, D), bf16), gsm=((rows, C), f32), gqk=((8, KW, 2 * C), bf16), gv=((8, KW, C), bf16),
                    go=((KW, D), bf16), gu=((8, KW, F), bf16), gd=((8 * UZ, D), bf16))
     landed = dict(v_x=inputs["x"], v_ct=inputs["ct"], v_seg=segment_ids, v_cos=inputs["cos"], v_sin=inputs["sin"],
                   v_projection=inputs["b_projection"], v_output=inputs["b_output"], v_gain1=inputs["gain1"],
@@ -1125,9 +1166,10 @@
         colg=((8, F), f32), gd_part=((Z, UZ, D), bf16), gd_land=((3, UZ, D), bf16), gd_pass=((UZ, D), bf16),
         gu_part=((Z, KW, F), bf16), gu_land=((3, KW, F), bf16), gu_pass=((KW, F), bf16),
         go_part=((Z, KW, C), bf16), go_land=((3, KW, C), bf16), go_pass=((KW, C), bf16),
-        gq_part=((Z, KW, 3 * C), bf16), gq_land=((3, KW, 3 * C), bf16), gq_pass=((KW, 3 * C), bf16),
+        gqk_part=((Z, KW, 2 * C), bf16), gqk_land=((3, KW, 2 * C), bf16), gqk_pass=((KW, 2 * C), bf16),
+        gv_part=((Z, KW, C), bf16), gv_land=((3, KW, C), bf16), gv_pass=((KW, C), bf16),
         gd_all=((8 * UZ, D), bf16), gu_all=((8, KW, F), bf16), go_all=((KW, D), bf16),
-        gq_all=((8, KW, 3 * C), bf16), da=((T, D), bf16), dc_tok=((T, D), bf16), dc=((L, C), bf16),
+        gqk_all=((8, KW, 2 * C), bf16), gv_all=((8, KW, C), bf16), da=((T, D), bf16), dc_tok=((T, D), bf16), dc=((L, C), bf16),
         da_cols=((L, C), bf16), c_all=((L, D), bf16), dq=((L, C), f32), dproj=((L, 3 * C), bf16),
         vec_all=((8, 8, D), f32), vec_plane=((8, D), f32), vec_z=((Z, 8, D), f32), vec_sum=((8, D), f32),
         col_z=((Z, 8, F), f32), col_sum=((8, F), f32), col_all=((8, 8, F), f32),
@@ -1147,51 +1189,103 @@
         compiler_params=pltpu.CompilerParams(collective_id=0, has_side_effects=True, vmem_limit_bytes=67043328),
         name="fused_layer",
     )(*inputs.values())
-    out, dx, gsm, gq, go, gu, gd = results
-    steps = 8
-
-    def tile(value):
-        return pl.BlockSpec((value.shape[0] // steps, value.shape[1]), lambda i: (i, 0))
-
-    def grouped(value):
-        return pl.BlockSpec((8, value.shape[1] // steps, value.shape[2]), lambda i: (0, i, 0))
-
-    def whole(n):
-        return pl.BlockSpec((1, n), lambda i: (0, 0))
+    out, dx, gsm, gqk, gv, go, gu, gd = results
     wide = [jax.ShapeDtypeStruct(value.shape, f32) for value in (projection, output_weight, up_weight, down_weight)]
-    counts = [value.shape[0] for value in small.values()]
+    narrow = [jax.ShapeDtypeStruct((1, value.shape[0]) if value is not projection_bias else (value.shape[0] // C, C), f32)
+              for value in small.values()]
+    sources = [out, dx, gqk, gv, go, gu, gd, gsm]
+    outcomes = [out, dx] + wide + narrow
     results = pl.pallas_call(
         partial(widen, tuple(starts.values())),
-        grid=(steps,),
-        out_shape=[jax.ShapeDtypeStruct((T, D), bf16)] * 2 + wide + [jax.ShapeDtypeStruct((1, n), f32) for n in counts],
-        in_specs=[tile(out), tile(dx), grouped(gq), tile(go), grouped(gu), tile(gd),
-                  pl.BlockSpec((rows, C), lambda i: (0, 0))],
-        out_specs=[tile(out), tile(dx), *map(tile, wide), *map(whole, counts)],
+        out_shape=[jax.ShapeDtypeStruct(value.shape, value.dtype) for value in outcomes],
+        in_specs=[anywhere] * len(sources),
+        out_specs=[anywhere] * len(outcomes),
+        scratch_shapes=[pltpu.VMEM(value.shape, value.dtype) for value in sources + outcomes[2:]]
+        + [pltpu.SemaphoreType.DMA((LOCAL,))] * 2,
+        compiler_params=pltpu.CompilerParams(vmem_limit_bytes=56 << 20),
         name="widen",
-    )(out, dx, gq, go, gu, gd, gsm)
+    )(*sources)
     out, dx, gq, go, gu, gd = results[:6]
-    pb, ob, g1, s1, ub, db, g2, s2 = [value[0] for value in results[6:]]
+    pb, ob, g1, s1, ub, db, g2, s2 = [value.reshape(-1) for value in results[6:]]
     return (out[None], dx[None], gq, pb, go, ob, g1, s1, gu, ub, gd, db, g2, s2)
 
 
-def widen(starts, out, dx, gq, go, gu, gd, small, *results):
-    C = small.shape[1]
-    for source, result in zip((out, dx), results):
-        result[...] = source[...]
-    results[3][...] = go[...].astype(f32)
-    results[5][...] = gd[...].astype(f32)
-    for source, result in ((gq, results[2]), (gu, results[4])):
-        for o in range(source.shape[0]):
-            for p in range(source.shape[2] // C):
-                lane = (p * source.shape[0] + o) * C
-                result[:, lane:lane + C] = source[o, :, p * C:(p + 1) * C].astype(f32)
-    for start, result in zip(starts, results[6:]):
-        for i in range(result.shape[1] // C):
-            result[0:1, i * C:(i + 1) * C] = small[start + i:start + i + 1, :]
-
-
-BATCHES = 36
-LANDINGS = 112
+def widen(starts, *refs):
+    sources, results = refs[:8], refs[8:22]
+    held, made, insem, outsem = refs[22:30], refs[30:42], refs[42], refs[43]
+    out, dx, gqk, gv, go, gu, gd, gsm = held
+    C = gsm.shape[1]
+    count = [0, 0]
+
+    def fetch(source, ref):
+        copy = pltpu.make_async_copy(source, ref, insem.at[count[0]])
+        count[0] += 1
+        copy.start()
+        return copy
+    stores = []
+
+    def store(ref, result):
+        copy = pltpu.make_async_copy(ref, result, outsem.at[count[1]])
+        count[1] += 1
+        copy.start()
+        stores.append(copy)
+
+    def piece(i, at, n):
+        window = (slice(None), pl.ds(at, n)) if len(held[i].shape) == 3 else (pl.ds(at, n),)
+        return fetch(sources[i].at[window], held[i].at[window])
+
+    def grouped(i, target, at, n, first):
+        source, result = held[i], made[target]
+        groups = source.shape[0]
+
+        def step(j, carry):
+            rows = pl.ds(pl.multiple_of(at + j * 32, 32), 32)
+            for o in range(groups):
+                for p in range(source.shape[2] // C):
+                    lane = ((first + p) * groups + o) * C
+                    result[rows, lane:lane + C] = source[o, rows, p * C:(p + 1) * C].astype(f32)
+            return carry
+        lax.fori_loop(0, n // 32, step, 0)
+
+    def plain(i, target, at, n, _):
+        source, result = held[i], made[target]
+
+        def step(j, carry):
+            rows = pl.ds(pl.multiple_of(at + j * 32, 32), 32)
+            result[rows, :] = source[rows, :].astype(f32)
+            return carry
+        lax.fori_loop(0, n // 32, step, 0)
+
+    work = []
+    for i, target, n, body, first in ((5, 2, 64, grouped, 0), (6, 3, 256, plain, 0), (2, 0, 64, grouped, 0),
+                                      (3, 0, 64, grouped, 2), (4, 1, 256, plain, 0)):
+        total = held[i].shape[-2]
+        for at in range(0, total, n):
+            work.append((piece(i, at, n), i, target, at, n, body, first))
+    whole = [fetch(sources[i], held[i]) for i in (0, 1, 7)]
+    for copy, i, target, at, n, body, first in work:
+        copy.wait()
+        body(i, target, at, n, first)
+        if i != 2:
+            rows = pl.ds(at, n)
+            store(made[target].at[rows], results[2 + target].at[rows])
+    for copy in whole:
+        copy.wait()
+    store(out, results[0])
+    store(dx, results[1])
+    for start, ref, result in zip(starts, made[4:], results[6:]):
+        if ref.shape[1] == C:
+            ref[...] = gsm[start:start + ref.shape[0], :]
+        else:
+            for i in range(ref.shape[1] // C):
+                ref[0:1, i * C:(i + 1) * C] = gsm[start + i:start + i + 1, :]
+        store(ref, result)
+    for copy in stores:
+        copy.wait()
+
+
+BATCHES = 38
+LANDINGS = 144
 LOCAL = 32
 
 

time: 186 us -> 175 us (0.941)
  Pallas kernels: 181 us -> 174 us
    pallas_call x1, Pallas kernels: 172 us -> 167 us  [fused_shards(): pl.pallas_call(partial(fused_layer, sizes), out_shape=[jax.ShapeDtypeStru...]
    pallas_call x1, Pallas kernels: 9.3 us -> 6.89 us  [fused_shards(): pl.pallas_call(partial(widen, tuple(starts.values())), out_shape=[jax.Sha...]
where the time goes in v4:
time: 175 us
  Pallas kernels  174 us (99%)
    pallas_call x1, Pallas kernels, fused_shards(): pl.pallas_call(partial(fused_layer, sizes), out_shape=[jax.ShapeDtypeStru...  167 us
    pallas_call x1, Pallas kernels, fused_shards(): pl.pallas_call(partial(widen, tuple(starts.values())), out_shape=[jax.Sha...  6.89 us

profile of v4, /device:TPU:0, one launch (start us, length us, event | category | flops | bytes accessed | tf_op | source)
XLA Modules:
  0.0 175.0 jit_solution(10499012770765132126)
XLA Ops:
  0.7 167.3 %fused_layer.1 = (bf16[128,1024]{1,0:T(8,128)(2,1)}, bf16[128,1024]{1,0:T(8,128)(2,1)}, f32[32,128]{1,0:T(8,128)}, bf16[8,256,256]{2,1,0:T(8,128)(2,1)}, bf16[8,...) custom-call(bf16[128,1024]{1,0:T(8,128)(2,1)} %bitcast.20, ...), custom_call_target="tpu_custom_call" | custom-call | tf_op jit(solution)/shard_map/fused_layer/pallas_call | solution.py:1182
  168.0 6.9 %widen.1 = (bf16[128,1024]{1,0:T(8,128)(2,1)}, bf16[128,1024]{1,0:T(8,128)(2,1)}, f32[256,3072]{1,0:T(8,128)}, f32[256,1024]{1,0:T(8,128)}, f32[256,4096]{1,0:T(...) custom-call(bf16[128,1024]{1,0:T(8,128)(2,1)} %get-tuple-element.36., ...), custom_call_target="tpu_custom_call" | custom-call | tf_op jit(solution)/shard_map/widen/pallas_call | solution.py:1198

commit v5 on v4

--- a/solution.py
+++ b/solution.py
@@ -474,24 +474,26 @@
                 arrived(self.place(pz(k)), self.base + k - 1)
 
     class Fold:
-        def __init__(self, parts, landing, passing):
-            self.parts, self.landing, self.passing = parts, landing, passing
-            self.batch, self.base = Batch(3, passing), landings(3)
+        def __init__(self, parts, landing, passing, first=0, count=None):
+            self.rows = pl.ds(first, count or passing.shape[0])
+            self.parts, self.landing, self.passing = parts, landing, passing.at[self.rows]
+            self.batch, self.base = Batch(3, self.passing), landings(3)
 
         def start(self):
-            self.batch.send(self.parts.at[pz(3)], self.landing.at[1], self.base + 1, (s, pz(1)))
-            self.batch.send(self.parts.at[pz(1)], self.landing.at[0], self.base, (s, pz(1)))
+            for i, k in ((1, 3), (0, 1)):
+                self.batch.send(self.parts.at[pz(k), self.rows], self.landing.at[i, self.rows], self.base + i, (s, pz(1)))
 
         def middle(self):
-            arrived(self.landing.at[1], self.base + 1)
-            self.passing[...] = (self.parts[pz(2)].astype(f32) + self.landing[1].astype(f32)).astype(bf16)
-            self.batch.send(self.passing, self.landing.at[2], self.base + 2, (s, pz(2)))
+            arrived(self.landing.at[1, self.rows], self.base + 1)
+            self.passing[...] = (self.parts[pz(2), self.rows, :].astype(f32)
+                                 + self.landing[1, self.rows, :].astype(f32)).astype(bf16)
+            self.batch.send(self.passing, self.landing.at[2, self.rows], self.base + 2, (s, pz(2)))
 
         def finish(self):
-            arrived(self.landing.at[0], self.base)
-            arrived(self.landing.at[2], self.base + 2)
-            return (self.parts[z].astype(f32) + self.landing[0].astype(f32)
-                    + self.landing[2].astype(f32)).astype(bf16)
+            arrived(self.landing.at[0, self.rows], self.base)
+            arrived(self.landing.at[2, self.rows], self.base + 2)
+            return (self.parts[z, self.rows, :].astype(f32) + self.landing[0, self.rows, :].astype(f32)
+                    + self.landing[2, self.rows, :].astype(f32)).astype(bf16)
 
     class Scatter:
         def __init__(self, parts, low, mid, high):
@@ -857,8 +859,8 @@
 
     fold_y = Scatter(parts, r.low1, mid, r.high1)
     gd_part, gu_part = r.gd_part, r.gu_part
-    fold_dn = Fold(gd_part, r.gd_land, r.gd_pass)
-    fold_up = Fold(gu_part, r.gu_land, r.gu_pass)
+    folds_dn = [Fold(gd_part, r.gd_land, r.gd_pass, i * (UZ // 2), UZ // 2) for i in range(2)]
+    folds_up = [Fold(gu_part, r.gu_land, r.gu_pass, i * (KW // 2), KW // 2) for i in range(2)]
 
     def down_grad(k):
         gd_part[pz(k)] = mm(g_t[block_of(pz(k), UZ), :], dz_all[...]).astype(bf16)
@@ -884,18 +886,21 @@
     gather_dz.pass_far()
     fold_y.onward(2)
     gather_dz.wait(7)
+    down_grad(3)
+    down_grad(1)
+    folds_dn[0].start()
+    folds_dn[1].start()
     unlower(3)
     unlift(3)
     fold_y.pair(3)
-    down_grad(1)
-    down_grad(3)
-    fold_dn.start()
+    up_grad(3)
     fold_y.onward(3)
 
     up_grad(1)
-    up_grad(3)
     down_grad(2)
     fold_y.cross()
+    folds_dn[0].middle()
+    folds_up[0].start()
     down_grad(0)
     up_grad(2)
     up_grad(0)
@@ -931,8 +936,8 @@
     vec_all = r.vec_all
     share_vec = Share(7, vecg)
     share_vec.plane(lambda o: vecg, vec_all.at[s])
-    fold_dn.middle()
-    fold_up.start()
+    folds_dn[1].middle()
+    folds_up[1].start()
     share_dc.wait()
 
     delta, dq, dproj = r.delta, r.dq, r.dproj
@@ -980,18 +985,21 @@
     def attend_back_and_fold(i):
         attend_back(i)
 
-        @pl.when(i == 1)
+        @pl.when(i == 4)
         def _():
             share_da.wait()
-            out_grad(1)
-            out_grad(3)
+            for k in (3, 1, 2, 0):
+                out_grad(k)
             fold_o.start()
 
-        @pl.when(i == 3)
+        @pl.when(i == 6)
         def _():
-            out_grad(2)
-            out_grad(0)
+            folds_up[0].middle()
     loop(L // T, attend_back_and_fold)
+
+    for i in range(2):
+        gd_all[pl.ds(pl.multiple_of(s * UZ + i * (UZ // 2), UZ // 2), UZ // 2), :] = folds_dn[i].finish()
+    gather_gd.start()
 
     def dq_rows(i):
         here = pl.ds(at(i, T), T)
@@ -1010,18 +1018,16 @@
         gv_part[pz(k)] = grad[:, 2 * C:]
     projection_grad(3)
     projection_grad(1)
-    fold_qk.start()
-    gd_all[block_of(s, UZ), :] = fold_dn.finish()
-    gather_gd.start()
     fold_x = Scatter(parts, r.low2, mid, r.high2)
 
     def unproject(j):
         parts[j] = mm(dproj[block_of(chip_of(j), T2), :], w_qkv[...], NT).astype(bf16)
         fold_x.pair(j)
+    fold_qk.start()
     unproject(3)
     unproject(1)
     fold_x.onward(3)
-    fold_up.middle()
+    folds_up[1].middle()
     fold_v.start()
     unproject(2)
     fold_x.onward(1)
@@ -1045,9 +1051,8 @@
     share_sum = Share(3, vec_plane)
     share_sum.column(vec_plane, vec_z.at[z])
     vec_z[z] = total
+    gather_gd.pass_far()
     fold_o.middle()
-    fold_qk.middle()
-    gather_gd.pass_far()
     fold_x.ready()
     dx_ref = r.v_dx
 
@@ -1057,11 +1062,10 @@
         dx_ref[rows, :] = (dh1[rows, :] + fold_x.rows(start, R)).astype(bf16)
     loop(T // R, input_back, 2)
     outs.append(local(dx_ref, r.dx))
-    gu_all[s] = fold_up.finish()
+    for i in range(2):
+        gu_all[s, pl.ds(i * (KW // 2), KW // 2), :] = folds_up[i].finish()
     gather_gu.start()
-    fold_v.middle()
-    go_all[:, block_of(s, C)] = fold_o.finish()
-    gather_go.start()
+    fold_qk.middle()
     gather_gd.wait()
     outs.append(local(gd_all, r.gd))
     share_col.wait()
@@ -1070,18 +1074,20 @@
     share_cols = Share(7, col_sum)
     share_cols.plane(lambda o: col_sum, col_all.at[s])
     col_all[s] = col_sum[...]
+    fold_v.middle()
     gather_gu.pass_near()
+    go_all[:, block_of(s, C)] = fold_o.finish()
+    gather_go.start()
     gqk_all[s] = fold_qk.finish()
     gather_gqk.start()
-    gather_go.pass_near()
-    gather_gu.pass_far()
     gv_all[s] = fold_v.finish()
     gather_gv.start()
-    gather_go.pass_far()
+    gather_gu.pass_far()
+    gather_go.pass_near()
+    gather_gqk.pass_near()
+    gather_gv.pass_near()
     gather_gu.wait()
     outs.append(local(gu_all, r.gu))
-    gather_go.wait()
-    outs.append(local(go_all, r.go))
 
     share_sum.wait()
     share_cols.wait()
@@ -1101,10 +1107,11 @@
         at_row = first_row.projection_bias + i
         gsm[at_row:at_row + 1, :] = col_all[number % S, 1:2, block_of(number // S, C)]
     outs.append(local(gsm, r.gsm))
-    gather_gqk.pass_near()
-    gather_gv.pass_near()
+    gather_go.pass_far()
     gather_gqk.pass_far()
     gather_gv.pass_far()
+    gather_go.wait()
+    outs.append(local(go_all, r.go))
     gather_gqk.wait()
     outs.append(local(gqk_all, r.gqk))
     gather_gv.wait()
@@ -1284,8 +1291,8 @@
         copy.wait()
 
 
-BATCHES = 38
-LANDINGS = 144
+BATCHES = 42
+LANDINGS = 148
 LOCAL = 32
 
 

time: 175 us -> 171 us (0.977)
  Pallas kernels: 174 us -> 169 us
    pallas_call x1, Pallas kernels: 167 us -> 163 us  [fused_shards(): pl.pallas_call(partial(fused_layer, sizes), out_shape=[jax.ShapeDtypeStru...]
where the time goes in v5:
time: 171 us; the launch traced here: 170 us
  Pallas kernels  169 us (99%)
    pallas_call x1, Pallas kernels, fused_shards(): pl.pallas_call(partial(fused_layer, sizes), out_shape=[jax.ShapeDtypeStru...  163 us
    pallas_call x1, Pallas kernels, fused_shards(): pl.pallas_call(partial(widen, tuple(starts.values())), out_shape=[jax.Sha...  6.89 us

profile of v5, /device:TPU:0, one launch (start us, length us, event | category | flops | bytes accessed | tf_op | source)
XLA Modules:
  0.0 170.3 jit_solution(895529096570358053)
XLA Ops:
  0.7 162.6 %fused_layer.1 = (bf16[128,1024]{1,0:T(8,128)(2,1)}, bf16[128,1024]{1,0:T(8,128)(2,1)}, f32[32,128]{1,0:T(8,128)}, bf16[8,256,256]{2,1,0:T(8,128)(2,1)}, bf16[8,...) custom-call(bf16[128,1024]{1,0:T(8,128)(2,1)} %bitcast.20, ...), custom_call_target="tpu_custom_call" | custom-call | tf_op jit(solution)/shard_map/fused_layer/pallas_call | solution.py:1189
  163.3 6.9 %widen.1 = (bf16[128,1024]{1,0:T(8,128)(2,1)}, bf16[128,1024]{1,0:T(8,128)(2,1)}, f32[256,3072]{1,0:T(8,128)}, f32[256,1024]{1,0:T(8,128)}, f32[256,4096]{1,0:T(...) custom-call(bf16[128,1024]{1,0:T(8,128)(2,1)} %get-tuple-element.36., ...), custom_call_target="tpu_custom_call" | custom-call | tf_op jit(solution)/shard_map/widen/pallas_call | solution.py:1205

commit v6 on v5

--- a/solution.py
+++ b/solution.py
@@ -496,23 +496,29 @@
                     + self.landing[2, self.rows, :].astype(f32)).astype(bf16)
 
     class Scatter:
-        def __init__(self, parts, low, mid, high):
+        def __init__(self, parts, low, mid, high, first=0, count=T):
             self.parts, self.low, self.mid, self.high = parts, low, mid, high
-            self.batch, self.base, self.far, self.last = Batch(7, mid.at[0]), landings(4), landings(2), landings()
+            self.first, self.count, self.window = first, count, pl.ds(first, count)
+            self.batch = Batch(7, mid.at[0, self.window])
+            self.base, self.far, self.last = landings(4), landings(2), landings()
+
+        def rows_of(self, which):
+            return pl.ds(pl.multiple_of(which * T + self.first, self.count), self.count)
 
         def half(self, ref, j, i):
-            return ref.at[j, :, pl.ds(i * (D // 2), D // 2)]
+            return ref.at[j, self.window, pl.ds(i * (D // 2), D // 2)]
 
         def send(self, j, i, slot, k):
             self.batch.send(self.half(self.mid, j, i), self.half(self.high, j, i), slot, (ps(k), z))
 
         def pair(self, j):
-            self.batch.send(self.parts.at[j, block_of(1 - core, T)], self.low.at[j], self.base + j, (ps(1), z))
+            self.batch.send(self.parts.at[j, self.rows_of(1 - core)], self.low.at[j, self.window],
+                            self.base + j, (ps(1), z))
 
         def onward(self, j):
-            arrived(self.low.at[j], self.base + j)
-            own = self.parts[j, block_of(core, T), :].astype(f32)
-            self.mid[j] = (own + self.low[j].astype(f32)).astype(bf16)
+            arrived(self.low.at[j, self.window], self.base + j)
+            own = self.parts[j, self.rows_of(core), :].astype(f32)
+            self.mid[j, self.window, :] = (own + self.low[j, self.window, :].astype(f32)).astype(bf16)
             if j == 1:
                 self.send(1, 0, self.last, 2)
             elif j == 2:
@@ -529,8 +535,8 @@
                 self.send(j, i, self.last, k)
 
         def ready(self):
-            arrived(self.low.at[0], self.base)
-            arrived(self.high.at[pl.ds(1, 2)], self.last)
+            arrived(self.low.at[0, self.window], self.base)
+            arrived(self.high.at[pl.ds(1, 2), self.window], self.last)
 
         def rows(self, at, n):
             own = self.parts[0, pl.ds(pl.multiple_of(core * T + at, n), n), :].astype(f32)
@@ -781,7 +787,8 @@
     def lower(j):
         parts[j] = mm(g_ref[block_of(chip_of(j), T2), :], w_dn[...]).astype(bf16)
 
-    fold_z = Scatter(parts, r.low0, mid, r.high0)
+    H = T // 2
+    folds_z = [Scatter(parts, r.low0, mid, r.high0, i * H, H) for i in range(2)]
     y_t, g_t = r.y_t, r.g_t
     gather_y.wait(1)
     lift(0)
@@ -798,17 +805,21 @@
     turn(y_all, y_t)
     turn(g_ref, g_t)
     spread_dn.wait()
-    for j in (3, 1, 2, 0):
+    for j in (3, 1, 2):
         lower(j)
-        fold_z.pair(j)
-        if j == 1:
-            fold_z.onward(3)
-        if j == 2:
-            fold_z.onward(1)
-    fold_z.onward(2)
-    fold_z.cross()
-    gather_c.pass_near()
-    fold_z.ready()
+        for fold in folds_z:
+            fold.pair(j)
+    for j in (3, 1, 2):
+        folds_z[0].onward(j)
+    folds_z[1].onward(3)
+    lower(0)
+    for fold in folds_z:
+        fold.pair(0)
+    folds_z[0].cross()
+    folds_z[1].onward(1)
+    folds_z[1].onward(2)
+    folds_z[1].cross()
+    folds_z[0].ready()
 
     dh2, out_ref = r.dh2, r.v_out
 
@@ -823,7 +834,7 @@
     def second_norm(i):
         start = at(i, R)
         rows = pl.ds(start, R)
-        normal, root = norm(y1[rows, :] + fold_z.rows(start, R) + row(DOWN_BIAS))
+        normal, root = norm(y1[rows, :] + folds_z[0].rows(start, R) + row(DOWN_BIAS))
         out_ref[rows, :] = (normal * row(SECOND_GAIN) + row(SECOND_SHIFT)).astype(bf16)
         e = ct_ref[rows, :].astype(f32)
         grad = norm_back(e, normal, root, row(SECOND_GAIN))
@@ -833,11 +844,15 @@
         add_row(3, dz.astype(f32))
         add_row(4, e * normal)
         add_row(5, e)
-    loop(T // R, second_norm, 2)
+    gathers_dz = [Gather(lambda o, i=i: dz_all.at[block_of(2 * o + i, H)], False) for i in range(2)]
+    loop(H // R, second_norm, 2)
+    gathers_dz[0].start()
+    folds_z[1].ready()
+    loop(H // R, lambda i: second_norm(i + H // R), 2)
+    gathers_dz[1].start()
     outs = [local(out_ref, r.out)]
-    gather_dz = Gather(lambda o: dz_all.at[block_of(o, T)], False)
-    gather_dz.start()
-    fold_z.batch.close()
+    for fold in folds_z:
+        fold.batch.close()
 
     colg = r.colg
     colg[...] = jnp.zeros((8, F), f32)
@@ -868,24 +883,28 @@
     def up_grad(k):
         gu_part[pz(k)] = mm(y_t[block_of(pz(k), KW), :], du_ref[...]).astype(bf16)
 
-    gather_c.pass_far()
-    gather_dz.wait(1)
+    def dz_wait(k):
+        for gather in gathers_dz:
+            gather.wait(k)
+    dz_wait(1)
     unlower(0)
     unlift(0)
     fold_y.pair(0)
-    gather_dz.pass_near()
-    gather_dz.wait(3)
+    gathers_dz[0].pass_near()
+    gathers_dz[1].pass_near()
+    dz_wait(3)
     unlower(1)
     unlift(1)
     fold_y.pair(1)
-    gather_dz.wait(5)
+    gathers_dz[0].pass_far()
+    dz_wait(5)
     unlower(2)
     fold_y.onward(1)
     unlift(2)
     fold_y.pair(2)
-    gather_dz.pass_far()
+    gathers_dz[1].pass_far()
     fold_y.onward(2)
-    gather_dz.wait(7)
+    dz_wait(7)
     down_grad(3)
     down_grad(1)
     folds_dn[0].start()
@@ -904,7 +923,6 @@
     down_grad(0)
     up_grad(2)
     up_grad(0)
-    gather_c.wait()
     fold_y.ready()
 
     dh1, da = r.dh1, r.da
@@ -933,9 +951,11 @@
     share_da = Share(7, da_cols.at[pl.ds(0, T)])
     share_da.plane(lambda o: da.at[:, block_of(o, C)], da_cols.at[block_of(s, T)])
     da_cols[block_of(s, T), :] = da[:, block_of(s, C)]
-    vec_all = r.vec_all
-    share_vec = Share(7, vecg)
-    share_vec.plane(lambda o: vecg, vec_all.at[s])
+    vec_z, vec_all = r.vec_z, r.vec_all
+    share_vec = Share(3, vec_z.at[0])
+    for k in (2, 3, 1):
+        share_vec.batch.send(vecg.at[:, block_of(pz(k), KW)], vec_z.at[z], share_vec.slot, (s, pz(k)))
+    vec_z[z] = vecg[:, block_of(z, KW)]
     folds_dn[1].middle()
     folds_up[1].start()
     share_dc.wait()
@@ -985,21 +1005,23 @@
     def attend_back_and_fold(i):
         attend_back(i)
 
-        @pl.when(i == 4)
+        @pl.when(i == 0)
         def _():
-            share_da.wait()
-            for k in (3, 1, 2, 0):
-                out_grad(k)
-            fold_o.start()
+            gather_c.pass_near()
+
+        @pl.when(i == 5)
+        def _():
+            for part in range(2):
+                at_row = pl.multiple_of(s * UZ + part * (UZ // 2), UZ // 2)
+                gd_all[pl.ds(at_row, UZ // 2), :] = folds_dn[part].finish()
+            gather_gd.start()
 
         @pl.when(i == 6)
         def _():
             folds_up[0].middle()
+            gather_c.pass_far()
     loop(L // T, attend_back_and_fold)
 
-    for i in range(2):
-        gd_all[pl.ds(pl.multiple_of(s * UZ + i * (UZ // 2), UZ // 2), UZ // 2), :] = folds_dn[i].finish()
-    gather_gd.start()
 
     def dq_rows(i):
         here = pl.ds(at(i, T), T)
@@ -1033,26 +1055,42 @@
     fold_x.onward(1)
     unproject(0)
     fold_x.onward(2)
+    gather_c.wait()
+    share_da.wait()
+    for k in (3, 1):
+        out_grad(k)
+    fold_o.start()
+    for k in (2, 0):
+        out_grad(k)
     projection_grad(2)
     projection_grad(0)
     fold_x.cross()
     gather_gd.pass_near()
-    col_z = r.col_z
-    share_col = Share(3, colg)
-    share_col.column(colg, col_z.at[z])
-    col_z[z] = colg[...]
-    vec_all[s] = vecg[...]
+    col_z, col_own = r.col_z, r.col_own
+    col_own[...] = jnp.zeros((8, C), f32)
+    for i in range(Z):
+        col_own[i:i + 1, :] = colg[0:1, i * C:(i + 1) * C]
+    for i in range(3):
+        col_own[Z + i:Z + i + 1, :] = colg[1:2, i * C:(i + 1) * C]
+    share_col = Share(3, col_own)
+    share_col.column(col_own, col_z.at[z])
+    col_z[z] = col_own[...]
     share_vec.wait()
-    vec_plane, vec_z = r.vec_plane, r.vec_z
-    total = vec_all[0]
-    for o in range(1, S):
-        total = total + vec_all[o]
-    vec_plane[...] = total
-    share_sum = Share(3, vec_plane)
-    share_sum.column(vec_plane, vec_z.at[z])
-    vec_z[z] = total
+    vec_sum = r.vec_sum
+    vec_sum[...] = vec_z[0] + vec_z[1] + vec_z[2] + vec_z[3]
+    share_sum = Share(7, vec_sum)
+    share_sum.plane(lambda o: vec_sum, vec_all.at[s])
+    vec_all[s] = vec_sum[...]
+    for i in range(2):
+        gu_all[s, pl.ds(i * (KW // 2), KW // 2), :] = folds_up[i].finish()
+    gather_gu.start()
+    fold_qk.middle()
+
+    @pl.when(zhigh == 1)
+    def _():
+        fold_v.middle()
+        fold_o.middle()
     gather_gd.pass_far()
-    fold_o.middle()
     fold_x.ready()
     dx_ref = r.v_dx
 
@@ -1062,28 +1100,27 @@
         dx_ref[rows, :] = (dh1[rows, :] + fold_x.rows(start, R)).astype(bf16)
     loop(T // R, input_back, 2)
     outs.append(local(dx_ref, r.dx))
-    for i in range(2):
-        gu_all[s, pl.ds(i * (KW // 2), KW // 2), :] = folds_up[i].finish()
-    gather_gu.start()
-    fold_qk.middle()
     gather_gd.wait()
     outs.append(local(gd_all, r.gd))
+    gather_gu.pass_near()
+
+    @pl.when(zhigh == 0)
+    def _():
+        fold_v.middle()
+        fold_o.middle()
+    gqk_all[s] = fold_qk.finish()
+    gather_gqk.start()
+    gv_all[s] = fold_v.finish()
+    gather_gv.start()
+    go_all[:, block_of(s, C)] = fold_o.finish()
+    gather_go.start()
+    gather_gu.pass_far()
     share_col.wait()
     col_all, col_sum = r.col_all, r.col_sum
     col_sum[...] = col_z[0] + col_z[1] + col_z[2] + col_z[3]
     share_cols = Share(7, col_sum)
     share_cols.plane(lambda o: col_sum, col_all.at[s])
     col_all[s] = col_sum[...]
-    fold_v.middle()
-    gather_gu.pass_near()
-    go_all[:, block_of(s, C)] = fold_o.finish()
-    gather_go.start()
-    gqk_all[s] = fold_qk.finish()
-    gather_gqk.start()
-    gv_all[s] = fold_v.finish()
-    gather_gv.start()
-    gather_gu.pass_far()
-    gather_go.pass_near()
     gather_gqk.pass_near()
     gather_gv.pass_near()
     gather_gu.wait()
@@ -1091,25 +1128,26 @@
 
     share_sum.wait()
     share_cols.wait()
-    vec_sum = r.vec_sum
-    vec_sum[...] = vec_z[0] + vec_z[1] + vec_z[2] + vec_z[3]
+    total = vec_all[0]
+    for o in range(1, S):
+        total = total + vec_all[o]
     gsm = r.v_gsm
     gsm[...] = jnp.zeros(gsm.shape, f32)
     for start, i in wide:
         for half in range(KW // C):
-            at_row = start + half
-            gsm[at_row:at_row + 1, :] = vec_sum[i:i + 1, block_of(z * (KW // C) + half, C)]
+            gsm[start + half:start + half + 1, :] = total[i:i + 1, half * C:(half + 1) * C]
     for o in range(S):
         at_row = first_row.up_bias + o
-        gsm[at_row:at_row + 1, :] = col_all[o, 0:1, block_of(z, C)]
+        gsm[at_row:at_row + 1, :] = col_all[o, pl.ds(z, 1), :]
     for i in range(per):
         number = z * per + i
         at_row = first_row.projection_bias + i
-        gsm[at_row:at_row + 1, :] = col_all[number % S, 1:2, block_of(number // S, C)]
+        gsm[at_row:at_row + 1, :] = col_all[number % S, pl.ds(Z + number // S, 1), :]
     outs.append(local(gsm, r.gsm))
-    gather_go.pass_far()
+    gather_go.pass_near()
     gather_gqk.pass_far()
     gather_gv.pass_far()
+    gather_go.pass_far()
     gather_go.wait()
     outs.append(local(go_all, r.go))
     gather_gqk.wait()
@@ -1178,8 +1216,8 @@
         gd_all=((8 * UZ, D), bf16), gu_all=((8, KW, F), bf16), go_all=((KW, D), bf16),
         gqk_all=((8, KW, 2 * C), bf16), gv_all=((8, KW, C), bf16), da=((T, D), bf16), dc_tok=((T, D), bf16), dc=((L, C), bf16),
         da_cols=((L, C), bf16), c_all=((L, D), bf16), dq=((L, C), f32), dproj=((L, 3 * C), bf16),
-        vec_all=((8, 8, D), f32), vec_plane=((8, D), f32), vec_z=((Z, 8, D), f32), vec_sum=((8, D), f32),
-        col_z=((Z, 8, F), f32), col_sum=((8, F), f32), col_all=((8, 8, F), f32),
+        vec_all=((8, 8, KW), f32), vec_z=((Z, 8, KW), f32), vec_sum=((8, KW), f32), col_own=((8, C), f32),
+        col_z=((Z, 8, C), f32), col_sum=((8, C), f32), col_all=((8, 8, C), f32),
         low0=(PART, bf16), high0=(PART, bf16), low1=(PART, bf16), high1=(PART, bf16), low2=(PART, bf16),
         high2=(PART, bf16), ssem=(BATCHES,), rsem=(LANDINGS,), lsem=(LOCAL,))
     names = [*inputs, *outputs, *scratch]
@@ -1291,8 +1329,8 @@
         copy.wait()
 
 
-BATCHES = 42
-LANDINGS = 148
+BATCHES = 44
+LANDINGS = 166
 LOCAL = 32
 
 

time: 171 us -> 165 us (0.965)
  Pallas kernels: 169 us -> 163 us
    pallas_call x1, Pallas kernels: 163 us -> 157 us  [fused_shards(): pl.pallas_call(partial(fused_layer, sizes), out_shape=[jax.ShapeDtypeStru...]
where the time goes in v6:
time: 165 us; the launch traced here: 164 us
  Pallas kernels  163 us (99%)
    pallas_call x1, Pallas kernels, fused_shards(): pl.pallas_call(partial(fused_layer, sizes), out_shape=[jax.ShapeDtypeStru...  157 us
    pallas_call x1, Pallas kernels, fused_shards(): pl.pallas_call(partial(widen, tuple(starts.values())), out_shape=[jax.Sha...  6.89 us

profile of v6, /device:TPU:0, one launch (start us, length us, event | category | flops | bytes accessed | tf_op | source)
XLA Modules:
  0.0 164.3 jit_solution(6398060051166473730)
XLA Ops:
  0.7 156.6 %fused_layer.1 = (bf16[128,1024]{1,0:T(8,128)(2,1)}, bf16[128,1024]{1,0:T(8,128)(2,1)}, f32[32,128]{1,0:T(8,128)}, bf16[8,256,256]{2,1,0:T(8,128)(2,1)}, bf16[8,...) custom-call(bf16[128,1024]{1,0:T(8,128)(2,1)} %bitcast.20, ...), custom_call_target="tpu_custom_call" | custom-call | tf_op jit(solution)/shard_map/fused_layer/pallas_call | solution.py:1227
  157.2 6.9 %widen.1 = (bf16[128,1024]{1,0:T(8,128)(2,1)}, bf16[128,1024]{1,0:T(8,128)(2,1)}, f32[256,3072]{1,0:T(8,128)}, f32[256,1024]{1,0:T(8,128)}, f32[256,4096]{1,0:T(...) custom-call(bf16[128,1024]{1,0:T(8,128)(2,1)} %get-tuple-element.36., ...), custom_call_target="tpu_custom_call" | custom-call | tf_op jit(solution)/shard_map/widen/pallas_call | solution.py:1243

commit v7 on v6

--- a/solution.py
+++ b/solution.py
@@ -821,7 +821,7 @@
     folds_z[1].cross()
     folds_z[0].ready()
 
-    dh2, out_ref = r.dh2, r.v_out
+    dh2, out_ref = r.dh2, r.out
 
     def add_row(i, value):
         vecg[i:i + 1, :] = vecg[i:i + 1, :] + jnp.sum(value, axis=0, keepdims=True)
@@ -850,7 +850,6 @@
     folds_z[1].ready()
     loop(H // R, lambda i: second_norm(i + H // R), 2)
     gathers_dz[1].start()
-    outs = [local(out_ref, r.out)]
     for fold in folds_z:
         fold.batch.close()
 
@@ -990,7 +989,7 @@
         dproj[here, C:2 * C] = (dk * cos_ref[here, :] - swapped(dk) * sin_ref[here, :]).astype(bf16)
         dq[...] = dq[...] + mm(jnp.concatenate(slopes, axis=0), jnp.concatenate(keys, axis=0), TN)
 
-    gd_all, gu_all, go_all, gqk_all, gv_all = r.gd_all, r.gu_all, r.go_all, r.gqk_all, r.gv_all
+    gd_all, gu_all, go_all, gqk_all, gv_all = r.gd, r.gu, r.go, r.gqk, r.gv
     gather_gd = Gather(lambda o: gd_all.at[block_of(o, UZ)])
     gather_gu = Gather(lambda o: gu_all.at[o])
     gather_go = Gather(lambda o: go_all.at[:, block_of(o, C)])
@@ -1092,16 +1091,14 @@
         fold_o.middle()
     gather_gd.pass_far()
     fold_x.ready()
-    dx_ref = r.v_dx
+    dx_ref = r.dx
 
     def input_back(i):
         start = at(i, R)
         rows = pl.ds(start, R)
         dx_ref[rows, :] = (dh1[rows, :] + fold_x.rows(start, R)).astype(bf16)
     loop(T // R, input_back, 2)
-    outs.append(local(dx_ref, r.dx))
     gather_gd.wait()
-    outs.append(local(gd_all, r.gd))
     gather_gu.pass_near()
 
     @pl.when(zhigh == 0)
@@ -1124,14 +1121,13 @@
     gather_gqk.pass_near()
     gather_gv.pass_near()
     gather_gu.wait()
-    outs.append(local(gu_all, r.gu))
 
     share_sum.wait()
     share_cols.wait()
     total = vec_all[0]
     for o in range(1, S):
         total = total + vec_all[o]
-    gsm = r.v_gsm
+    gsm = r.gsm
     gsm[...] = jnp.zeros(gsm.shape, f32)
     for start, i in wide:
         for half in range(KW // C):
@@ -1143,19 +1139,13 @@
         number = z * per + i
         at_row = first_row.projection_bias + i
         gsm[at_row:at_row + 1, :] = col_all[number % S, pl.ds(Z + number // S, 1), :]
-    outs.append(local(gsm, r.gsm))
     gather_go.pass_near()
     gather_gqk.pass_far()
     gather_gv.pass_far()
     gather_go.pass_far()
     gather_go.wait()
-    outs.append(local(go_all, r.go))
     gather_gqk.wait()
-    outs.append(local(gqk_all, r.gqk))
     gather_gv.wait()
-    outs.append(local(gv_all, r.gv))
-    for copy in outs:
-        copy.wait()
     for batch in closing:
         batch.close()
     assert counter[0] <= LANDINGS and counter[1] <= BATCHES and counter[2] <= LOCAL, counter
@@ -1197,7 +1187,6 @@
     PART = (4, T, D)
     scratch = {name: (value.shape, value.dtype) for name, value in landed.items()}
     scratch.update(
-        v_out=((T, D), bf16), v_dx=((T, D), bf16), v_gsm=((rows, C), f32),
         x_all=((L, D), bf16), x_t=((D, L), bf16), w_qkv=((D, 3 * C), bf16), st_proj=((KW, 3 * C), f32),
         w_o=((D, D), bf16), st_wo=((KW, C), f32), w_up=((D, F), bf16), st_up=((KW, F), f32),
         w_dn=((F, D), bf16), st_dn=((UZ, D), f32), small_all=((Z, rows, C), f32), vec=((8, D), f32),
@@ -1213,8 +1202,7 @@
         go_part=((Z, KW, C), bf16), go_land=((3, KW, C), bf16), go_pass=((KW, C), bf16),
         gqk_part=((Z, KW, 2 * C), bf16), gqk_land=((3, KW, 2 * C), bf16), gqk_pass=((KW, 2 * C), bf16),
         gv_part=((Z, KW, C), bf16), gv_land=((3, KW, C), bf16), gv_pass=((KW, C), bf16),
-        gd_all=((8 * UZ, D), bf16), gu_all=((8, KW, F), bf16), go_all=((KW, D), bf16),
-        gqk_all=((8, KW, 2 * C), bf16), gv_all=((8, KW, C), bf16), da=((T, D), bf16), dc_tok=((T, D), bf16), dc=((L, C), bf16),
+        da=((T, D), bf16), dc_tok=((T, D), bf16), dc=((L, C), bf16),
         da_cols=((L, C), bf16), c_all=((L, D), bf16), dq=((L, C), f32), dproj=((L, 3 * C), bf16),
         vec_all=((8, 8, KW), f32), vec_z=((Z, 8, KW), f32), vec_sum=((8, KW), f32), col_own=((8, C), f32),
         col_z=((Z, 8, C), f32), col_sum=((8, C), f32), col_all=((8, 8, C), f32),
@@ -1223,15 +1211,15 @@
     names = [*inputs, *outputs, *scratch]
     sizes = SimpleNamespace(names=names, T=T, D=D, L=L, F=F, first_row=SimpleNamespace(**starts))
 
-    anywhere = pl.BlockSpec(memory_space=pl.ANY)
+    anywhere, near = pl.BlockSpec(memory_space=pl.ANY), pl.BlockSpec(memory_space=pltpu.VMEM)
     results = pl.pallas_call(
         partial(fused_layer, sizes),
-        out_shape=[jax.ShapeDtypeStruct(*what) for what in outputs.values()],
+        out_shape=[pltpu.VMEM(*what) for what in outputs.values()],
         in_specs=[anywhere] * len(inputs),
-        out_specs=[anywhere] * len(outputs),
+        out_specs=[near] * len(outputs),
         scratch_shapes=[pltpu.VMEM(*what) if len(what) == 2 else pltpu.SemaphoreType.DMA(what)
                         for what in scratch.values()],
-        compiler_params=pltpu.CompilerParams(collective_id=0, has_side_effects=True, vmem_limit_bytes=67043328),
+        compiler_params=pltpu.CompilerParams(collective_id=0, has_side_effects=True, vmem_limit_bytes=57 << 20),
         name="fused_layer",
     )(*inputs.values())
     out, dx, gsm, gqk, gv, go, gu, gd = results
@@ -1243,11 +1231,11 @@
     results = pl.pallas_call(
         partial(widen, tuple(starts.values())),
         out_shape=[jax.ShapeDtypeStruct(value.shape, value.dtype) for value in outcomes],
-        in_specs=[anywhere] * len(sources),
+        in_specs=[near] * len(sources),
         out_specs=[anywhere] * len(outcomes),
-        scratch_shapes=[pltpu.VMEM(value.shape, value.dtype) for value in sources + outcomes[2:]]
-        + [pltpu.SemaphoreType.DMA((LOCAL,))] * 2,
-        compiler_params=pltpu.CompilerParams(vmem_limit_bytes=56 << 20),
+        scratch_shapes=[pltpu.VMEM(value.shape, value.dtype) for value in outcomes[2:]]
+        + [pltpu.SemaphoreType.DMA((LOCAL,))],
+        compiler_params=pltpu.CompilerParams(vmem_limit_bytes=20 << 20),
         name="widen",
     )(*sources)
     out, dx, gq, go, gu, gd = results[:6]
@@ -1256,28 +1244,15 @@
 
 
 def widen(starts, *refs):
-    sources, results = refs[:8], refs[8:22]
-    held, made, insem, outsem = refs[22:30], refs[30:42], refs[42], refs[43]
+    held, results, made, outsem = refs[:8], refs[8:22], refs[22:34], refs[34]
     out, dx, gqk, gv, go, gu, gd, gsm = held
     C = gsm.shape[1]
-    count = [0, 0]
-
-    def fetch(source, ref):
-        copy = pltpu.make_async_copy(source, ref, insem.at[count[0]])
-        count[0] += 1
-        copy.start()
-        return copy
     stores = []
 
     def store(ref, result):
-        copy = pltpu.make_async_copy(ref, result, outsem.at[count[1]])
-        count[1] += 1
+        copy = pltpu.make_async_copy(ref, result, outsem.at[len(stores)])
         copy.start()
         stores.append(copy)
-
-    def piece(i, at, n):
-        window = (slice(None), pl.ds(at, n)) if len(held[i].shape) == 3 else (pl.ds(at, n),)
-        return fetch(sources[i].at[window], held[i].at[window])
 
     def grouped(i, target, at, n, first):
         source, result = held[i], made[target]
@@ -1301,23 +1276,19 @@
             return carry
         lax.fori_loop(0, n // 32, step, 0)
 
+    store(out, results[0])
+    store(dx, results[1])
     work = []
     for i, target, n, body, first in ((5, 2, 64, grouped, 0), (6, 3, 256, plain, 0), (2, 0, 64, grouped, 0),
                                       (3, 0, 64, grouped, 2), (4, 1, 256, plain, 0)):
         total = held[i].shape[-2]
         for at in range(0, total, n):
-            work.append((piece(i, at, n), i, target, at, n, body, first))
-    whole = [fetch(sources[i], held[i]) for i in (0, 1, 7)]
-    for copy, i, target, at, n, body, first in work:
-        copy.wait()
+            work.append((i, target, at, n, body, first))
+    for i, target, at, n, body, first in work:
         body(i, target, at, n, first)
         if i != 2:
             rows = pl.ds(at, n)
             store(made[target].at[rows], results[2 + target].at[rows])
-    for copy in whole:
-        copy.wait()
-    store(out, results[0])
-    store(dx, results[1])
     for start, ref, result in zip(starts, made[4:], results[6:]):
         if ref.shape[1] == C:
             ref[...] = gsm[start:start + ref.shape[0], :]

time: 165 us -> 162 us (0.982)
  Pallas kernels: 163 us -> 161 us
    pallas_call x1, Pallas kernels: 6.89 us -> 5.03 us  [fused_shards(): pl.pallas_call(partial(widen, tuple(starts.values())), out_shape=[jax.Sha...]
where the time goes in v7:
time: 162 us
  Pallas kernels  161 us (99%)
    pallas_call x1, Pallas kernels, fused_shards(): pl.pallas_call(partial(fused_layer, sizes), out_shape=[pltpu.VMEM(*what)...  156 us
    pallas_call x1, Pallas kernels, fused_shards(): pl.pallas_call(partial(widen, tuple(starts.values())), out_shape=[jax.Sha...  5.03 us

profile of v7, /device:TPU:0, one launch (start us, length us, event | category | flops | bytes accessed | tf_op | source)
XLA Modules:
  0.0 161.7 jit_solution(10669659205264584861)
XLA Ops:
  0.7 155.9 %fused_layer.1 = (bf16[128,1024]{1,0:T(8,128)(2,1)S(1)}, bf16[128,1024]{1,0:T(8,128)(2,1)S(1)}, f32[32,128]{1,0:T(8,128)S(1)}, bf16[8,256,256]{2,1,0:T(8,128)(2,...) custom-call(bf16[128,1024]{1,0:T(8,128)(2,1)} %bitcast.20, ...), custom_call_target="tpu_custom_call" | custom-call | tf_op jit(solution)/shard_map/fused_layer/pallas_call | solution.py:1215
  156.5 5.0 %widen.1 = (bf16[128,1024]{1,0:T(8,128)(2,1)}, bf16[128,1024]{1,0:T(8,128)(2,1)}, f32[256,3072]{1,0:T(8,128)}, f32[256,1024]{1,0:T(8,128)}, f32[256,4096]{1,0:T(...) custom-call(bf16[128,1024]{1,0:T(8,128)(2,1)S(1)} %get-tuple-element, ...), custom_call_target="tpu_custom_call" | custom-call | tf_op jit(solution)/shard_map/widen/pallas_call | solution.py:1231

commit v8 on v7

--- a/solution.py
+++ b/solution.py
@@ -1084,8 +1084,9 @@
         gu_all[s, pl.ds(i * (KW // 2), KW // 2), :] = folds_up[i].finish()
     gather_gu.start()
     fold_qk.middle()
-
-    @pl.when(zhigh == 1)
+    inner = flip(zlow, zhigh) == 1
+
+    @pl.when(inner)
     def _():
         fold_v.middle()
         fold_o.middle()
@@ -1101,17 +1102,20 @@
     gather_gd.wait()
     gather_gu.pass_near()
 
-    @pl.when(zhigh == 0)
+    @pl.when(jnp.logical_not(inner))
     def _():
         fold_v.middle()
-        fold_o.middle()
     gqk_all[s] = fold_qk.finish()
     gather_gqk.start()
+
+    @pl.when(jnp.logical_not(inner))
+    def _():
+        fold_o.middle()
     gv_all[s] = fold_v.finish()
     gather_gv.start()
+    gather_gu.pass_far()
     go_all[:, block_of(s, C)] = fold_o.finish()
     gather_go.start()
-    gather_gu.pass_far()
     share_col.wait()
     col_all, col_sum = r.col_all, r.col_sum
     col_sum[...] = col_z[0] + col_z[1] + col_z[2] + col_z[3]
@@ -1122,6 +1126,9 @@
     gather_gv.pass_near()
     gather_gu.wait()
 
+    gather_go.pass_near()
+    gather_gqk.pass_far()
+    gather_gv.pass_far()
     share_sum.wait()
     share_cols.wait()
     total = vec_all[0]
@@ -1139,9 +1146,6 @@
         number = z * per + i
         at_row = first_row.projection_bias + i
         gsm[at_row:at_row + 1, :] = col_all[number % S, pl.ds(Z + number // S, 1), :]
-    gather_go.pass_near()
-    gather_gqk.pass_far()
-    gather_gv.pass_far()
     gather_go.pass_far()
     gather_go.wait()
     gather_gqk.wait()
@@ -1300,9 +1304,9 @@
         copy.wait()
 
 
-BATCHES = 44
-LANDINGS = 166
-LOCAL = 32
+BATCHES = 34
+LANDINGS = 155
+LOCAL = 26
 
 
 def fits(mesh):

time: 162 us -> 158 us (0.975)
  Pallas kernels: 161 us -> 157 us
    pallas_call x1, Pallas kernels: 156 us -> 152 us  [fused_shards(): pl.pallas_call(partial(fused_layer, sizes), out_shape=[pltpu.VMEM(*what)...]
where the time goes in v8:
time: 158 us
  Pallas kernels  157 us (99%)
    pallas_call x1, Pallas kernels, fused_shards(): pl.pallas_call(partial(fused_layer, sizes), out_shape=[pltpu.VMEM(*what)...  152 us
    pallas_call x1, Pallas kernels, fused_shards(): pl.pallas_call(partial(widen, tuple(starts.values())), out_shape=[jax.Sha...  4.98 us

profile of v8, /device:TPU:0, one launch (start us, length us, event | category | flops | bytes accessed | tf_op | source)
XLA Modules:
  0.0 158.0 jit_solution(13180934377060853503)
XLA Ops:
  0.7 152.2 %fused_layer.1 = (bf16[128,1024]{1,0:T(8,128)(2,1)S(1)}, bf16[128,1024]{1,0:T(8,128)(2,1)S(1)}, f32[32,128]{1,0:T(8,128)S(1)}, bf16[8,256,256]{2,1,0:T(8,128)(2,...) custom-call(bf16[128,1024]{1,0:T(8,128)(2,1)} %bitcast.20, ...), custom_call_target="tpu_custom_call" | custom-call | tf_op jit(solution)/shard_map/fused_layer/pallas_call | solution.py:1219
  152.8 5.0 %widen.1 = (bf16[128,1024]{1,0:T(8,128)(2,1)}, bf16[128,1024]{1,0:T(8,128)(2,1)}, f32[256,3072]{1,0:T(8,128)}, f32[256,1024]{1,0:T(8,128)}, f32[256,4096]{1,0:T(...) custom-call(bf16[128,1024]{1,0:T(8,128)(2,1)S(1)} %get-tuple-element, ...), custom_call_target="tpu_custom_call" | custom-call | tf_op jit(solution)/shard_map/widen/pallas_call | solution.py:1235

commit v9 on v8

--- a/solution.py
+++ b/solution.py
@@ -356,6 +356,12 @@
     def pz(k):
         return flip(zlow, k % 2) + 2 * flip(zhigh, k // 2)
 
+    inner = flip(zlow, zhigh) == 1
+
+    def by_plane(for_inner, for_outer):
+        pl.when(inner)(for_inner)
+        pl.when(jnp.logical_not(inner))(for_outer)
+
     def chip_of(j):
         return flip(xbit, j % 2) + 2 * flip(ybit, j // 2)
 
@@ -383,7 +389,12 @@
     class Batch:
         def __init__(self, count, like):
             self.slot, self.bytes, self.open = take(1), count * size(like), True
+            self.one, self.shares = size(like), None
             closing.append(self)
+
+        def drain(self, n):
+            everything = extent(n)
+            pltpu.make_async_copy(everything, everything, ssem.at[self.slot]).wait()
 
         def send(self, src, dst, slot, dev):
             pltpu.make_async_remote_copy(
@@ -391,9 +402,10 @@
                 device_id=dev, device_id_type=MESH).start()
 
         def close(self):
-            if self.open:
-                everything = extent(self.bytes)
-                pltpu.make_async_copy(everything, everything, ssem.at[self.slot]).wait()
+            if self.open and self.shares:
+                by_plane(*[partial(self.drain, n * self.one) for n in self.shares])
+            elif self.open:
+                self.drain(self.bytes)
             self.open = False
 
     def local(src, dst):
@@ -464,6 +476,13 @@
             there = self.place(pz(2))
             arrived(there, self.base + 1)
             self.batch.send(there, there, self.base + 2, (s, pz(1)))
+
+        def meet(self):
+            def for_inner():
+                self.pass_on()
+                self.start(3)
+            by_plane(for_inner, lambda: arrived(self.place(pz(2)), self.base + 1))
+            self.batch.shares = (4, 2)
 
         def wait(self):
             for k in (1, 3):
@@ -736,7 +755,7 @@
         def _():
             share_c.batch.send(c_heads.at[block_of(ps(k), T)], c_tok.at[:, block_of(s, C)], share_c.slot, (ps(k), z))
     loop(8, attend_and_send)
-    spread_up.pass_on()
+    spread_up.meet()
     spread_dn.start()
     c_tok[:, block_of(s, C)] = c_heads[block_of(s, T), :]
     gather_o.wait()
@@ -797,7 +816,7 @@
     lift(1)
     gather_y.wait(5)
     lift(2)
-    spread_dn.pass_on()
+    spread_dn.meet()
     gather_y.pass_far()
     gather_c.start(c_tok)
     gather_y.wait(7)
@@ -1084,7 +1103,6 @@
         gu_all[s, pl.ds(i * (KW // 2), KW // 2), :] = folds_up[i].finish()
     gather_gu.start()
     fold_qk.middle()
-    inner = flip(zlow, zhigh) == 1
 
     @pl.when(inner)
     def _():

time: 158 us -> 157 us (level)
  no operation moved by 1% of the time
where the time goes in v9:
time: 157 us; the launch traced here: 156 us
  Pallas kernels  156 us (99%)
    pallas_call x1, Pallas kernels, fused_shards(): pl.pallas_call(partial(fused_layer, sizes), out_shape=[pltpu.VMEM(*what)...  151 us
    pallas_call x1, Pallas kernels, fused_shards(): pl.pallas_call(partial(widen, tuple(starts.values())), out_shape=[jax.Sha...  4.98 us

profile of v9, /device:TPU:0, one launch (start us, length us, event | category | flops | bytes accessed | tf_op | source)
XLA Modules:
  0.0 156.5 jit_solution(1492591430149769462)
XLA Ops:
  0.7 150.7 %fused_layer.1 = (bf16[128,1024]{1,0:T(8,128)(2,1)S(1)}, bf16[128,1024]{1,0:T(8,128)(2,1)S(1)}, f32[32,128]{1,0:T(8,128)S(1)}, bf16[8,256,256]{2,1,0:T(8,128)(2,...) custom-call(bf16[128,1024]{1,0:T(8,128)(2,1)} %bitcast.20, ...), custom_call_target="tpu_custom_call" | custom-call | tf_op jit(solution)/shard_map/fused_layer/pallas_call | solution.py:1237
  151.4 5.0 %widen.1 = (bf16[128,1024]{1,0:T(8,128)(2,1)}, bf16[128,1024]{1,0:T(8,128)(2,1)}, f32[256,3072]{1,0:T(8,128)}, f32[256,1024]{1,0:T(8,128)}, f32[256,4096]{1,0:T(...) custom-call(bf16[128,1024]{1,0:T(8,128)(2,1)S(1)} %get-tuple-element, ...), custom_call_target="tpu_custom_call" | custom-call | tf_op jit(solution)/shard_map/widen/pallas_call | solution.py:1253

commit v10 on v9

--- a/solution.py
+++ b/solution.py
@@ -514,6 +514,41 @@
             return (self.parts[z, self.rows, :].astype(f32) + self.landing[0, self.rows, :].astype(f32)
                     + self.landing[2, self.rows, :].astype(f32)).astype(bf16)
 
+    class FoldInner:
+        def __init__(self, parts, landing, passing, first=0, count=None):
+            self.rows = pl.ds(first, count or passing.shape[0])
+            self.parts, self.landing, self.passing = parts, landing, passing.at[self.rows]
+            self.batch, self.base = Batch(3, self.passing), landings(4)
+
+            @pl.when(jnp.logical_not(inner))
+            def _():
+                landing[3, self.rows, :] = jnp.zeros(self.passing.shape, bf16)
+
+        def send(self, slab, i, k):
+            self.batch.send(self.parts.at[slab, self.rows], self.landing.at[i, self.rows], self.base + i, (s, pz(k)))
+
+        def start(self):
+            by_plane(lambda: None, lambda: self.send(pz(3), 1, 1))
+            self.send(pz(1), 0, 1)
+            by_plane(lambda: self.send(pz(3), 3, 3), lambda: None)
+
+        def middle(self):
+            def for_inner():
+                arrived(self.landing.at[1, self.rows], self.base + 1)
+                self.passing[...] = (self.parts[pz(2), self.rows, :].astype(f32)
+                                     + self.landing[1, self.rows, :].astype(f32)).astype(bf16)
+                self.batch.send(self.passing, self.landing.at[2, self.rows], self.base + 2, (s, pz(2)))
+            by_plane(for_inner, lambda: self.send(pz(2), 2, 2))
+
+        def finish(self):
+            arrived(self.landing.at[0, self.rows], self.base)
+            arrived(self.landing.at[2, self.rows], self.base + 2)
+            pl.when(inner)(lambda: arrived(self.landing.at[3, self.rows], self.base + 3))
+            total = self.parts[z, self.rows, :].astype(f32)
+            for i in (0, 2, 3):
+                total = total + self.landing[i, self.rows, :].astype(f32)
+            return total.astype(bf16)
+
     class Scatter:
         def __init__(self, parts, low, mid, high, first=0, count=T):
             self.parts, self.low, self.mid, self.high = parts, low, mid, high
@@ -1015,7 +1050,7 @@
     gather_gqk = Gather(lambda o: gqk_all.at[o])
     gather_gv = Gather(lambda o: gv_all.at[o])
     go_part = r.go_part
-    fold_o = Fold(go_part, r.go_land, r.go_pass)
+    fold_o = FoldInner(go_part, r.go_land, r.go_pass)
 
     def out_grad(k):
         go_part[pz(k)] = mm(c_all[:, block_of(pz(k), KW)], da_cols[...], TN).astype(bf16)
@@ -1050,7 +1085,7 @@
 
     gqk_part, gv_part = r.gqk_part, r.gv_part
     fold_qk = Fold(gqk_part, r.gqk_land, r.gqk_pass)
-    fold_v = Fold(gv_part, r.gv_land, r.gv_pass)
+    fold_v = FoldInner(gv_part, r.gv_land, r.gv_pass)
 
     def projection_grad(k):
         grad = mm(x_t[block_of(pz(k), KW), :], dproj[...]).astype(bf16)
@@ -1104,10 +1139,8 @@
     gather_gu.start()
     fold_qk.middle()
 
-    @pl.when(inner)
-    def _():
-        fold_v.middle()
-        fold_o.middle()
+    fold_v.middle()
+    fold_o.middle()
     gather_gd.pass_far()
     fold_x.ready()
     dx_ref = r.dx
@@ -1120,15 +1153,9 @@
     gather_gd.wait()
     gather_gu.pass_near()
 
-    @pl.when(jnp.logical_not(inner))
-    def _():
-        fold_v.middle()
     gqk_all[s] = fold_qk.finish()
     gather_gqk.start()
 
-    @pl.when(jnp.logical_not(inner))
-    def _():
-        fold_o.middle()
     gv_all[s] = fold_v.finish()
     gather_gv.start()
     gather_gu.pass_far()
@@ -1221,9 +1248,9 @@
         parts=((4, 2 * T, D), bf16), mid=((4, T, D), bf16), dh2=((T, D), f32), dh1=((T, D), f32),
         colg=((8, F), f32), gd_part=((Z, UZ, D), bf16), gd_land=((3, UZ, D), bf16), gd_pass=((UZ, D), bf16),
         gu_part=((Z, KW, F), bf16), gu_land=((3, KW, F), bf16), gu_pass=((KW, F), bf16),
-        go_part=((Z, KW, C), bf16), go_land=((3, KW, C), bf16), go_pass=((KW, C), bf16),
+        go_part=((Z, KW, C), bf16), go_land=((4, KW, C), bf16), go_pass=((KW, C), bf16),
         gqk_part=((Z, KW, 2 * C), bf16), gqk_land=((3, KW, 2 * C), bf16), gqk_pass=((KW, 2 * C), bf16),
-        gv_part=((Z, KW, C), bf16), gv_land=((3, KW, C), bf16), gv_pass=((KW, C), bf16),
+        gv_part=((Z, KW, C), bf16), gv_land=((4, KW, C), bf16), gv_pass=((KW, C), bf16),
         da=((T, D), bf16), dc_tok=((T, D), bf16), dc=((L, C), bf16),
         da_cols=((L, C), bf16), c_all=((L, D), bf16), dq=((L, C), f32), dproj=((L, 3 * C), bf16),
         vec_all=((8, 8, KW), f32), vec_z=((Z, 8, KW), f32), vec_sum=((8, KW), f32), col_own=((8, C), f32),
@@ -1323,7 +1350,7 @@
 
 
 BATCHES = 34
-LANDINGS = 155
+LANDINGS = 157
 LOCAL = 26
 
 

time: 157 us -> 157 us (level)
  no operation moved by 1% of the time
where the time goes in v10:
time: 157 us
  Pallas kernels  156 us (99%)
    pallas_call x1, Pallas kernels, fused_shards(): pl.pallas_call(partial(fused_layer, sizes), out_shape=[pltpu.VMEM(*what)...  151 us
    pallas_call x1, Pallas kernels, fused_shards(): pl.pallas_call(partial(widen, tuple(starts.values())), out_shape=[jax.Sha...  4.98 us

profile of v10, /device:TPU:0, one launch (start us, length us, event | category | flops | bytes accessed | tf_op | source)
XLA Modules:
  0.0 156.5 jit_solution(4054388491602168388)
XLA Ops:
  0.7 150.7 %fused_layer.1 = (bf16[128,1024]{1,0:T(8,128)(2,1)S(1)}, bf16[128,1024]{1,0:T(8,128)(2,1)S(1)}, f32[32,128]{1,0:T(8,128)S(1)}, bf16[8,256,256]{2,1,0:T(8,128)(2,...) custom-call(bf16[128,1024]{1,0:T(8,128)(2,1)} %bitcast.20, ...), custom_call_target="tpu_custom_call" | custom-call | tf_op jit(solution)/shard_map/fused_layer/pallas_call | solution.py:1264
  151.4 5.0 %widen.1 = (bf16[128,1024]{1,0:T(8,128)(2,1)}, bf16[128,1024]{1,0:T(8,128)(2,1)}, f32[256,3072]{1,0:T(8,128)}, f32[256,1024]{1,0:T(8,128)}, f32[256,4096]{1,0:T(...) custom-call(bf16[128,1024]{1,0:T(8,128)(2,1)S(1)} %get-tuple-element, ...), custom_call_target="tpu_custom_call" | custom-call | tf_op jit(solution)/shard_map/widen/pallas_call | solution.py:1280
